TPU v7x, 256 devices: a whole 4x4x8 slice. The times are simulated.
256 devices in a mesh: dp: 64 (over y, z_hi, x), mp: 4 (over z_lo, core).
Axes of the slice: x: 4, y: 4, z: 8 (z_hi: 4, z_lo: 2; z = z_hi * 2 + z_lo), core: 2. Of those that a mesh axis runs over, the one named last changes fastest.
Arguments:
- tokens: bfloat16 [4096, 2, 3072], P('dp'), may hold values from -6 to 6
- norm_gain_vector: float32 [3072], replicated, may hold values from 0.5 to 1.5
- query_weight: bfloat16 [3072, 1536], P('dp', 'mp'), may hold values from -0.109375 to 0.109375
- key_weight: bfloat16 [3072, 1536], P('dp', 'mp'), may hold values from -0.4375 to 0.4375
- value_weight: bfloat16 [3072, 1536], P('dp', 'mp'), may hold values from -0.109375 to 0.109375
- output_weight: bfloat16 [3072, 1536], P('dp', 'mp'), may hold values from -0.15625 to 0.15625
- prefix_cache: bfloat16 [64, 64, 2, 1536], P('dp', None, None, 'mp'), may hold values from -64 to 64
- lengths: int32 [4096], P('dp'), may hold values from 1 to 2, 5120 in all
- groups: int32 [4096], P('dp'), may hold values from 0 to 3
- deal_slot: int32 [4096], P('dp'), may hold values from 0 to 4095, as said below
- owners: int32 [64], replicated, may hold values from 0 to 63, each once
Outputs:
- hidden: bfloat16 [4096, 2, 3072], P('dp', None, 'mp')
- suffix_cache: bfloat16 [4096, 2, 2, 1536], P('dp', None, None, 'mp')
Inputs may be any that keep to these rules, and one draw needn't show every extreme that they name: Every value once; the 64 requests that start on one index of dp go to 64 different devices deal_slot // 64, one to each.
All inputs are finite; a program needn't handle non-finite values. No bound on the sum of `lengths` on one device may be relied on, other than what follows from the above.
Results may differ from a plain program's by a relative error of at most 0.013.
The roundings to bfloat16 on the way count: a program that leaves them out, or rounds other values in their place, can miss the bound.
Values may be sent and summed in bfloat16 or wider, within the bound.
No kernel may reach another device: no remote copies, remote signals or barrier semaphores. Data moves between devices by JAX's collectives and lax.ppermute only.
A program may use at most 128 MiB of HBM per device.

v0:
```python
import math

import jax
import jax.numpy as jnp
import numpy as np
from jax import lax
from jax.experimental import pallas as pl
from jax.experimental.pallas import tpu as pltpu
from jax.sharding import PartitionSpec as P


HD = 96
PREFIX = 1024
NEG = -1e30


def dp_shift(axis, amount):
    stride = {"y": 16, "zh": 4, "x": 1}[axis]
    perm = []
    for i in range(64):
        at = (i // stride) % 4
        perm.append((i, i + (((at + amount) % 4) - at) * stride))
    return perm


def shift(value, axis, amount):
    return lax.ppermute(value, "dp", dp_shift(axis, amount))


def mp_xor(value, mask):
    return lax.ppermute(value, "mp", [(i, i ^ mask) for i in range(4)])


def swap_y_mp(value):
    perm = []
    for i in range(64):
        y, rest = divmod(i, 16)
        for m in range(4):
            perm.append((i * 4 + m, (m * 16 + rest) * 4 + y))
    return lax.ppermute(value, ("dp", "mp"), perm)


def dot_nt(a, b):
    return lax.dot_general(a, b, (((1,), (1,)), ((), ())), preferred_element_type=jnp.float32)


def dot_tn(a, b):
    return lax.dot_general(a, b, (((0,), (0,)), ((), ())), preferred_element_type=jnp.float32)


def rope_tables():
    position = (PREFIX + np.arange(2)).astype(np.float32)
    frequency = np.float32(10000.0) ** (-np.arange(HD // 2).astype(np.float32) * np.float32(2.0) / np.float32(HD))
    angles = position[:, None] * frequency.astype(np.float32)[None, :]
    angles = np.concatenate([angles, angles], axis=-1).astype(np.float32)
    return np.cos(angles).astype(np.float32), np.sin(angles).astype(np.float32)


def qkv_kernel(
    pos_ref, own_ref, oth_ref, w0, w1, w2, w3, cos_ref, sin_ref,
    q_out, k_out, v_out, info_out, send_out, wsc,
):
    y, zh, x, c = pos_ref[0], pos_ref[1], pos_ref[2], pos_ref[3]
    for kx, piece in enumerate((w0, w1, w2, w3)):
        xa = (x - kx) & 3
        for kz in range(4):
            wsc[(zh - kz) & 3, xa] = piece[kz]
    accs = [None, None]
    for ky in range(4):
        ya = (y - ky) & 3
        lanes = pl.ds(pl.multiple_of(ya * 768, 128), 768)
        rhs = wsc[:, :, :, 288 * ky : 288 * ky + 288].reshape(768, 288)
        for i, ref in enumerate((own_ref, oth_ref)):
            part = jnp.dot(
                ref[:, :, lanes].reshape(256, 768), rhs, preferred_element_type=jnp.float32
            )
            accs[i] = part if accs[i] is None else accs[i] + part
    first = c == 0
    slots = (jnp.where(first, accs[0], accs[1]), jnp.where(first, accs[1], accs[0]))

    def rotate(values, t):
        turned = jnp.concatenate([-values[:, 48:], values[:, :48]], axis=1)
        return (values * cos_ref[t : t + 1, :] + turned * sin_ref[t : t + 1, :]).astype(jnp.bfloat16)

    info = own_ref[:, :, 3072:3200].reshape(256, 128).astype(jnp.float32)
    info_out[...] = info
    live = info[:, 2:3] > 1.5
    parts = []
    for t in range(2):
        rows = pl.ds(256 * t, 256)
        q_out[rows, :] = rotate(slots[t][:, :96], t)
        keyed = rotate(slots[t][:, 96:192], t)
        valued = slots[t][:, 192:288].astype(jnp.bfloat16)
        k_out[rows, :] = keyed
        v_out[rows, :] = valued
        if t == 1:
            keyed = jnp.where(live, keyed.astype(jnp.float32), 0.0).astype(jnp.bfloat16)
            valued = jnp.where(live, valued.astype(jnp.float32), 0.0).astype(jnp.bfloat16)
        parts += [keyed, valued]
    packed = jnp.concatenate(parts, axis=1)
    dest_iota = lax.broadcasted_iota(jnp.int32, (64, 64), 1).astype(jnp.float32)
    lane_iota = lax.broadcasted_iota(jnp.int32, (64, 128), 1)
    extras = jnp.zeros((64, 128), jnp.float32)
    for ky in range(4):
        block = info[64 * ky : 64 * ky + 64]
        pick = jnp.where(block[:, 0:1] == dest_iota, 1.0, 0.0).astype(jnp.bfloat16)
        moved = dot_tn(pick, packed[64 * ky : 64 * ky + 64])
        send_out[:, 384 * ky : 384 * ky + 384] = moved.astype(jnp.bfloat16)
        slot = jnp.where(lane_iota == ky, block[:, 1:2], 0.0).astype(jnp.bfloat16)
        extras = extras + dot_tn(pick, slot)
    send_out[:, 1536:1664] = extras.astype(jnp.bfloat16)


def attend_kernel(q_ref, k_ref, v_ref, info_ref, kg_ref, p0, p1, p2, p3, out_ref, s_ref, keys_ref, values_ref):
    factor = math.log2(math.e) / math.sqrt(HD)
    for ky in range(4):
        for kx, piece in enumerate((p0, p1, p2, p3)):
            rows = pl.ds(256 * kx, 256)
            keys_ref[ky, rows, :] = piece[:, :, 192 * ky : 192 * ky + 96].reshape(256, 96)
            values_ref[ky, rows, :] = piece[:, :, 192 * ky + 96 : 192 * ky + 192].reshape(256, 96)
    group = info_ref[:, 3:4]
    live = info_ref[:, 2:3] > 1.5

    def one_slot(t, carry):
        rows = pl.ds(pl.multiple_of(256 * t, 256), 256)
        queries = q_ref[rows, :]
        wide = queries.astype(jnp.float32)
        first = jnp.sum(wide * k_ref[0:256, :].astype(jnp.float32), axis=1, keepdims=True)
        second = jnp.sum(wide * k_ref[256:512, :].astype(jnp.float32), axis=1, keepdims=True)
        second = jnp.where(jnp.logical_and(live, t == 1), second, NEG)

        def score(ky, top):
            scores = dot_nt(queries, keys_ref[ky])
            scores = jnp.where(group == kg_ref[pl.ds(ky, 1), :], scores, NEG)
            s_ref[ky] = scores
            return jnp.maximum(top, jnp.max(scores, axis=1, keepdims=True))

        top = lax.fori_loop(0, 4, score, jnp.maximum(first, second))
        total = jnp.zeros((256, 1), jnp.float32)
        acc = jnp.zeros((256, 96), jnp.float32)
        for i, value in enumerate((first, second)):
            weight = jnp.exp2((value - top) * factor)
            total = total + weight
            values = v_ref[256 * i : 256 * i + 256, :].astype(jnp.float32)
            acc = acc + weight.astype(jnp.bfloat16).astype(jnp.float32) * values

        def gather(ky, state):
            total, acc = state
            weights = jnp.exp2((s_ref[ky] - top) * factor)
            total = total + jnp.sum(weights, axis=1, keepdims=True)
            acc = acc + jnp.dot(
                weights.astype(jnp.bfloat16), values_ref[ky], preferred_element_type=jnp.float32
            )
            return total, acc

        total, acc = lax.fori_loop(0, 4, gather, (total, acc))
        out_ref[rows, :] = (acc / total).astype(jnp.bfloat16)
        return carry

    lax.fori_loop(0, 2, one_slot, 0)


def order_kernel(pos_ref, w0, w1, w2, w3, out_ref):
    y, zh, x = pos_ref[0], pos_ref[1], pos_ref[2]
    for ky, piece in enumerate((w0, w1, w2, w3)):
        for kx in range(4):
            for kz in range(4):
                out_ref[(y - ky) & 3, (zh - kz) & 3, (x - kx) & 3] = piece[kx, kz]


def out_kernel(pos_ref, a0, a1, a2, a3, w_ref, len_ref, out_ref):
    m = pos_ref[4]
    acc = None
    for k, block in enumerate((a0, a1, a2, a3)):
        weight = w_ref[m ^ k].reshape(768, 384)
        part = dot_nt(block[...].reshape(128, 384), weight)
        acc = part if acc is None else acc + part
    out_ref[:, 0:768] = acc[0:64].astype(jnp.bfloat16)
    out_ref[:, 768:1536] = jnp.where(len_ref[...] > 1, acc[64:128], 0.0).astype(jnp.bfloat16)


def unpack_kernel(recv_ref, out_ref):
    slot_iota = lax.broadcasted_iota(jnp.int32, (64, 64), 1).astype(jnp.float32)
    for head in range(4):
        rows = pl.ds(16 * head, 16)
        data = jnp.concatenate(
            [recv_ref[rows, 384 * ky : 384 * ky + 384] for ky in range(4)], axis=0
        )
        tail = recv_ref[rows, 1536:1664].astype(jnp.float32)
        slots = jnp.concatenate([tail[:, ky : ky + 1] for ky in range(4)], axis=0)
        pick = jnp.where(slots == slot_iota, 1.0, 0.0).astype(jnp.bfloat16)
        moved = dot_tn(pick, data).astype(jnp.bfloat16)
        for part in range(4):
            out_ref[:, 384 * part + 96 * head : 384 * part + 96 * head + 96] = moved[
                :, 96 * part : 96 * part + 96
            ]


def call(kernel, outs, inputs, scratch=(), scalars=0):
    vmem = pl.BlockSpec(memory_space=pltpu.VMEM)
    smem = pl.BlockSpec(memory_space=pltpu.SMEM)
    single = not isinstance(outs, (list, tuple))
    return pl.pallas_call(
        kernel,
        out_shape=outs,
        in_specs=[smem] * scalars + [vmem] * (len(inputs) - scalars),
        out_specs=vmem if single else [vmem] * len(outs),
        scratch_shapes=list(scratch),
    )(*inputs)


def struct(shape, dtype=jnp.bfloat16):
    return jax.ShapeDtypeStruct(shape, dtype)


def spread(value, axis):
    return [value] + [shift(value, axis, k) for k in (1, 2, 3)]


def on_device(
    tokens, norm_gain_vector, query_weight, key_weight, value_weight, output_weight,
    prefix_cache, lengths, groups, deal_slot, owners,
):
    dp = lax.axis_index("dp")
    m = lax.axis_index("mp")
    y, zh, x, c = dp // 16, (dp // 4) % 4, dp % 4, m % 2
    pos = jnp.stack([y, zh, x, c, m]).astype(jnp.int32)

    by_head = jnp.stack(
        [
            jnp.concatenate(
                [w[:, 96 * h : 96 * h + 96] for w in (query_weight, key_weight, value_weight)], axis=1
            )
            for h in range(4)
        ]
    )
    block = prefix_cache[0]
    prefix_by_head = jnp.stack(
        [
            jnp.concatenate([block[:, 0, 96 * h : 96 * h + 96], block[:, 1, 96 * h : 96 * h + 96]], axis=1)
            for h in range(4)
        ]
    )

    def head_exchange(stacked):
        got = []
        for k in range(4):
            piece = lax.dynamic_index_in_dim(stacked, (y + k) % 4, 0, keepdims=False)
            got.append(piece if k == 0 else shift(piece, "y", k))
        return jnp.concatenate(got, axis=1)

    weight_rows = head_exchange(by_head)
    weight_z = jnp.stack(spread(weight_rows, "zh"))
    weight_pieces = spread(weight_z, "x")

    own = lax.dynamic_index_in_dim(tokens, c, 1, keepdims=False).astype(jnp.float32)
    scale = lax.rsqrt(jnp.mean(own * own, axis=-1, keepdims=True) + 1e-05)
    normed = (own * scale * norm_gain_vector).astype(jnp.bfloat16)
    extras = jnp.stack([deal_slot // 64, deal_slot % 64, lengths, groups], axis=1).astype(jnp.bfloat16)
    extras = jnp.pad(extras, ((0, 0), (0, 124)))
    sent = jnp.concatenate([normed, extras], axis=1)
    own_rows = jnp.stack(spread(sent, "y"))
    other_rows = mp_xor(own_rows, 1)

    prefix_rows = head_exchange(prefix_by_head)
    prefix_z = jnp.stack(spread(prefix_rows, "zh"))
    prefix_pieces = spread(prefix_z, "x")

    out_w = swap_y_mp(output_weight)
    out_z = jnp.stack(spread(out_w, "zh"))
    out_x = jnp.stack(spread(out_z, "x"))
    out_pieces = spread(out_x, "y")

    cosine, sine = rope_tables()
    queries, keyed, valued, info, send = call(
        qkv_kernel,
        [struct((512, 96)), struct((512, 96)), struct((512, 96)), struct((256, 128), jnp.float32), struct((64, 1664))],
        [pos, own_rows, other_rows, *weight_pieces, jnp.asarray(cosine), jnp.asarray(sine)],
        scratch=[pltpu.VMEM((4, 4, 48, 1152), jnp.bfloat16)],
        scalars=1,
    )
    received = lax.all_to_all(send, "dp", split_axis=0, concat_axis=0, tiled=True)

    r4 = jnp.arange(4, dtype=jnp.int32)
    source = (
        ((y - r4) % 4)[:, None, None] * 16 + ((x - r4) % 4)[None, :, None] + ((zh - r4) % 4)[None, None, :] * 4
    ).reshape(64)
    block_group = jnp.sum(
        jnp.where(owners[None, :] == source[:, None], (jnp.arange(64, dtype=jnp.int32) // 16)[None, :], 0), axis=1
    )
    key_group = jnp.broadcast_to(block_group.astype(jnp.float32)[:, None], (64, 64)).reshape(4, 1024)

    attended = call(
        attend_kernel,
        struct((512, 96)),
        [queries, keyed, valued, info, key_group, *prefix_pieces],
        scratch=[
            pltpu.VMEM((4, 256, 1024), jnp.float32),
            pltpu.VMEM((4, 1024, 96), jnp.bfloat16),
            pltpu.VMEM((4, 1024, 96), jnp.bfloat16),
        ],
    )
    attended = attended.reshape(2, 4, 64, 96)
    back = [attended[:, 0]] + [shift(attended[:, k], "y", -k) for k in (1, 2, 3)]
    heads = []
    for h in range(4):
        at = (h - y) % 4
        heads.append(
            jnp.where(at < 2, jnp.where(at == 0, back[0], back[1]), jnp.where(at == 2, back[2], back[3]))
        )
    home = jnp.concatenate(heads, axis=2)
    home_all = [home] + [mp_xor(home, k) for k in (1, 2, 3)]

    out_weight = call(order_kernel, struct((4, 4, 4, 48, 384)), [pos, *out_pieces], scalars=1)
    hidden = call(
        out_kernel, struct((64, 1536)), [pos, *home_all, out_weight, lengths[:, None]], scalars=1
    ).reshape(64, 2, 768)
    suffix_cache = call(unpack_kernel, struct((64, 1536)), [received]).reshape(64, 2, 2, 384)
    return hidden, suffix_cache


def solution(mesh):
    in_specs = (
        P("dp", None, None),
        P(),
        P("dp", "mp"),
        P("dp", "mp"),
        P("dp", "mp"),
        P("dp", "mp"),
        P("dp", None, None, "mp"),
        P("dp"),
        P("dp"),
        P("dp"),
        P(),
    )
    out_specs = (P("dp", None, "mp"), P("dp", None, None, "mp"))
    return jax.shard_map(on_device, mesh=mesh, in_specs=in_specs, out_specs=out_specs, check_vma=False)
```

profile of v0, /device:TPU:1, one launch (start us, length us, event | category | flops | bytes accessed | tf_op | source)
XLA Modules:
  0.0 190.8 jit_solution(11430499770684636707)
XLA Ops:
  3.6 3.6 %collective-permute-start.2 = (bf16[64,3200]{1,0:T(8,128)(2,1)S(1)}, bf16[64,3200]{1,0:T(8,128)(2,1)S(1)}, u32[]{:S(2)}, u32[]{:S(2)}) collective-permute-start(bf16[64,3200]{1,0:T(8,128)(2,1)S(1)} %get-tuple-element.13), channel_id=1, source_target_pairs={{0,192},{4,196},{8,200},{12,204},{16,208},{20,212},{24,216},{28,22... | collective-permute-start | bytes 1228808 | tf_op jit(solution)/shard_map/ppermute | solution.py:27
  12.5 12.3 %collective-permute-done.2 = bf16[64,3200]{1,0:T(8,128)(2,1)S(1)} collective-permute-done((bf16[64,3200]{1,0:T(8,128)(2,1)S(1)}, bf16[64,3200]{1,0:T(8,128)(2,1)S(1)}, u32[]{:S(2)}, u32[]{:S(2)}) %collective-permute-start.2) | collective-permute-done | bytes 409632 | tf_op jit(solution)/shard_map/ppermute | solution.py:27
  24.8 3.6 %collective-permute-start.15 = (bf16[64,192]{1,0:T(8,128)(2,1)S(1)}, bf16[64,192]{1,0:T(8,128)(2,1)S(1)}, u32[]{:S(2)}, u32[]{:S(2)}) collective-permute-start(bf16[64,192]{1,0:T(8,128)(2,1)S(1)} %get-tuple-element.28), channel_id=1, source_target_pairs={{0,192},{4,196},{8,200},{12,204},{16,208},{20,212},{24,216},{28,22... | collective-permute-start | bytes 73736 | tf_op jit(solution)/shard_map/ppermute | solution.py:27
  31.4 5.1 %collective-permute-start.28 = (bf16[48,384]{1,0:T(8,128)(2,1)S(1)}, bf16[48,384]{1,0:T(8,128)(2,1)S(1)}, u32[]{:S(2)}, u32[]{:S(2)}) collective-permute-start(bf16[48,384]{1,0:T(8,128)(2,1)S(1)} %copy-done.22), channel_id=1, source_target_pairs={{0,0},{1,64},{2,128},{3,192},{4,4},{5,68},{6,132},{7,196},{8,8},{9... | collective-permute-start | bytes 110600 | tf_op jit(solution)/shard_map/ppermute | solution.py:40
  38.9 5.6 %collective-permute-start.31 = (bf16[48,384]{1,0:T(8,128)(2,1)S(1)}, bf16[48,384]{1,0:T(8,128)(2,1)S(1)}, u32[]{:S(2)}, u32[]{:S(2)}) collective-permute-start(bf16[48,384]{1,0:T(8,128)(2,1)S(1)} %collective-permute-done.28), channel_id=1, source_target_pairs={{0,48},{4,52},{8,56},{12,60},{16,0},{20,4},{24,8},{28,12},{32,16},... | collective-permute-start | bytes 110600 | tf_op jit(solution)/shard_map/ppermute | solution.py:27
  45.4 2.4 %collective-permute-start.29 = (bf16[48,384]{1,0:T(8,128)(2,1)S(1)}, bf16[48,384]{1,0:T(8,128)(2,1)S(1)}, u32[]{:S(2)}, u32[]{:S(2)}) collective-permute-start(bf16[48,384]{1,0:T(8,128)(2,1)S(1)} %collective-permute-done.28), channel_id=1, source_target_pairs={{0,16},{4,20},{8,24},{12,28},{16,32},{20,36},{24,40},{28,44},{32,4... | collective-permute-start | bytes 110600 | tf_op jit(solution)/shard_map/ppermute | solution.py:27
  51.9 3.4 %collective-permute-start.8 = (bf16[48,1152]{1,0:T(8,128)(2,1)S(1)}, bf16[48,1152]{1,0:T(8,128)(2,1)S(1)}, u32[]{:S(2)}, u32[]{:S(2)}) collective-permute-start(bf16[48,1152]{1,0:T(8,128)(2,1)S(1)} %concatenate.41), channel_id=1, source_target_pairs={{0,32},{4,36},{8,40},{12,44},{16,48},{20,52},{24,56},{28,60},{32,0... | collective-permute-start | bytes 331784 | tf_op jit(solution)/shard_map/ppermute | solution.py:27
  55.3 2.3 %collective-permute-start.7 = (bf16[48,1152]{1,0:T(8,128)(2,1)S(1)}, bf16[48,1152]{1,0:T(8,128)(2,1)S(1)}, u32[]{:S(2)}, u32[]{:S(2)}) collective-permute-start(bf16[48,1152]{1,0:T(8,128)(2,1)S(1)} %concatenate.41), channel_id=1, source_target_pairs={{0,16},{4,20},{8,24},{12,28},{16,32},{20,36},{24,40},{28,44},{32,4... | collective-permute-start | bytes 331784 | tf_op jit(solution)/shard_map/ppermute | solution.py:27
  58.3 2.3 %collective-permute-done.9 = bf16[48,1152]{1,0:T(8,128)(2,1)S(1)} collective-permute-done((bf16[48,1152]{1,0:T(8,128)(2,1)S(1)}, bf16[48,1152]{1,0:T(8,128)(2,1)S(1)}, u32[]{:S(2)}, u32[]{:S(2)}) %collective-permute-start.9) | collective-permute-done | bytes 110624 | tf_op jit(solution)/shard_map/ppermute | solution.py:27
  61.1 2.5 %collective-permute-start.34 = (bf16[4,48,384]{2,1,0:T(8,128)(2,1)}, bf16[4,48,384]{2,1,0:T(8,128)(2,1)S(1)}, u32[]{:S(2)}, u32[]{:S(2)}) collective-permute-start(bf16[4,48,384]{2,1,0:T(8,128)(2,1)} %get-tuple-element.19), channel_id=1, source_target_pairs={{0,12},{4,0},{8,4},{12,8},{16,28},{20,16},{24,20},{28,24},{32,44},... | collective-permute-start | bytes 442376 | tf_op jit(solution)/shard_map/ppermute | solution.py:27
  65.3 2.5 %collective-permute-start.11 = (bf16[4,48,1152]{2,1,0:T(8,128)(2,1)S(1)}, bf16[4,48,1152]{2,1,0:T(8,128)(2,1)}, u32[]{:S(2)}, u32[]{:S(2)}) collective-permute-start(bf16[4,48,1152]{2,1,0:T(8,128)(2,1)S(1)} %pad_maximum_fusion.2.w0), channel_id=1, source_target_pairs={{0,8},{4,12},{8,0},{12,4},{16,24},{20,28},{24,16},{28,20},{32,40},... | collective-permute-start | bytes 1327112 | tf_op jit(solution)/shard_map/ppermute | solution.py:27
  71.0 4.5 %collective-permute-done.16 = bf16[64,768]{1,0:T(8,128)(2,1)S(1)} collective-permute-done((bf16[64,768]{1,0:T(8,128)(2,1)}, bf16[64,768]{1,0:T(8,128)(2,1)S(1)}, u32[]{:S(2)}, u32[]{:S(2)}) %collective-permute-start.16) | collective-permute-done | bytes 98336 | tf_op jit(solution)/shard_map/ppermute | solution.py:27
  75.5 2.8 %collective-permute-start.33 = (bf16[4,48,384]{2,1,0:T(8,128)(2,1)}, bf16[4,48,384]{2,1,0:T(8,128)(2,1)S(1)}, u32[]{:S(2)}, u32[]{:S(2)}) collective-permute-start(bf16[4,48,384]{2,1,0:T(8,128)(2,1)} %get-tuple-element.19), channel_id=1, source_target_pairs={{0,8},{4,12},{8,0},{12,4},{16,24},{20,28},{24,16},{28,20},{32,40},... | collective-permute-start | bytes 442376 | tf_op jit(solution)/shard_map/ppermute | solution.py:27
  86.2 2.9 %collective-permute-start.20 = (bf16[4,64,768]{2,1,0:T(8,128)(2,1)}, bf16[4,64,768]{2,1,0:T(8,128)(2,1)}, u32[]{:S(2)}, u32[]{:S(2)}) collective-permute-start(bf16[4,64,768]{2,1,0:T(8,128)(2,1)} %pad_maximum_fusion.3.p0), channel_id=1, source_target_pairs={{0,8},{4,12},{8,0},{12,4},{16,24},{20,28},{24,16},{28,20},{32,40},... | collective-permute-start | bytes 1179656 | tf_op jit(solution)/shard_map/ppermute | solution.py:27
  94.2 9.4 %collective-permute-done.12.w3 = bf16[4,48,1152]{2,1,0:T(8,128)(2,1)} collective-permute-done((bf16[4,48,1152]{2,1,0:T(8,128)(2,1)S(1)}, bf16[4,48,1152]{2,1,0:T(8,128)(2,1)}, u32[]{:S(2)}, u32[]{:S(2)}) %collective-permute-start.12) | collective-permute-done | bytes 442400 | tf_op jit(solution)/shard_map/ppermute | solution.py:27
  103.6 4.1 %collective-permute-start.35 = (bf16[4,4,48,384]{3,2,1,0:T(8,128)(2,1)S(1)}, bf16[4,4,48,384]{3,2,1,0:T(8,128)(2,1)}, u32[]{:S(2)}, u32[]{:S(2)}) collective-permute-start(bf16[4,4,48,384]{3,2,1,0:T(8,128)(2,1)S(1)} %pad_maximum_fusion.1.w0), channel_id=1, source_target_pairs={{0,64},{4,68},{8,72},{12,76},{16,80},{20,84},{24,88},{28,92},{32,9... | collective-permute-start | bytes 1769480 | tf_op jit(solution)/shard_map/ppermute | solution.py:27
  108.7 6.0 %shard_map.140 = (bf16[512,96]{1,0:T(8,128)(2,1)}, bf16[512,96]{1,0:T(8,128)(2,1)}, bf16[512,96]{1,0:T(8,128)(2,1)}, f32[256,128]{1,0:T(8,128)}, bf16[64,1664]{1,0:T(8,128)(2,1)}) custom-call(s32[5]{0:T(128)} %stack.147.pos_ref, bf16[4,64,3200]{2,1,0:T(8,128)(2,1)} %copy-done.1, bf16[4,64,3200]{2,1,0:T(8,128)(2,1)} %collective-permute-done.3.oth_ref, ...), custom_call_target="tpu_custom_call" | custom-call | tf_op jit(solution)/shard_map/pallas_call | solution.py:203
  116.8 10.6 %shard_map.141 = bf16[512,96]{1,0:T(8,128)(2,1)} custom-call(bf16[512,96]{1,0:T(8,128)(2,1)} %get-tuple-element.7.q_ref, bf16[512,96]{1,0:T(8,128)(2,1)} %get-tuple-element.8.k_ref, bf16[512,96]{1,0:T(8,128)(2,1)} %get-tuple-element.9.v_ref, f32[256,128]{1,0:T(8,128)} %get-tuple-element.10.info_ref, f32[4,1024]{1,0:T(4,128)} %broadcast_in_dim.19.kg_ref, ...), custom_call_target="tpu_custom_call" | custom-call | tf_op jit(solution)/shard_map/pallas_call | solution.py:203
  129.0 4.2 %collective-permute-done.23 = bf16[2,64,96]{2,1,0:T(8,128)(2,1)S(1)} collective-permute-done((bf16[2,64,96]{2,1,0:T(8,128)(2,1)S(1)}, bf16[2,64,96]{2,1,0:T(8,128)(2,1)S(1)}, u32[]{:S(2)}, u32[]{:S(2)}) %collective-permute-start.23) | collective-permute-done | bytes 24608 | tf_op jit(solution)/shard_map/ppermute | solution.py:27
  135.5 16.5 %all-to-all-start = ((bf16[64,2,832]{2,1,0:T(2,128)(2,1)}), bf16[64,2,832]{2,1,0:T(2,128)(2,1)S(1)}, u32[]{:S(2)}, u32[]{:S(2)}) async-start(bf16[64,2,832]{2,1,0:T(2,128)(2,1)} %reshape.148), calls=%async_computation | async-start | bytes 458752 | tf_op jit(solution)/shard_map/all_to_all | solution.py:282
  152.9 9.2 %collective-permute-start.25 = (bf16[2,64,384]{2,1,0:T(8,128)(2,1)S(1)}, bf16[2,64,384]{2,1,0:T(8,128)(2,1)S(1)}, u32[]{:S(2)}, u32[]{:S(2)}) collective-permute-start(bf16[2,64,384]{2,1,0:T(8,128)(2,1)S(1)} %pad_maximum_fusion.8.a0), channel_id=1, source_target_pairs={{0,1},{1,0},{2,3},{3,2},{4,5},{5,4},{6,7},{7,6},{8,9},{9,8},{10,11... | collective-permute-start | bytes 294920 | tf_op jit(solution)/shard_map/ppermute | solution.py:31
  162.1 12.0 %collective-permute-start.26 = (bf16[2,64,384]{2,1,0:T(8,128)(2,1)S(1)}, bf16[2,64,384]{2,1,0:T(8,128)(2,1)S(1)}, u32[]{:S(2)}, u32[]{:S(2)}) collective-permute-start(bf16[2,64,384]{2,1,0:T(8,128)(2,1)S(1)} %pad_maximum_fusion.8.a0), channel_id=1, source_target_pairs={{0,2},{1,3},{2,0},{3,1},{4,6},{5,7},{6,4},{7,5},{8,10},{9,11},{10,... | collective-permute-start | bytes 294920 | tf_op jit(solution)/shard_map/ppermute | solution.py:31
  175.8 3.2 %shard_map.142.w_ref = bf16[4,4,4,48,384]{4,3,2,1,0:T(8,128)(2,1)} custom-call(s32[5]{0:T(128)} %stack.147.pos_ref, bf16[4,4,48,384]{3,2,1,0:T(8,128)(2,1)} %copy-done.2, bf16[4,4,48,384]{3,2,1,0:T(8,128)(2,1)} %collective-permute-done.35.w1, bf16[4,4,48,384]{3,2,1,0:T(8,128)(2,1)} %copy-done.4, bf16[4,4,48,384]{3,2,1,0:T(8,128)(2,1)} %collective-permute-done.37.w3), custom_call_target="tpu_custom_call" | custom-call | tf_op jit(solution)/shard_map/pallas_call | solution.py:203
  180.9 3.4 %shard_map.143 = bf16[64,1536]{1,0:T(8,128)(2,1)} custom-call(s32[5]{0:T(128)} %stack.147.pos_ref, bf16[2,64,384]{2,1,0:T(8,128)(2,1)} %copy-done.7, bf16[2,64,384]{2,1,0:T(8,128)(2,1)} %copy-done.13, bf16[2,64,384]{2,1,0:T(8,128)(2,1)} %copy-done.14, bf16[2,64,384]{2,1,0:T(8,128)(2,1)} %copy-done.15, bf16[4,4,4,48,384]{4,3,2,1,0:T(8,128)(2,1)} %shard_map.142.w_ref, ...), custom_call_target="tpu_custom_call" | custom-call | tf_op jit(solution)/shard_map/pallas_call | solution.py:203
  (158 shorter events, 55.6 us)
Async XLA Ops:
  3.6 21.2 %collective-permute-start.2 = (bf16[64,3200]{1,0:T(8,128)(2,1)S(1)}, bf16[64,3200]{1,0:T(8,128)(2,1)S(1)}, u32[]{:S(2)}, u32[]{:S(2)}) collective-permute-start(bf16[64,3200]{1,0:T(8,128)(2,1)S(1)} %get-tuple-element.13), channel_id=1, source_target_pairs={{0,192},{4,196},{8,200},{12,204},{16,208},{20,212},{24,216},{28,22... | collective-permute-start | bytes 1228808 | tf_op jit(solution)/shard_map/ppermute | solution.py:27
  7.2 21.1 %collective-permute-start.1 = (bf16[64,3200]{1,0:T(8,128)(2,1)S(1)}, bf16[64,3200]{1,0:T(8,128)(2,1)}, u32[]{:S(2)}, u32[]{:S(2)}) collective-permute-start(bf16[64,3200]{1,0:T(8,128)(2,1)S(1)} %get-tuple-element.13), channel_id=1, source_target_pairs={{0,128},{4,132},{8,136},{12,140},{16,144},{20,148},{24,152},{28,15... | collective-permute-start | bytes 1228808 | tf_op jit(solution)/shard_map/ppermute | solution.py:27
  7.5 21.7 %collective-permute-start = (bf16[64,3200]{1,0:T(8,128)(2,1)S(1)}, bf16[64,3200]{1,0:T(8,128)(2,1)S(1)}, u32[]{:S(2)}, u32[]{:S(2)}) collective-permute-start(bf16[64,3200]{1,0:T(8,128)(2,1)S(1)} %get-tuple-element.13), channel_id=1, source_target_pairs={{0,64},{4,68},{8,72},{12,76},{16,80},{20,84},{24,88},{28,92},{32,9... | collective-permute-start | bytes 1228808 | tf_op jit(solution)/shard_map/ppermute | solution.py:27
  8.8 35.6 %collective-permute-start.4 = (bf16[48,288]{1,0:T(8,128)(2,1)S(1)}, bf16[48,288]{1,0:T(8,128)(2,1)}, u32[]{:S(2)}, u32[]{:S(2)}) collective-permute-start(bf16[48,288]{1,0:T(8,128)(2,1)S(1)} %get-tuple-element.22), channel_id=1, source_target_pairs={{0,64},{4,68},{8,72},{12,76},{16,80},{20,84},{24,88},{28,92},{32,9... | collective-permute-start | bytes 82952 | tf_op jit(solution)/shard_map/ppermute | solution.py:27
  10.5 34.9 %collective-permute-start.5 = (bf16[48,288]{1,0:T(8,128)(2,1)S(1)}, bf16[48,288]{1,0:T(8,128)(2,1)}, u32[]{:S(2)}, u32[]{:S(2)}) collective-permute-start(bf16[48,288]{1,0:T(8,128)(2,1)S(1)} %get-tuple-element.21), channel_id=1, source_target_pairs={{0,128},{4,132},{8,136},{12,140},{16,144},{20,148},{24,152},{28,15... | collective-permute-start | bytes 82952 | tf_op jit(solution)/shard_map/ppermute | solution.py:27
  36.6 71.1 %collective-permute-start.3 = (bf16[4,64,3200]{2,1,0:T(8,128)(2,1)S(1)}, bf16[4,64,3200]{2,1,0:T(8,128)(2,1)}, u32[]{:S(2)}, u32[]{:S(2)}) collective-permute-start(bf16[4,64,3200]{2,1,0:T(8,128)(2,1)S(1)} %pad_maximum_fusion.own_ref), channel_id=1, source_target_pairs={{0,1},{1,0},{2,3},{3,2},{4,5},{5,4},{6,7},{7,6},{8,9},{9,8},{10,11... | collective-permute-start | bytes 4915208 | tf_op jit(solution)/shard_map/ppermute | solution.py:31
  37.3 11.2 %collective-permute-start.6 = (bf16[48,288]{1,0:T(8,128)(2,1)S(1)}, bf16[48,288]{1,0:T(8,128)(2,1)S(1)}, u32[]{:S(2)}, u32[]{:S(2)}) collective-permute-start(bf16[48,288]{1,0:T(8,128)(2,1)S(1)} %get-tuple-element.20), channel_id=1, source_target_pairs={{0,192},{4,196},{8,200},{12,204},{16,208},{20,212},{24,216},{28,22... | collective-permute-start | bytes 82952 | tf_op jit(solution)/shard_map/ppermute | solution.py:27
  38.9 11.7 %collective-permute-start.31 = (bf16[48,384]{1,0:T(8,128)(2,1)S(1)}, bf16[48,384]{1,0:T(8,128)(2,1)S(1)}, u32[]{:S(2)}, u32[]{:S(2)}) collective-permute-start(bf16[48,384]{1,0:T(8,128)(2,1)S(1)} %collective-permute-done.28), channel_id=1, source_target_pairs={{0,48},{4,52},{8,56},{12,60},{16,0},{20,4},{24,8},{28,12},{32,16},... | collective-permute-start | bytes 110600 | tf_op jit(solution)/shard_map/ppermute | solution.py:27
  48.5 16.9 %collective-permute-start.18 = (bf16[64,768]{1,0:T(8,128)(2,1)}, bf16[64,768]{1,0:T(8,128)(2,1)}, u32[]{:S(2)}, u32[]{:S(2)}) collective-permute-start(bf16[64,768]{1,0:T(8,128)(2,1)} %pad_maximum_fusion.7), channel_id=1, source_target_pairs={{0,48},{4,52},{8,56},{12,60},{16,0},{20,4},{24,8},{28,12},{32,16},... | collective-permute-start | bytes 294920 | tf_op jit(solution)/shard_map/ppermute | solution.py:27
  61.1 17.1 %collective-permute-start.34 = (bf16[4,48,384]{2,1,0:T(8,128)(2,1)}, bf16[4,48,384]{2,1,0:T(8,128)(2,1)S(1)}, u32[]{:S(2)}, u32[]{:S(2)}) collective-permute-start(bf16[4,48,384]{2,1,0:T(8,128)(2,1)} %get-tuple-element.19), channel_id=1, source_target_pairs={{0,12},{4,0},{8,4},{12,8},{16,28},{20,16},{24,20},{28,24},{32,44},... | collective-permute-start | bytes 442376 | tf_op jit(solution)/shard_map/ppermute | solution.py:27
  64.0 25.1 %collective-permute-start.10 = (bf16[4,48,1152]{2,1,0:T(8,128)(2,1)S(1)}, bf16[4,48,1152]{2,1,0:T(8,128)(2,1)S(1)}, u32[]{:S(2)}, u32[]{:S(2)}) collective-permute-start(bf16[4,48,1152]{2,1,0:T(8,128)(2,1)S(1)} %pad_maximum_fusion.2.w0), channel_id=1, source_target_pairs={{0,4},{4,8},{8,12},{12,0},{16,20},{20,24},{24,28},{28,16},{32,36},... | collective-permute-start | bytes 1327112 | tf_op jit(solution)/shard_map/ppermute | solution.py:27
  65.3 24.3 %collective-permute-start.11 = (bf16[4,48,1152]{2,1,0:T(8,128)(2,1)S(1)}, bf16[4,48,1152]{2,1,0:T(8,128)(2,1)}, u32[]{:S(2)}, u32[]{:S(2)}) collective-permute-start(bf16[4,48,1152]{2,1,0:T(8,128)(2,1)S(1)} %pad_maximum_fusion.2.w0), channel_id=1, source_target_pairs={{0,8},{4,12},{8,0},{12,4},{16,24},{20,28},{24,16},{28,20},{32,40},... | collective-permute-start | bytes 1327112 | tf_op jit(solution)/shard_map/ppermute | solution.py:27
  82.8 31.9 %collective-permute-start.19 = (bf16[4,64,768]{2,1,0:T(8,128)(2,1)}, bf16[4,64,768]{2,1,0:T(8,128)(2,1)}, u32[]{:S(2)}, u32[]{:S(2)}) collective-permute-start(bf16[4,64,768]{2,1,0:T(8,128)(2,1)} %pad_maximum_fusion.3.p0), channel_id=1, source_target_pairs={{0,4},{4,8},{8,12},{12,0},{16,20},{20,24},{24,28},{28,16},{32,36},... | collective-permute-start | bytes 1179656 | tf_op jit(solution)/shard_map/ppermute | solution.py:27
  86.2 30.6 %collective-permute-start.20 = (bf16[4,64,768]{2,1,0:T(8,128)(2,1)}, bf16[4,64,768]{2,1,0:T(8,128)(2,1)}, u32[]{:S(2)}, u32[]{:S(2)}) collective-permute-start(bf16[4,64,768]{2,1,0:T(8,128)(2,1)} %pad_maximum_fusion.3.p0), channel_id=1, source_target_pairs={{0,8},{4,12},{8,0},{12,4},{16,24},{20,28},{24,16},{28,20},{32,40},... | collective-permute-start | bytes 1179656 | tf_op jit(solution)/shard_map/ppermute | solution.py:27
  89.1 27.7 %collective-permute-start.21 = (bf16[4,64,768]{2,1,0:T(8,128)(2,1)}, bf16[4,64,768]{2,1,0:T(8,128)(2,1)}, u32[]{:S(2)}, u32[]{:S(2)}) collective-permute-start(bf16[4,64,768]{2,1,0:T(8,128)(2,1)} %pad_maximum_fusion.3.p0), channel_id=1, source_target_pairs={{0,12},{4,0},{8,4},{12,8},{16,28},{20,16},{24,20},{28,24},{32,44},... | collective-permute-start | bytes 1179656 | tf_op jit(solution)/shard_map/ppermute | solution.py:27
  89.6 13.9 %collective-permute-start.12 = (bf16[4,48,1152]{2,1,0:T(8,128)(2,1)S(1)}, bf16[4,48,1152]{2,1,0:T(8,128)(2,1)}, u32[]{:S(2)}, u32[]{:S(2)}) collective-permute-start(bf16[4,48,1152]{2,1,0:T(8,128)(2,1)S(1)} %pad_maximum_fusion.2.w0), channel_id=1, source_target_pairs={{0,12},{4,0},{8,4},{12,8},{16,28},{20,16},{24,20},{28,24},{32,44},... | collective-permute-start | bytes 1327112 | tf_op jit(solution)/shard_map/ppermute | solution.py:27
  103.6 70.5 %collective-permute-start.35 = (bf16[4,4,48,384]{3,2,1,0:T(8,128)(2,1)S(1)}, bf16[4,4,48,384]{3,2,1,0:T(8,128)(2,1)}, u32[]{:S(2)}, u32[]{:S(2)}) collective-permute-start(bf16[4,4,48,384]{3,2,1,0:T(8,128)(2,1)S(1)} %pad_maximum_fusion.1.w0), channel_id=1, source_target_pairs={{0,64},{4,68},{8,72},{12,76},{16,80},{20,84},{24,88},{28,92},{32,9... | collective-permute-start | bytes 1769480 | tf_op jit(solution)/shard_map/ppermute | solution.py:27
  107.7 67.3 %collective-permute-start.36 = (bf16[4,4,48,384]{3,2,1,0:T(8,128)(2,1)S(1)}, bf16[4,4,48,384]{3,2,1,0:T(8,128)(2,1)S(1)}, u32[]{:S(2)}, u32[]{:S(2)}) collective-permute-start(bf16[4,4,48,384]{3,2,1,0:T(8,128)(2,1)S(1)} %pad_maximum_fusion.1.w0), channel_id=1, source_target_pairs={{0,128},{4,132},{8,136},{12,140},{16,144},{20,148},{24,152},{28,15... | collective-permute-start | bytes 1769480 | tf_op jit(solution)/shard_map/ppermute | solution.py:27
  114.7 60.3 %collective-permute-start.37 = (bf16[4,4,48,384]{3,2,1,0:T(8,128)(2,1)S(1)}, bf16[4,4,48,384]{3,2,1,0:T(8,128)(2,1)}, u32[]{:S(2)}, u32[]{:S(2)}) collective-permute-start(bf16[4,4,48,384]{3,2,1,0:T(8,128)(2,1)S(1)} %pad_maximum_fusion.1.w0), channel_id=1, source_target_pairs={{0,192},{4,196},{8,200},{12,204},{16,208},{20,212},{24,216},{28,22... | collective-permute-start | bytes 1769480 | tf_op jit(solution)/shard_map/ppermute | solution.py:27
  128.3 23.7 %collective-permute-start.24 = (bf16[2,64,96]{2,1,0:T(8,128)(2,1)S(1)}, bf16[2,64,96]{2,1,0:T(8,128)(2,1)S(1)}, u32[]{:S(2)}, u32[]{:S(2)}) collective-permute-start(bf16[2,64,96]{2,1,0:T(8,128)(2,1)S(1)} %get-tuple-element.26), channel_id=1, source_target_pairs={{0,64},{4,68},{8,72},{12,76},{16,80},{20,84},{24,88},{28,92},{32,9... | collective-permute-start | bytes 73736 | tf_op jit(solution)/shard_map/ppermute | solution.py:27
  133.2 18.8 %collective-permute-start.22 = (bf16[2,64,96]{2,1,0:T(8,128)(2,1)S(1)}, bf16[2,64,96]{2,1,0:T(8,128)(2,1)S(1)}, u32[]{:S(2)}, u32[]{:S(2)}) collective-permute-start(bf16[2,64,96]{2,1,0:T(8,128)(2,1)S(1)} %get-tuple-element.24), channel_id=1, source_target_pairs={{0,192},{4,196},{8,200},{12,204},{16,208},{20,212},{24,216},{28,22... | collective-permute-start | bytes 73736 | tf_op jit(solution)/shard_map/ppermute | solution.py:27
  135.5 50.5 %all-to-all-start = ((bf16[64,2,832]{2,1,0:T(2,128)(2,1)}), bf16[64,2,832]{2,1,0:T(2,128)(2,1)S(1)}, u32[]{:S(2)}, u32[]{:S(2)}) async-start(bf16[64,2,832]{2,1,0:T(2,128)(2,1)} %reshape.148), calls=%async_computation | async-start | bytes 458752 | tf_op jit(solution)/shard_map/all_to_all | solution.py:282
  152.9 26.1 %collective-permute-start.25 = (bf16[2,64,384]{2,1,0:T(8,128)(2,1)S(1)}, bf16[2,64,384]{2,1,0:T(8,128)(2,1)S(1)}, u32[]{:S(2)}, u32[]{:S(2)}) collective-permute-start(bf16[2,64,384]{2,1,0:T(8,128)(2,1)S(1)} %pad_maximum_fusion.8.a0), channel_id=1, source_target_pairs={{0,1},{1,0},{2,3},{3,2},{4,5},{5,4},{6,7},{7,6},{8,9},{9,8},{10,11... | collective-permute-start | bytes 294920 | tf_op jit(solution)/shard_map/ppermute | solution.py:31
  162.1 16.9 %collective-permute-start.26 = (bf16[2,64,384]{2,1,0:T(8,128)(2,1)S(1)}, bf16[2,64,384]{2,1,0:T(8,128)(2,1)S(1)}, u32[]{:S(2)}, u32[]{:S(2)}) collective-permute-start(bf16[2,64,384]{2,1,0:T(8,128)(2,1)S(1)} %pad_maximum_fusion.8.a0), channel_id=1, source_target_pairs={{0,2},{1,3},{2,0},{3,1},{4,6},{5,7},{6,4},{7,5},{8,10},{9,11},{10,... | collective-permute-start | bytes 294920 | tf_op jit(solution)/shard_map/ppermute | solution.py:31
  (38 other events, 414.2 us)
where the time goes:
time: 192 us; the launch traced here: 191 us
  starting transfers between devices  98.1 us (51%)
  waiting for transfers between devices  38 us (20%)
  Pallas kernels  25.3 us (13%)
  other arithmetic  14.2 us (7%)
  local copies, waits for them, and re-layouts  14 us (7%)
    ppermute x33, starting transfers between devices, shift(): return lax.ppermute(value, 'dp', dp_shift(axis, amount))  55.1 us
    ppermute x33, waiting for transfers between devices, shift(): return lax.ppermute(value, 'dp', dp_shift(axis, amount))  36.7 us
    pallas_call x5, Pallas kernels, call(): pl.pallas_call(kernel, out_shape=outs, in_specs=[smem] * scalars + [vmem]...  25.3 us
    ppermute x4, starting transfers between devices, mp_xor(): return lax.ppermute(value, 'mp', [(i, i ^ mask) for i in range(4)])  21.4 us
    all_to_all x1, starting transfers between devices, on_device(): lax.all_to_all(send, 'dp', split_axis=0, concat_axis=0, tiled=True)  16.5 us
    ppermute x1, starting transfers between devices, swap_y_mp(): return lax.ppermute(value, ('dp', 'mp'), perm)  5.14 us
    unnamed x50, local copies, waits for them, and re-layouts  4.85 us
  transfers between devices with their start and end apart: 39, of which 10 were waited for; matrix products, arithmetic and copies ran while one was open for 10% of the time, Pallas kernels for 12%

commit v1 on v0

--- a/solution.py
+++ b/solution.py
@@ -14,30 +14,41 @@
 NEG = -1e30
 
 
-def dp_shift(axis, amount):
-    stride = {"y": 16, "zh": 4, "x": 1}[axis]
+def place(dp, m):
+    return dp // 16, (dp // 4) % 4, dp % 4, m // 2, m % 2
+
+
+def index_of(y, zh, x, zl, core):
+    return ((y % 4) * 16 + (zh % 4) * 4 + x % 4) * 4 + zl * 2 + core
+
+
+def move(value, where):
     perm = []
-    for i in range(64):
-        at = (i // stride) % 4
-        perm.append((i, i + (((at + amount) % 4) - at) * stride))
-    return perm
-
-
-def shift(value, axis, amount):
-    return lax.ppermute(value, "dp", dp_shift(axis, amount))
+    for dp in range(64):
+        for m in range(4):
+            perm.append((dp * 4 + m, index_of(*where(*place(dp, m)))))
+    return lax.ppermute(value, ("dp", "mp"), perm)
+
+
+def shift(value, axis, k):
+    step = {"y": (k, 0, 0), "zh": (0, k, 0), "x": (0, 0, k)}[axis]
+    return move(value, lambda y, zh, x, zl, core: (y + step[0], zh + step[1], x + step[2], zl, core))
 
 
 def mp_xor(value, mask):
-    return lax.ppermute(value, "mp", [(i, i ^ mask) for i in range(4)])
+    return move(value, lambda y, zh, x, zl, core: (y, zh, x, zl ^ (mask // 2), core ^ (mask % 2)))
 
 
 def swap_y_mp(value):
-    perm = []
-    for i in range(64):
-        y, rest = divmod(i, 16)
-        for m in range(4):
-            perm.append((i * 4 + m, (m * 16 + rest) * 4 + y))
-    return lax.ppermute(value, ("dp", "mp"), perm)
+    return move(value, lambda y, zh, x, zl, core: (2 * zl + core, zh, x, y // 2, y % 2))
+
+
+def next_chip(value):
+    return move(value, lambda y, zh, x, zl, core: (y, zh + 1 if zl else zh - 1, x, 1 - zl, core))
+
+
+def to_pair(value, side):
+    return move(value, lambda y, zh, x, zl, core: (y, zh + side if zl else zh - side, x, zl, core))
 
 
 def dot_nt(a, b):
@@ -64,17 +75,13 @@
     for kx, piece in enumerate((w0, w1, w2, w3)):
         xa = (x - kx) & 3
         for kz in range(4):
-            wsc[(zh - kz) & 3, xa] = piece[kz]
-    accs = [None, None]
-    for ky in range(4):
-        ya = (y - ky) & 3
-        lanes = pl.ds(pl.multiple_of(ya * 768, 128), 768)
-        rhs = wsc[:, :, :, 288 * ky : 288 * ky + 288].reshape(768, 288)
-        for i, ref in enumerate((own_ref, oth_ref)):
-            part = jnp.dot(
-                ref[:, :, lanes].reshape(256, 768), rhs, preferred_element_type=jnp.float32
-            )
-            accs[i] = part if accs[i] is None else accs[i] + part
+            for ky in range(4):
+                wsc[(y - ky) & 3, (zh - kz) & 3, xa] = piece[ky, :, 288 * kz : 288 * kz + 288]
+    rhs = wsc[...].reshape(3072, 288)
+    accs = [
+        jnp.dot(ref[:, :, 0:3072].reshape(256, 3072), rhs, preferred_element_type=jnp.float32)
+        for ref in (own_ref, oth_ref)
+    ]
     first = c == 0
     slots = (jnp.where(first, accs[0], accs[1]), jnp.where(first, accs[1], accs[0]))
 
@@ -113,29 +120,33 @@
 
 def attend_kernel(q_ref, k_ref, v_ref, info_ref, kg_ref, p0, p1, p2, p3, out_ref, s_ref, keys_ref, values_ref):
     factor = math.log2(math.e) / math.sqrt(HD)
-    for ky in range(4):
-        for kx, piece in enumerate((p0, p1, p2, p3)):
-            rows = pl.ds(256 * kx, 256)
-            keys_ref[ky, rows, :] = piece[:, :, 192 * ky : 192 * ky + 96].reshape(256, 96)
-            values_ref[ky, rows, :] = piece[:, :, 192 * ky + 96 : 192 * ky + 192].reshape(256, 96)
+    for kz in range(4):
+        for ky, piece in enumerate((p0, p1, p2, p3)):
+            for half in range(2):
+                rows = pl.ds(256 * ky + 128 * half, 128)
+                lane = 384 * kz + 192 * half
+                keys_ref[kz, rows, :] = piece[:, :, lane : lane + 96].reshape(128, 96)
+                values_ref[kz, rows, :] = piece[:, :, lane + 96 : lane + 192].reshape(128, 96)
     group = info_ref[:, 3:4]
     live = info_ref[:, 2:3] > 1.5
 
-    def one_slot(t, carry):
-        rows = pl.ds(pl.multiple_of(256 * t, 256), 256)
+    def one_slot(t):
+        rows = pl.ds(256 * t, 256)
         queries = q_ref[rows, :]
         wide = queries.astype(jnp.float32)
         first = jnp.sum(wide * k_ref[0:256, :].astype(jnp.float32), axis=1, keepdims=True)
         second = jnp.sum(wide * k_ref[256:512, :].astype(jnp.float32), axis=1, keepdims=True)
-        second = jnp.where(jnp.logical_and(live, t == 1), second, NEG)
+        second = jnp.where(live, second, NEG) if t == 1 else jnp.full_like(second, NEG)
 
         def score(ky, top):
             scores = dot_nt(queries, keys_ref[ky])
-            scores = jnp.where(group == kg_ref[pl.ds(ky, 1), :], scores, NEG)
+            scores = jnp.where(group == kg_ref[ky : ky + 1, :], scores, NEG)
             s_ref[ky] = scores
             return jnp.maximum(top, jnp.max(scores, axis=1, keepdims=True))
 
-        top = lax.fori_loop(0, 4, score, jnp.maximum(first, second))
+        top = jnp.maximum(first, second)
+        for kz in range(4):
+            top = score(kz, top)
         total = jnp.zeros((256, 1), jnp.float32)
         acc = jnp.zeros((256, 96), jnp.float32)
         for i, value in enumerate((first, second)):
@@ -153,11 +164,12 @@
             )
             return total, acc
 
-        total, acc = lax.fori_loop(0, 4, gather, (total, acc))
+        for kz in range(4):
+            total, acc = gather(kz, (total, acc))
         out_ref[rows, :] = (acc / total).astype(jnp.bfloat16)
-        return carry
-
-    lax.fori_loop(0, 2, one_slot, 0)
+
+    for t in range(2):
+        one_slot(t)
 
 
 def order_kernel(pos_ref, w0, w1, w2, w3, out_ref):
@@ -165,7 +177,7 @@
     for ky, piece in enumerate((w0, w1, w2, w3)):
         for kx in range(4):
             for kz in range(4):
-                out_ref[(y - ky) & 3, (zh - kz) & 3, (x - kx) & 3] = piece[kx, kz]
+                out_ref[(y - ky) & 3, (zh - kz) & 3, (x - kx) & 3] = piece[kx, :, 384 * kz : 384 * kz + 384]
 
 
 def out_kernel(pos_ref, a0, a1, a2, a3, w_ref, len_ref, out_ref):
@@ -180,15 +192,14 @@
 
 
 def unpack_kernel(recv_ref, out_ref):
-    slot_iota = lax.broadcasted_iota(jnp.int32, (64, 64), 1).astype(jnp.float32)
+    slot_iota = lax.broadcasted_iota(jnp.int32, (256, 64), 1).astype(jnp.float32)
+    source_head = (lax.broadcasted_iota(jnp.int32, (256, 1), 0) // 4) % 4
+    data = jnp.concatenate([recv_ref[:, 384 * k : 384 * k + 384] for k in range(4)], axis=0)
+    tail = recv_ref[:, 1536:1664].astype(jnp.float32)
+    slots = jnp.concatenate([tail[:, k : k + 1] for k in range(4)], axis=0)
     for head in range(4):
-        rows = pl.ds(16 * head, 16)
-        data = jnp.concatenate(
-            [recv_ref[rows, 384 * ky : 384 * ky + 384] for ky in range(4)], axis=0
-        )
-        tail = recv_ref[rows, 1536:1664].astype(jnp.float32)
-        slots = jnp.concatenate([tail[:, ky : ky + 1] for ky in range(4)], axis=0)
-        pick = jnp.where(slots == slot_iota, 1.0, 0.0).astype(jnp.bfloat16)
+        own = jnp.where(source_head == head, slots, -1.0)
+        pick = jnp.where(own == slot_iota, 1.0, 0.0).astype(jnp.bfloat16)
         moved = dot_tn(pick, data).astype(jnp.bfloat16)
         for part in range(4):
             out_ref[:, 384 * part + 96 * head : 384 * part + 96 * head + 96] = moved[
@@ -226,32 +237,28 @@
     y, zh, x, c = dp // 16, (dp // 4) % 4, dp % 4, m % 2
     pos = jnp.stack([y, zh, x, c, m]).astype(jnp.int32)
 
-    by_head = jnp.stack(
-        [
+    zl = m // 2
+    block = prefix_cache[0]
+    blank = jnp.zeros((48, 96), jnp.bfloat16)
+    by_head = []
+    for h in range(4):
+        cols = slice(96 * h, 96 * h + 96)
+        projections = [w[:, cols] for w in (query_weight, key_weight, value_weight)]
+        pairs = [block[r : r + 32, kind, cols] for r in (0, 32) for kind in (0, 1)]
+        by_head.append(
             jnp.concatenate(
-                [w[:, 96 * h : 96 * h + 96] for w in (query_weight, key_weight, value_weight)], axis=1
+                [jnp.concatenate([*projections, blank], axis=1), jnp.concatenate(pairs, axis=1)], axis=0
             )
-            for h in range(4)
-        ]
-    )
-    block = prefix_cache[0]
-    prefix_by_head = jnp.stack(
-        [
-            jnp.concatenate([block[:, 0, 96 * h : 96 * h + 96], block[:, 1, 96 * h : 96 * h + 96]], axis=1)
-            for h in range(4)
-        ]
-    )
-
-    def head_exchange(stacked):
-        got = []
-        for k in range(4):
-            piece = lax.dynamic_index_in_dim(stacked, (y + k) % 4, 0, keepdims=False)
-            got.append(piece if k == 0 else shift(piece, "y", k))
-        return jnp.concatenate(got, axis=1)
-
-    weight_rows = head_exchange(by_head)
-    weight_z = jnp.stack(spread(weight_rows, "zh"))
-    weight_pieces = spread(weight_z, "x")
+        )
+    by_head = jnp.stack(by_head)
+    got = []
+    for k in range(4):
+        piece = lax.dynamic_index_in_dim(by_head, (zh + k) % 4, 0, keepdims=False)
+        piece = jnp.concatenate([piece, output_weight], axis=0)
+        got.append(piece if k == 0 else shift(piece, "zh", k))
+    weight_rows = jnp.concatenate([g[0:48, 0:288] for g in got], axis=1)
+    prefix_rows = jnp.concatenate([g[48:80] for g in got], axis=1)
+    out_rows = jnp.concatenate([g[80:128] for g in got], axis=1)
 
     own = lax.dynamic_index_in_dim(tokens, c, 1, keepdims=False).astype(jnp.float32)
     scale = lax.rsqrt(jnp.mean(own * own, axis=-1, keepdims=True) + 1e-05)
@@ -259,36 +266,38 @@
     extras = jnp.stack([deal_slot // 64, deal_slot % 64, lengths, groups], axis=1).astype(jnp.bfloat16)
     extras = jnp.pad(extras, ((0, 0), (0, 124)))
     sent = jnp.concatenate([normed, extras], axis=1)
-    own_rows = jnp.stack(spread(sent, "y"))
+    outer = next_chip(sent)
+    inner = mp_xor(outer, 2)
+    far = next_chip(inner)
+    own_rows = jnp.stack([sent, outer, inner, far])
     other_rows = mp_xor(own_rows, 1)
 
-    prefix_rows = head_exchange(prefix_by_head)
-    prefix_z = jnp.stack(spread(prefix_rows, "zh"))
-    prefix_pieces = spread(prefix_z, "x")
-
-    out_w = swap_y_mp(output_weight)
-    out_z = jnp.stack(spread(out_w, "zh"))
-    out_x = jnp.stack(spread(out_z, "x"))
-    out_pieces = spread(out_x, "y")
+    weight_pieces = spread(jnp.stack(spread(weight_rows, "y")), "x")
+    both = jnp.concatenate([prefix_rows, swap_y_mp(out_rows)], axis=0)
+    both_x = spread(both, "x")
+    prefix_pieces = spread(jnp.stack([b[0:32] for b in both_x]), "y")
+    out_pieces = spread(jnp.stack([b[32:80] for b in both_x]), "y")
 
     cosine, sine = rope_tables()
     queries, keyed, valued, info, send = call(
         qkv_kernel,
         [struct((512, 96)), struct((512, 96)), struct((512, 96)), struct((256, 128), jnp.float32), struct((64, 1664))],
         [pos, own_rows, other_rows, *weight_pieces, jnp.asarray(cosine), jnp.asarray(sine)],
-        scratch=[pltpu.VMEM((4, 4, 48, 1152), jnp.bfloat16)],
+        scratch=[pltpu.VMEM((4, 4, 4, 48, 288), jnp.bfloat16)],
         scalars=1,
     )
     received = lax.all_to_all(send, "dp", split_axis=0, concat_axis=0, tiled=True)
 
     r4 = jnp.arange(4, dtype=jnp.int32)
     source = (
-        ((y - r4) % 4)[:, None, None] * 16 + ((x - r4) % 4)[None, :, None] + ((zh - r4) % 4)[None, None, :] * 4
+        ((zh - r4) % 4)[:, None, None] * 4 + ((y - r4) % 4)[None, :, None] * 16 + ((x - r4) % 4)[None, None, :]
     ).reshape(64)
     block_group = jnp.sum(
         jnp.where(owners[None, :] == source[:, None], (jnp.arange(64, dtype=jnp.int32) // 16)[None, :], 0), axis=1
     )
-    key_group = jnp.broadcast_to(block_group.astype(jnp.float32)[:, None], (64, 64)).reshape(4, 1024)
+    key_group = jnp.broadcast_to(
+        block_group.astype(jnp.float32).reshape(4, 4, 1, 4, 1), (4, 4, 2, 4, 32)
+    ).reshape(4, 1024)
 
     attended = call(
         attend_kernel,
@@ -301,12 +310,12 @@
         ],
     )
     attended = attended.reshape(2, 4, 64, 96)
-    back = [attended[:, 0]] + [shift(attended[:, k], "y", -k) for k in (1, 2, 3)]
+    back = [attended[:, 0], to_pair(attended[:, 1], 1), to_pair(attended[:, 2], -1), to_pair(attended[:, 3], 2)]
     heads = []
     for h in range(4):
-        at = (h - y) % 4
+        at = jnp.where(zl == 0, h - zh, zh - h) % 4
         heads.append(
-            jnp.where(at < 2, jnp.where(at == 0, back[0], back[1]), jnp.where(at == 2, back[2], back[3]))
+            jnp.where(at < 2, jnp.where(at == 0, back[0], back[1]), jnp.where(at == 2, back[3], back[2]))
         )
     home = jnp.concatenate(heads, axis=2)
     home_all = [home] + [mp_xor(home, k) for k in (1, 2, 3)]

time: 192 us -> 171 us (0.89)
  starting transfers between devices: 98.1 us -> 61.6 us
  waiting for transfers between devices: 38 us -> 65.3 us
  other arithmetic: 14.2 us -> 6.41 us
  Pallas kernels: 25.3 us -> 21.9 us
    ppermute x38 -> x29, starting transfers between devices: 81.6 us -> 51.5 us  [move(): return lax.ppermute(value, ('dp', 'mp'), perm)]
    ppermute x38 -> x29, waiting for transfers between devices: 38 us -> 65.3 us  [move(): return lax.ppermute(value, ('dp', 'mp'), perm)]
    all_to_all x1, starting transfers between devices: 16.5 us -> 10 us  [on_device(): lax.all_to_all(send, 'dp', split_axis=0, concat_axis=0, tiled=True)]
    another operation x14 -> x10, other arithmetic: 7.22 us -> 3.28 us  [the longest x2 1.3 us: on_device(): own_rows = jnp.stack([sent, outer, inner, far])]
    pallas_call x5, Pallas kernels: 25.3 us -> 21.9 us  [call(): pl.pallas_call(kernel, out_shape=outs, in_specs=[smem] * scalars + [vmem]...]
    unnamed x50 -> x52, local copies, waits for them, and re-layouts: 4.85 us -> 5 us
  transfers between devices with their start and end apart: 39 -> 30, of which waited for: 10 -> 11; matrix products, arithmetic and copies ran while one was open for 10% -> 7% of each run, Pallas kernels for 12% -> 12%
where the time goes in v1:
time: 171 us; the launch traced here: 170 us
  waiting for transfers between devices  65.3 us (38%)
  starting transfers between devices  61.6 us (36%)
  Pallas kernels  21.9 us (13%)
  local copies, waits for them, and re-layouts  13.5 us (8%)
  other arithmetic  6.41 us (4%)
    ppermute x29, waiting for transfers between devices, move(): return lax.ppermute(value, ('dp', 'mp'), perm)  65.3 us
    ppermute x29, starting transfers between devices, move(): return lax.ppermute(value, ('dp', 'mp'), perm)  51.5 us
    pallas_call x5, Pallas kernels, call(): pl.pallas_call(kernel, out_shape=outs, in_specs=[smem] * scalars + [vmem]...  21.9 us
    all_to_all x1, starting transfers between devices, on_device(): lax.all_to_all(send, 'dp', split_axis=0, concat_axis=0, tiled=True)  10 us
    unnamed x52, local copies, waits for them, and re-layouts  5 us
  transfers between devices with their start and end apart: 30, of which 11 were waited for; matrix products, arithmetic and copies ran while one was open for 7% of the time, Pallas kernels for 12%

profile of v1, /device:TPU:1, one launch (start us, length us, event | category | flops | bytes accessed | tf_op | source)
XLA Modules:
  0.0 169.9 jit_solution(6805316257766438711)
XLA Ops:
  3.6 6.5 %collective-permute-start = (bf16[64,3200]{1,0:T(8,128)(2,1)S(1)}, bf16[64,3200]{1,0:T(8,128)(2,1)S(1)}, u32[]{:S(2)}, u32[]{:S(2)}) collective-permute-start(bf16[64,3200]{1,0:T(8,128)(2,1)S(1)} %get-tuple-element.13), channel_id=1, source_target_pairs={{0,50},{1,51},{2,16},{3,17},{4,54},{5,55},{6,20},{7,21},{8,58},{9,... | collective-permute-start | bytes 1228808 | tf_op jit(solution)/shard_map/ppermute | solution.py:30
  10.9 3.2 %collective-permute-start.5 = (bf16[128,384]{1,0:T(8,128)(2,1)S(1)}, bf16[128,384]{1,0:T(8,128)(2,1)S(1)}, u32[]{:S(2)}, u32[]{:S(2)}) collective-permute-start(bf16[128,384]{1,0:T(8,128)(2,1)S(1)} %get-tuple-element.42), channel_id=1, source_target_pairs={{0,32},{1,33},{2,34},{3,35},{4,36},{5,37},{6,38},{7,39},{8,40},{9,... | collective-permute-start | bytes 294920 | tf_op jit(solution)/shard_map/ppermute | solution.py:30
  16.4 10.2 %collective-permute-done.6 = bf16[128,384]{1,0:T(8,128)(2,1)S(1)} collective-permute-done((bf16[128,384]{1,0:T(8,128)(2,1)S(1)}, bf16[128,384]{1,0:T(8,128)(2,1)S(1)}, u32[]{:S(2)}, u32[]{:S(2)}) %collective-permute-start.6) | collective-permute-done | bytes 98336 | tf_op jit(solution)/shard_map/ppermute | solution.py:30
  26.7 4.6 %collective-permute-start.13 = (bf16[48,1536]{1,0:T(8,128)(2,1)S(1)}, bf16[48,1536]{1,0:T(8,128)(2,1)S(1)}, u32[]{:S(2)}, u32[]{:S(2)}) collective-permute-start(bf16[48,1536]{1,0:T(8,128)(2,1)S(1)} %pad_maximum_fusion.6), channel_id=1, source_target_pairs={{0,0},{1,64},{2,128},{3,192},{4,4},{5,68},{6,132},{7,196},{8,8},{9... | collective-permute-start | bytes 442376 | tf_op jit(solution)/shard_map/ppermute | solution.py:30
  33.3 2.9 %collective-permute-start.9 = (bf16[48,1152]{1,0:T(8,128)(2,1)S(1)}, bf16[48,1152]{1,0:T(8,128)(2,1)S(1)}, u32[]{:S(2)}, u32[]{:S(2)}) collective-permute-start(bf16[48,1152]{1,0:T(8,128)(2,1)S(1)} %concatenate.79), channel_id=1, source_target_pairs={{0,192},{1,193},{2,194},{3,195},{4,196},{5,197},{6,198},{7,199},{8... | collective-permute-start | bytes 331784 | tf_op jit(solution)/shard_map/ppermute | solution.py:30
  37.7 2.6 %collective-permute-start.16 = (bf16[80,1536]{1,0:T(8,128)(2,1)S(1)}, bf16[80,1536]{1,0:T(8,128)(2,1)S(1)}, u32[]{:S(2)}, u32[]{:S(2)}) collective-permute-start(bf16[80,1536]{1,0:T(8,128)(2,1)S(1)} %pad_maximum_fusion.5), channel_id=1, source_target_pairs={{0,12},{1,13},{2,14},{3,15},{4,0},{5,1},{6,2},{7,3},{8,4},{9,5},{1... | collective-permute-start | bytes 737288 | tf_op jit(solution)/shard_map/ppermute | solution.py:30
  42.7 2.4 %collective-permute-done.7 = bf16[48,1152]{1,0:T(8,128)(2,1)S(1)} collective-permute-done((bf16[48,1152]{1,0:T(8,128)(2,1)S(1)}, bf16[48,1152]{1,0:T(8,128)(2,1)S(1)}, u32[]{:S(2)}, u32[]{:S(2)}) %collective-permute-start.7) | collective-permute-done | bytes 110624 | tf_op jit(solution)/shard_map/ppermute | solution.py:30
  46.4 2.5 %collective-permute-start.11 = (bf16[4,48,1152]{2,1,0:T(8,128)(2,1)S(1)}, bf16[4,48,1152]{2,1,0:T(8,128)(2,1)S(1)}, u32[]{:S(2)}, u32[]{:S(2)}) collective-permute-start(bf16[4,48,1152]{2,1,0:T(8,128)(2,1)S(1)} %pad_maximum_fusion.2.w0), channel_id=1, source_target_pairs={{0,8},{1,9},{2,10},{3,11},{4,12},{5,13},{6,14},{7,15},{8,0},{9,1},... | collective-permute-start | bytes 1327112 | tf_op jit(solution)/shard_map/ppermute | solution.py:30
  50.7 22.7 %collective-permute-done.15 = bf16[80,1536]{1,0:T(8,128)(2,1)S(1)} collective-permute-done((bf16[80,1536]{1,0:T(8,128)(2,1)S(1)}, bf16[80,1536]{1,0:T(8,128)(2,1)S(1)}, u32[]{:S(2)}, u32[]{:S(2)}) %collective-permute-start.15) | collective-permute-done | bytes 245792 | tf_op jit(solution)/shard_map/ppermute | solution.py:30
  73.7 8.5 %collective-permute-done.1 = bf16[64,3200]{1,0:T(8,128)(2,1)S(1)} collective-permute-done((bf16[64,3200]{1,0:T(8,128)(2,1)S(1)}, bf16[64,3200]{1,0:T(8,128)(2,1)S(1)}, u32[]{:S(2)}, u32[]{:S(2)}) %collective-permute-start.1) | collective-permute-done | bytes 409632 | tf_op jit(solution)/shard_map/ppermute | solution.py:30
  82.2 3.0 %collective-permute-start.2 = (bf16[64,3200]{1,0:T(8,128)(2,1)S(1)}, bf16[64,3200]{1,0:T(8,128)(2,1)S(1)}, u32[]{:S(2)}, u32[]{:S(2)}) collective-permute-start(bf16[64,3200]{1,0:T(8,128)(2,1)S(1)} %collective-permute-done.1), channel_id=1, source_target_pairs={{0,50},{1,51},{2,16},{3,17},{4,54},{5,55},{6,20},{7,21},{8,58},{9,... | collective-permute-start | bytes 1228808 | tf_op jit(solution)/shard_map/ppermute | solution.py:30
  85.2 6.7 %collective-permute-done.2 = bf16[64,3200]{1,0:T(8,128)(2,1)S(1)} collective-permute-done((bf16[64,3200]{1,0:T(8,128)(2,1)S(1)}, bf16[64,3200]{1,0:T(8,128)(2,1)S(1)}, u32[]{:S(2)}, u32[]{:S(2)}) %collective-permute-start.2) | collective-permute-done | bytes 409632 | tf_op jit(solution)/shard_map/ppermute | solution.py:30
  93.1 3.8 %collective-permute-start.3 = (bf16[4,64,3200]{2,1,0:T(8,128)(2,1)S(1)}, bf16[4,64,3200]{2,1,0:T(8,128)(2,1)S(1)}, u32[]{:S(2)}, u32[]{:S(2)}) collective-permute-start(bf16[4,64,3200]{2,1,0:T(8,128)(2,1)S(1)} %pad_maximum_fusion.own_ref), channel_id=1, source_target_pairs={{0,1},{1,0},{2,3},{3,2},{4,5},{5,4},{6,7},{7,6},{8,9},{9,8},{10,11... | collective-permute-start | bytes 4915208 | tf_op jit(solution)/shard_map/ppermute | solution.py:30
  102.8 2.3 %collective-permute-start.27 = (bf16[4,48,1536]{2,1,0:T(8,128)(2,1)S(1)}, bf16[4,48,1536]{2,1,0:T(8,128)(2,1)}, u32[]{:S(2)}, u32[]{:S(2)}) collective-permute-start(bf16[4,48,1536]{2,1,0:T(8,128)(2,1)S(1)} %pad_maximum_fusion.1.w0), channel_id=1, source_target_pairs={{0,128},{1,129},{2,130},{3,131},{4,132},{5,133},{6,134},{7,135},{8... | collective-permute-start | bytes 1769480 | tf_op jit(solution)/shard_map/ppermute | solution.py:30
  105.0 6.4 %shard_map.140 = (bf16[512,96]{1,0:T(8,128)(2,1)}, bf16[512,96]{1,0:T(8,128)(2,1)}, bf16[512,96]{1,0:T(8,128)(2,1)}, f32[256,128]{1,0:T(8,128)}, bf16[64,1664]{1,0:T(8,128)(2,1)}) custom-call(s32[5]{0:T(128)} %stack.117.pos_ref, bf16[4,64,3200]{2,1,0:T(8,128)(2,1)} %copy-done.1, bf16[4,64,3200]{2,1,0:T(8,128)(2,1)} %copy-done.4, ...), custom_call_target="tpu_custom_call" | custom-call | tf_op jit(solution)/shard_map/pallas_call | solution.py:214
  111.4 6.6 %collective-permute-done.17.p1 = bf16[4,32,1536]{2,1,0:T(8,128)(2,1)S(1)} collective-permute-done((bf16[4,32,1536]{2,1,0:T(8,128)(2,1)}, bf16[4,32,1536]{2,1,0:T(8,128)(2,1)S(1)}, u32[]{:S(2)}, u32[]{:S(2)}) %collective-permute-start.17) | collective-permute-done | bytes 393248 | tf_op jit(solution)/shard_map/ppermute | solution.py:30
  118.8 6.8 %shard_map.141 = bf16[512,96]{1,0:T(8,128)(2,1)} custom-call(bf16[512,96]{1,0:T(8,128)(2,1)} %get-tuple-element.7.q_ref, bf16[512,96]{1,0:T(8,128)(2,1)} %get-tuple-element.8.k_ref, bf16[512,96]{1,0:T(8,128)(2,1)} %get-tuple-element.9.v_ref, f32[256,128]{1,0:T(8,128)} %get-tuple-element.10.info_ref, f32[4,1024]{1,0:T(4,128)} %reshape.146.kg_ref, ...), custom_call_target="tpu_custom_call" | custom-call | tf_op jit(solution)/shard_map/pallas_call | solution.py:214
  126.4 3.2 %collective-permute-start.21 = (bf16[2,64,96]{2,1,0:T(8,128)(2,1)S(1)}, bf16[2,64,96]{2,1,0:T(8,128)(2,1)S(1)}, u32[]{:S(2)}, u32[]{:S(2)}) collective-permute-start(bf16[2,64,96]{2,1,0:T(8,128)(2,1)S(1)} %get-tuple-element.23), channel_id=1, source_target_pairs={{0,32},{1,33},{2,34},{3,35},{4,36},{5,37},{6,38},{7,39},{8,40},{9,... | collective-permute-start | bytes 73736 | tf_op jit(solution)/shard_map/ppermute | solution.py:30
  130.0 3.2 %collective-permute-done.21 = bf16[2,64,96]{2,1,0:T(8,128)(2,1)S(1)} collective-permute-done((bf16[2,64,96]{2,1,0:T(8,128)(2,1)S(1)}, bf16[2,64,96]{2,1,0:T(8,128)(2,1)S(1)}, u32[]{:S(2)}, u32[]{:S(2)}) %collective-permute-start.21) | collective-permute-done | bytes 24608 | tf_op jit(solution)/shard_map/ppermute | solution.py:30
  136.7 10.0 %all-to-all-start = ((bf16[64,2,832]{2,1,0:T(2,128)(2,1)}), bf16[64,2,832]{2,1,0:T(2,128)(2,1)S(1)}, u32[]{:S(2)}, u32[]{:S(2)}) async-start(bf16[64,2,832]{2,1,0:T(2,128)(2,1)} %reshape.151), calls=%async_computation | async-start | bytes 458752 | tf_op jit(solution)/shard_map/all_to_all | solution.py:289
  147.7 2.4 %collective-permute-start.23 = (bf16[2,64,384]{2,1,0:T(8,128)(2,1)S(1)}, bf16[2,64,384]{2,1,0:T(8,128)(2,1)S(1)}, u32[]{:S(2)}, u32[]{:S(2)}) collective-permute-start(bf16[2,64,384]{2,1,0:T(8,128)(2,1)S(1)} %pad_maximum_fusion.14.a0), channel_id=1, source_target_pairs={{0,1},{1,0},{2,3},{3,2},{4,5},{5,4},{6,7},{7,6},{8,9},{9,8},{10,11... | collective-permute-start | bytes 294920 | tf_op jit(solution)/shard_map/ppermute | solution.py:30
  150.1 2.5 %collective-permute-start.24 = (bf16[2,64,384]{2,1,0:T(8,128)(2,1)S(1)}, bf16[2,64,384]{2,1,0:T(8,128)(2,1)S(1)}, u32[]{:S(2)}, u32[]{:S(2)}) collective-permute-start(bf16[2,64,384]{2,1,0:T(8,128)(2,1)S(1)} %pad_maximum_fusion.14.a0), channel_id=1, source_target_pairs={{0,2},{1,3},{2,0},{3,1},{4,6},{5,7},{6,4},{7,5},{8,10},{9,11},{10,... | collective-permute-start | bytes 294920 | tf_op jit(solution)/shard_map/ppermute | solution.py:30
  154.3 3.2 %shard_map.142.w_ref = bf16[4,4,4,48,384]{4,3,2,1,0:T(8,128)(2,1)} custom-call(s32[5]{0:T(128)} %stack.117.pos_ref, bf16[4,48,1536]{2,1,0:T(8,128)(2,1)} %copy-done.2, bf16[4,48,1536]{2,1,0:T(8,128)(2,1)} %collective-permute-done.26.w1, bf16[4,48,1536]{2,1,0:T(8,128)(2,1)} %collective-permute-done.27.w2, bf16[4,48,1536]{2,1,0:T(8,128)(2,1)} %copy-done.5), custom_call_target="tpu_custom_call" | custom-call | tf_op jit(solution)/shard_map/pallas_call | solution.py:214
  160.1 3.4 %shard_map.143 = bf16[64,1536]{1,0:T(8,128)(2,1)} custom-call(s32[5]{0:T(128)} %stack.117.pos_ref, bf16[2,64,384]{2,1,0:T(8,128)(2,1)} %copy-done.10, bf16[2,64,384]{2,1,0:T(8,128)(2,1)} %copy-done.14, bf16[2,64,384]{2,1,0:T(8,128)(2,1)} %copy-done.15, bf16[2,64,384]{2,1,0:T(8,128)(2,1)} %copy-done.16, bf16[4,4,4,48,384]{4,3,2,1,0:T(8,128)(2,1)} %shard_map.142.w_ref, ...), custom_call_target="tpu_custom_call" | custom-call | tf_op jit(solution)/shard_map/pallas_call | solution.py:214
  (156 shorter events, 39.0 us)
Async XLA Ops:
  3.6 46.7 %collective-permute-start = (bf16[64,3200]{1,0:T(8,128)(2,1)S(1)}, bf16[64,3200]{1,0:T(8,128)(2,1)S(1)}, u32[]{:S(2)}, u32[]{:S(2)}) collective-permute-start(bf16[64,3200]{1,0:T(8,128)(2,1)S(1)} %get-tuple-element.13), channel_id=1, source_target_pairs={{0,50},{1,51},{2,16},{3,17},{4,54},{5,55},{6,20},{7,21},{8,58},{9,... | collective-permute-start | bytes 1228808 | tf_op jit(solution)/shard_map/ppermute | solution.py:30
  10.8 15.8 %collective-permute-start.4 = (bf16[128,384]{1,0:T(8,128)(2,1)S(1)}, bf16[128,384]{1,0:T(8,128)(2,1)S(1)}, u32[]{:S(2)}, u32[]{:S(2)}) collective-permute-start(bf16[128,384]{1,0:T(8,128)(2,1)S(1)} %get-tuple-element.43), channel_id=1, source_target_pairs={{0,16},{1,17},{2,18},{3,19},{4,20},{5,21},{6,22},{7,23},{8,24},{9,... | collective-permute-start | bytes 294920 | tf_op jit(solution)/shard_map/ppermute | solution.py:30
  10.9 15.7 %collective-permute-start.5 = (bf16[128,384]{1,0:T(8,128)(2,1)S(1)}, bf16[128,384]{1,0:T(8,128)(2,1)S(1)}, u32[]{:S(2)}, u32[]{:S(2)}) collective-permute-start(bf16[128,384]{1,0:T(8,128)(2,1)S(1)} %get-tuple-element.42), channel_id=1, source_target_pairs={{0,32},{1,33},{2,34},{3,35},{4,36},{5,37},{6,38},{7,39},{8,40},{9,... | collective-permute-start | bytes 294920 | tf_op jit(solution)/shard_map/ppermute | solution.py:30
  14.2 12.4 %collective-permute-start.6 = (bf16[128,384]{1,0:T(8,128)(2,1)S(1)}, bf16[128,384]{1,0:T(8,128)(2,1)S(1)}, u32[]{:S(2)}, u32[]{:S(2)}) collective-permute-start(bf16[128,384]{1,0:T(8,128)(2,1)S(1)} %get-tuple-element.41), channel_id=1, source_target_pairs={{0,48},{1,49},{2,50},{3,51},{4,52},{5,53},{6,54},{7,55},{8,56},{9,... | collective-permute-start | bytes 294920 | tf_op jit(solution)/shard_map/ppermute | solution.py:30
  26.7 10.9 %collective-permute-start.13 = (bf16[48,1536]{1,0:T(8,128)(2,1)S(1)}, bf16[48,1536]{1,0:T(8,128)(2,1)S(1)}, u32[]{:S(2)}, u32[]{:S(2)}) collective-permute-start(bf16[48,1536]{1,0:T(8,128)(2,1)S(1)} %pad_maximum_fusion.6), channel_id=1, source_target_pairs={{0,0},{1,64},{2,128},{3,192},{4,4},{5,68},{6,132},{7,196},{8,8},{9... | collective-permute-start | bytes 442376 | tf_op jit(solution)/shard_map/ppermute | solution.py:30
  37.7 12.4 %collective-permute-start.16 = (bf16[80,1536]{1,0:T(8,128)(2,1)S(1)}, bf16[80,1536]{1,0:T(8,128)(2,1)S(1)}, u32[]{:S(2)}, u32[]{:S(2)}) collective-permute-start(bf16[80,1536]{1,0:T(8,128)(2,1)S(1)} %pad_maximum_fusion.5), channel_id=1, source_target_pairs={{0,12},{1,13},{2,14},{3,15},{4,0},{5,1},{6,2},{7,3},{8,4},{9,5},{1... | collective-permute-start | bytes 737288 | tf_op jit(solution)/shard_map/ppermute | solution.py:30
  45.2 52.6 %collective-permute-start.10 = (bf16[4,48,1152]{2,1,0:T(8,128)(2,1)S(1)}, bf16[4,48,1152]{2,1,0:T(8,128)(2,1)S(1)}, u32[]{:S(2)}, u32[]{:S(2)}) collective-permute-start(bf16[4,48,1152]{2,1,0:T(8,128)(2,1)S(1)} %pad_maximum_fusion.2.w0), channel_id=1, source_target_pairs={{0,4},{1,5},{2,6},{3,7},{4,8},{5,9},{6,10},{7,11},{8,12},{9,13},{1... | collective-permute-start | bytes 1327112 | tf_op jit(solution)/shard_map/ppermute | solution.py:30
  46.4 52.5 %collective-permute-start.11 = (bf16[4,48,1152]{2,1,0:T(8,128)(2,1)S(1)}, bf16[4,48,1152]{2,1,0:T(8,128)(2,1)S(1)}, u32[]{:S(2)}, u32[]{:S(2)}) collective-permute-start(bf16[4,48,1152]{2,1,0:T(8,128)(2,1)S(1)} %pad_maximum_fusion.2.w0), channel_id=1, source_target_pairs={{0,8},{1,9},{2,10},{3,11},{4,12},{5,13},{6,14},{7,15},{8,0},{9,1},... | collective-permute-start | bytes 1327112 | tf_op jit(solution)/shard_map/ppermute | solution.py:30
  48.9 51.9 %collective-permute-start.12 = (bf16[4,48,1152]{2,1,0:T(8,128)(2,1)S(1)}, bf16[4,48,1152]{2,1,0:T(8,128)(2,1)S(1)}, u32[]{:S(2)}, u32[]{:S(2)}) collective-permute-start(bf16[4,48,1152]{2,1,0:T(8,128)(2,1)S(1)} %pad_maximum_fusion.2.w0), channel_id=1, source_target_pairs={{0,12},{1,13},{2,14},{3,15},{4,0},{5,1},{6,2},{7,3},{8,4},{9,5},{1... | collective-permute-start | bytes 1327112 | tf_op jit(solution)/shard_map/ppermute | solution.py:30
  50.0 23.4 %collective-permute-start.15 = (bf16[80,1536]{1,0:T(8,128)(2,1)S(1)}, bf16[80,1536]{1,0:T(8,128)(2,1)S(1)}, u32[]{:S(2)}, u32[]{:S(2)}) collective-permute-start(bf16[80,1536]{1,0:T(8,128)(2,1)S(1)} %pad_maximum_fusion.5), channel_id=1, source_target_pairs={{0,8},{1,9},{2,10},{3,11},{4,12},{5,13},{6,14},{7,15},{8,0},{9,1},... | collective-permute-start | bytes 737288 | tf_op jit(solution)/shard_map/ppermute | solution.py:30
  50.3 34.9 %collective-permute-start.14 = (bf16[80,1536]{1,0:T(8,128)(2,1)S(1)}, bf16[80,1536]{1,0:T(8,128)(2,1)S(1)}, u32[]{:S(2)}, u32[]{:S(2)}) collective-permute-start(bf16[80,1536]{1,0:T(8,128)(2,1)S(1)} %pad_maximum_fusion.5), channel_id=1, source_target_pairs={{0,4},{1,5},{2,6},{3,7},{4,8},{5,9},{6,10},{7,11},{8,12},{9,13},{1... | collective-permute-start | bytes 737288 | tf_op jit(solution)/shard_map/ppermute | solution.py:30
  73.5 8.7 %collective-permute-start.1 = (bf16[64,3200]{1,0:T(8,128)(2,1)S(1)}, bf16[64,3200]{1,0:T(8,128)(2,1)S(1)}, u32[]{:S(2)}, u32[]{:S(2)}) collective-permute-start(bf16[64,3200]{1,0:T(8,128)(2,1)S(1)} %collective-permute-done), channel_id=1, source_target_pairs={{0,2},{1,3},{2,0},{3,1},{4,6},{5,7},{6,4},{7,5},{8,10},{9,11},{10,... | collective-permute-start | bytes 1228808 | tf_op jit(solution)/shard_map/ppermute | solution.py:30
  82.2 9.7 %collective-permute-start.2 = (bf16[64,3200]{1,0:T(8,128)(2,1)S(1)}, bf16[64,3200]{1,0:T(8,128)(2,1)S(1)}, u32[]{:S(2)}, u32[]{:S(2)}) collective-permute-start(bf16[64,3200]{1,0:T(8,128)(2,1)S(1)} %collective-permute-done.1), channel_id=1, source_target_pairs={{0,50},{1,51},{2,16},{3,17},{4,54},{5,55},{6,20},{7,21},{8,58},{9,... | collective-permute-start | bytes 1228808 | tf_op jit(solution)/shard_map/ppermute | solution.py:30
  93.1 8.2 %collective-permute-start.3 = (bf16[4,64,3200]{2,1,0:T(8,128)(2,1)S(1)}, bf16[4,64,3200]{2,1,0:T(8,128)(2,1)S(1)}, u32[]{:S(2)}, u32[]{:S(2)}) collective-permute-start(bf16[4,64,3200]{2,1,0:T(8,128)(2,1)S(1)} %pad_maximum_fusion.own_ref), channel_id=1, source_target_pairs={{0,1},{1,0},{2,3},{3,2},{4,5},{5,4},{6,7},{7,6},{8,9},{9,8},{10,11... | collective-permute-start | bytes 4915208 | tf_op jit(solution)/shard_map/ppermute | solution.py:30
  97.8 20.3 %collective-permute-start.17 = (bf16[4,32,1536]{2,1,0:T(8,128)(2,1)}, bf16[4,32,1536]{2,1,0:T(8,128)(2,1)S(1)}, u32[]{:S(2)}, u32[]{:S(2)}) collective-permute-start(bf16[4,32,1536]{2,1,0:T(8,128)(2,1)} %pad_maximum_fusion.3.p0), channel_id=1, source_target_pairs={{0,64},{1,65},{2,66},{3,67},{4,68},{5,69},{6,70},{7,71},{8,72},{9,... | collective-permute-start | bytes 1179656 | tf_op jit(solution)/shard_map/ppermute | solution.py:30
  97.8 20.3 %collective-permute-start.18 = (bf16[4,32,1536]{2,1,0:T(8,128)(2,1)}, bf16[4,32,1536]{2,1,0:T(8,128)(2,1)}, u32[]{:S(2)}, u32[]{:S(2)}) collective-permute-start(bf16[4,32,1536]{2,1,0:T(8,128)(2,1)} %pad_maximum_fusion.3.p0), channel_id=1, source_target_pairs={{0,128},{1,129},{2,130},{3,131},{4,132},{5,133},{6,134},{7,135},{8... | collective-permute-start | bytes 1179656 | tf_op jit(solution)/shard_map/ppermute | solution.py:30
  99.0 19.7 %collective-permute-start.19 = (bf16[4,32,1536]{2,1,0:T(8,128)(2,1)}, bf16[4,32,1536]{2,1,0:T(8,128)(2,1)}, u32[]{:S(2)}, u32[]{:S(2)}) collective-permute-start(bf16[4,32,1536]{2,1,0:T(8,128)(2,1)} %pad_maximum_fusion.3.p0), channel_id=1, source_target_pairs={{0,192},{1,193},{2,194},{3,195},{4,196},{5,197},{6,198},{7,199},{8... | collective-permute-start | bytes 1179656 | tf_op jit(solution)/shard_map/ppermute | solution.py:30
  100.8 51.9 %collective-permute-start.26 = (bf16[4,48,1536]{2,1,0:T(8,128)(2,1)S(1)}, bf16[4,48,1536]{2,1,0:T(8,128)(2,1)}, u32[]{:S(2)}, u32[]{:S(2)}) collective-permute-start(bf16[4,48,1536]{2,1,0:T(8,128)(2,1)S(1)} %pad_maximum_fusion.1.w0), channel_id=1, source_target_pairs={{0,64},{1,65},{2,66},{3,67},{4,68},{5,69},{6,70},{7,71},{8,72},{9,... | collective-permute-start | bytes 1769480 | tf_op jit(solution)/shard_map/ppermute | solution.py:30
  102.8 50.7 %collective-permute-start.27 = (bf16[4,48,1536]{2,1,0:T(8,128)(2,1)S(1)}, bf16[4,48,1536]{2,1,0:T(8,128)(2,1)}, u32[]{:S(2)}, u32[]{:S(2)}) collective-permute-start(bf16[4,48,1536]{2,1,0:T(8,128)(2,1)S(1)} %pad_maximum_fusion.1.w0), channel_id=1, source_target_pairs={{0,128},{1,129},{2,130},{3,131},{4,132},{5,133},{6,134},{7,135},{8... | collective-permute-start | bytes 1769480 | tf_op jit(solution)/shard_map/ppermute | solution.py:30
  118.1 35.4 %collective-permute-start.28 = (bf16[4,48,1536]{2,1,0:T(8,128)(2,1)S(1)}, bf16[4,48,1536]{2,1,0:T(8,128)(2,1)S(1)}, u32[]{:S(2)}, u32[]{:S(2)}) collective-permute-start(bf16[4,48,1536]{2,1,0:T(8,128)(2,1)S(1)} %pad_maximum_fusion.1.w0), channel_id=1, source_target_pairs={{0,192},{1,193},{2,194},{3,195},{4,196},{5,197},{6,198},{7,199},{8... | collective-permute-start | bytes 1769480 | tf_op jit(solution)/shard_map/ppermute | solution.py:30
  129.6 17.2 %collective-permute-start.22 = (bf16[2,64,96]{2,1,0:T(8,128)(2,1)S(1)}, bf16[2,64,96]{2,1,0:T(8,128)(2,1)S(1)}, u32[]{:S(2)}, u32[]{:S(2)}) collective-permute-start(bf16[2,64,96]{2,1,0:T(8,128)(2,1)S(1)} %get-tuple-element.24), channel_id=1, source_target_pairs={{0,16},{1,17},{2,50},{3,51},{4,20},{5,21},{6,54},{7,55},{8,24},{9,... | collective-permute-start | bytes 73736 | tf_op jit(solution)/shard_map/ppermute | solution.py:30
  133.2 13.6 %collective-permute-start.20 = (bf16[2,64,96]{2,1,0:T(8,128)(2,1)S(1)}, bf16[2,64,96]{2,1,0:T(8,128)(2,1)S(1)}, u32[]{:S(2)}, u32[]{:S(2)}) collective-permute-start(bf16[2,64,96]{2,1,0:T(8,128)(2,1)S(1)} %get-tuple-element.22), channel_id=1, source_target_pairs={{0,48},{1,49},{2,18},{3,19},{4,52},{5,53},{6,22},{7,23},{8,56},{9,... | collective-permute-start | bytes 73736 | tf_op jit(solution)/shard_map/ppermute | solution.py:30
  136.7 28.4 %all-to-all-start = ((bf16[64,2,832]{2,1,0:T(2,128)(2,1)}), bf16[64,2,832]{2,1,0:T(2,128)(2,1)S(1)}, u32[]{:S(2)}, u32[]{:S(2)}) async-start(bf16[64,2,832]{2,1,0:T(2,128)(2,1)} %reshape.151), calls=%async_computation | async-start | bytes 458752 | tf_op jit(solution)/shard_map/all_to_all | solution.py:289
  147.7 9.8 %collective-permute-start.23 = (bf16[2,64,384]{2,1,0:T(8,128)(2,1)S(1)}, bf16[2,64,384]{2,1,0:T(8,128)(2,1)S(1)}, u32[]{:S(2)}, u32[]{:S(2)}) collective-permute-start(bf16[2,64,384]{2,1,0:T(8,128)(2,1)S(1)} %pad_maximum_fusion.14.a0), channel_id=1, source_target_pairs={{0,1},{1,0},{2,3},{3,2},{4,5},{5,4},{6,7},{7,6},{8,9},{9,8},{10,11... | collective-permute-start | bytes 294920 | tf_op jit(solution)/shard_map/ppermute | solution.py:30
  (30 other events, 299.9 us)

commit v2 on v1

--- a/solution.py
+++ b/solution.py
@@ -273,10 +273,8 @@
     other_rows = mp_xor(own_rows, 1)
 
     weight_pieces = spread(jnp.stack(spread(weight_rows, "y")), "x")
-    both = jnp.concatenate([prefix_rows, swap_y_mp(out_rows)], axis=0)
-    both_x = spread(both, "x")
-    prefix_pieces = spread(jnp.stack([b[0:32] for b in both_x]), "y")
-    out_pieces = spread(jnp.stack([b[32:80] for b in both_x]), "y")
+    prefix_pieces = spread(jnp.stack(spread(prefix_rows, "x")), "y")
+    out_pieces = spread(jnp.stack(spread(swap_y_mp(out_rows), "x")), "y")
 
     cosine, sine = rope_tables()
     queries, keyed, valued, info, send = call(

time: 171 us -> 170 us (level)
  waiting for transfers between devices: 65.3 us -> 54.1 us
  starting transfers between devices: 61.6 us -> 66.8 us
  other arithmetic: 6.41 us -> 9.47 us
  local copies, waits for them, and re-layouts: 13.5 us -> 15.7 us
    ppermute x29 -> x32, waiting for transfers between devices: 65.3 us -> 54.1 us  [move(): return lax.ppermute(value, ('dp', 'mp'), perm)]
    ppermute x29 -> x32, starting transfers between devices: 51.5 us -> 58.9 us  [move(): return lax.ppermute(value, ('dp', 'mp'), perm)]
    all_to_all x1, starting transfers between devices: 10 us -> 7.97 us  [on_device(): lax.all_to_all(send, 'dp', split_axis=0, concat_axis=0, tiled=True)]
    unnamed x52 -> x62, local copies, waits for them, and re-layouts: 5 us -> 4.99 us
  transfers between devices with their start and end apart: 30 -> 33, of which waited for: 11 -> 11; matrix products, arithmetic and copies ran while one was open for 7% -> 10% of each run, Pallas kernels for 12% -> 12%
where the time goes in v2:
time: 170 us; the launch traced here: 169 us
  starting transfers between devices  66.8 us (39%)
  waiting for transfers between devices  54.1 us (32%)
  Pallas kernels  22 us (13%)
  local copies, waits for them, and re-layouts  15.7 us (9%)
  other arithmetic  9.47 us (6%)
    ppermute x32, starting transfers between devices, move(): return lax.ppermute(value, ('dp', 'mp'), perm)  58.9 us
    ppermute x32, waiting for transfers between devices, move(): return lax.ppermute(value, ('dp', 'mp'), perm)  54.1 us
    pallas_call x5, Pallas kernels, call(): pl.pallas_call(kernel, out_shape=outs, in_specs=[smem] * scalars + [vmem]...  22 us
    all_to_all x1, starting transfers between devices, on_device(): lax.all_to_all(send, 'dp', split_axis=0, concat_axis=0, tiled=True)  7.97 us
    unnamed x62, local copies, waits for them, and re-layouts  4.99 us
  transfers between devices with their start and end apart: 33, of which 11 were waited for; matrix products, arithmetic and copies ran while one was open for 10% of the time, Pallas kernels for 12%

profile of v2, /device:TPU:1, one launch (start us, length us, event | category | flops | bytes accessed | tf_op | source)
XLA Modules:
  0.0 169.4 jit_solution(7645432072187004747)
XLA Ops:
  3.6 6.5 %collective-permute-start = (bf16[64,3200]{1,0:T(8,128)(2,1)S(1)}, bf16[64,3200]{1,0:T(8,128)(2,1)S(1)}, u32[]{:S(2)}, u32[]{:S(2)}) collective-permute-start(bf16[64,3200]{1,0:T(8,128)(2,1)S(1)} %get-tuple-element.13), channel_id=1, source_target_pairs={{0,50},{1,51},{2,16},{3,17},{4,54},{5,55},{6,20},{7,21},{8,58},{9,... | collective-permute-start | bytes 1228808 | tf_op jit(solution)/shard_map/ppermute | solution.py:30
  10.5 8.7 %collective-permute-done = bf16[64,3200]{1,0:T(8,128)(2,1)S(1)} collective-permute-done((bf16[64,3200]{1,0:T(8,128)(2,1)S(1)}, bf16[64,3200]{1,0:T(8,128)(2,1)S(1)}, u32[]{:S(2)}, u32[]{:S(2)}) %collective-permute-start) | collective-permute-done | bytes 409632 | tf_op jit(solution)/shard_map/ppermute | solution.py:30
  22.1 3.9 %collective-permute-start.5 = (bf16[128,384]{1,0:T(8,128)(2,1)}, bf16[128,384]{1,0:T(8,128)(2,1)S(1)}, u32[]{:S(2)}, u32[]{:S(2)}) collective-permute-start(bf16[128,384]{1,0:T(8,128)(2,1)} %get-tuple-element.44), channel_id=1, source_target_pairs={{0,32},{1,33},{2,34},{3,35},{4,36},{5,37},{6,38},{7,39},{8,40},{9,... | collective-permute-start | bytes 294920 | tf_op jit(solution)/shard_map/ppermute | solution.py:30
  29.2 4.0 %collective-permute-start.2 = (bf16[64,3200]{1,0:T(8,128)(2,1)S(1)}, bf16[64,3200]{1,0:T(8,128)(2,1)S(1)}, u32[]{:S(2)}, u32[]{:S(2)}) collective-permute-start(bf16[64,3200]{1,0:T(8,128)(2,1)S(1)} %collective-permute-done.1), channel_id=1, source_target_pairs={{0,50},{1,51},{2,16},{3,17},{4,54},{5,55},{6,20},{7,21},{8,58},{9,... | collective-permute-start | bytes 1228808 | tf_op jit(solution)/shard_map/ppermute | solution.py:30
  34.4 13.1 %collective-permute-done.2 = bf16[64,3200]{1,0:T(8,128)(2,1)S(1)} collective-permute-done((bf16[64,3200]{1,0:T(8,128)(2,1)S(1)}, bf16[64,3200]{1,0:T(8,128)(2,1)S(1)}, u32[]{:S(2)}, u32[]{:S(2)}) %collective-permute-start.2) | collective-permute-done | bytes 409632 | tf_op jit(solution)/shard_map/ppermute | solution.py:30
  51.7 2.8 %collective-permute-start.9 = (bf16[48,1152]{1,0:T(8,128)(2,1)S(1)}, bf16[48,1152]{1,0:T(8,128)(2,1)S(1)}, u32[]{:S(2)}, u32[]{:S(2)}) collective-permute-start(bf16[48,1152]{1,0:T(8,128)(2,1)S(1)} %concatenate.76), channel_id=1, source_target_pairs={{0,192},{1,193},{2,194},{3,195},{4,196},{5,197},{6,198},{7,199},{8... | collective-permute-start | bytes 331784 | tf_op jit(solution)/shard_map/ppermute | solution.py:30
  56.3 2.6 %collective-permute-start.15 = (bf16[32,1536]{1,0:T(8,128)(2,1)S(1)}, bf16[32,1536]{1,0:T(8,128)(2,1)S(1)}, u32[]{:S(2)}, u32[]{:S(2)}) collective-permute-start(bf16[32,1536]{1,0:T(8,128)(2,1)S(1)} %get-tuple-element.26), channel_id=1, source_target_pairs={{0,12},{1,13},{2,14},{3,15},{4,0},{5,1},{6,2},{7,3},{8,4},{9,5},{1... | collective-permute-start | bytes 294920 | tf_op jit(solution)/shard_map/ppermute | solution.py:30
  63.4 2.7 %collective-permute-start.25 = (bf16[48,1536]{1,0:T(8,128)(2,1)S(1)}, bf16[48,1536]{1,0:T(8,128)(2,1)S(1)}, u32[]{:S(2)}, u32[]{:S(2)}) collective-permute-start(bf16[48,1536]{1,0:T(8,128)(2,1)S(1)} %pad_maximum_fusion.5), channel_id=1, source_target_pairs={{0,0},{1,64},{2,128},{3,192},{4,4},{5,68},{6,132},{7,196},{8,8},{9... | collective-permute-start | bytes 442376 | tf_op jit(solution)/shard_map/ppermute | solution.py:30
  70.1 2.5 %collective-permute-start.28 = (bf16[48,1536]{1,0:T(8,128)(2,1)S(1)}, bf16[48,1536]{1,0:T(8,128)(2,1)S(1)}, u32[]{:S(2)}, u32[]{:S(2)}) collective-permute-start(bf16[48,1536]{1,0:T(8,128)(2,1)S(1)} %collective-permute-done.25), channel_id=1, source_target_pairs={{0,12},{1,13},{2,14},{3,15},{4,0},{5,1},{6,2},{7,3},{8,4},{9,5},{1... | collective-permute-start | bytes 442376 | tf_op jit(solution)/shard_map/ppermute | solution.py:30
  72.7 2.1 %collective-permute-start.27 = (bf16[48,1536]{1,0:T(8,128)(2,1)S(1)}, bf16[48,1536]{1,0:T(8,128)(2,1)S(1)}, u32[]{:S(2)}, u32[]{:S(2)}) collective-permute-start(bf16[48,1536]{1,0:T(8,128)(2,1)S(1)} %collective-permute-done.25), channel_id=1, source_target_pairs={{0,8},{1,9},{2,10},{3,11},{4,12},{5,13},{6,14},{7,15},{8,0},{9,1},... | collective-permute-start | bytes 442376 | tf_op jit(solution)/shard_map/ppermute | solution.py:30
  74.8 8.3 %collective-permute-done.28 = bf16[48,1536]{1,0:T(8,128)(2,1)S(1)} collective-permute-done((bf16[48,1536]{1,0:T(8,128)(2,1)S(1)}, bf16[48,1536]{1,0:T(8,128)(2,1)S(1)}, u32[]{:S(2)}, u32[]{:S(2)}) %collective-permute-start.28) | collective-permute-done | bytes 147488 | tf_op jit(solution)/shard_map/ppermute | solution.py:30
  85.7 7.0 %collective-permute-done.27 = bf16[48,1536]{1,0:T(8,128)(2,1)S(1)} collective-permute-done((bf16[48,1536]{1,0:T(8,128)(2,1)S(1)}, bf16[48,1536]{1,0:T(8,128)(2,1)S(1)}, u32[]{:S(2)}, u32[]{:S(2)}) %collective-permute-start.27) | collective-permute-done | bytes 147488 | tf_op jit(solution)/shard_map/ppermute | solution.py:30
  92.6 2.6 %collective-permute-done.26 = bf16[48,1536]{1,0:T(8,128)(2,1)S(1)} collective-permute-done((bf16[48,1536]{1,0:T(8,128)(2,1)S(1)}, bf16[48,1536]{1,0:T(8,128)(2,1)S(1)}, u32[]{:S(2)}, u32[]{:S(2)}) %collective-permute-start.26) | collective-permute-done | bytes 147488 | tf_op jit(solution)/shard_map/ppermute | solution.py:30
  101.7 6.7 %collective-permute-done.12.w3 = bf16[4,48,1152]{2,1,0:T(8,128)(2,1)} collective-permute-done((bf16[4,48,1152]{2,1,0:T(8,128)(2,1)S(1)}, bf16[4,48,1152]{2,1,0:T(8,128)(2,1)}, u32[]{:S(2)}, u32[]{:S(2)}) %collective-permute-start.12) | collective-permute-done | bytes 442400 | tf_op jit(solution)/shard_map/ppermute | solution.py:30
  111.0 6.4 %shard_map.140 = (bf16[512,96]{1,0:T(8,128)(2,1)}, bf16[512,96]{1,0:T(8,128)(2,1)}, bf16[512,96]{1,0:T(8,128)(2,1)}, f32[256,128]{1,0:T(8,128)}, bf16[64,1664]{1,0:T(8,128)(2,1)}) custom-call(s32[5]{0:T(128)} %stack.117.pos_ref, bf16[4,64,3200]{2,1,0:T(8,128)(2,1)} %copy-done.1, bf16[4,64,3200]{2,1,0:T(8,128)(2,1)} %collective-permute-done.3.oth_ref, ...), custom_call_target="tpu_custom_call" | custom-call | tf_op jit(solution)/shard_map/pallas_call | solution.py:214
  117.5 2.4 %collective-permute-start.31 = (bf16[4,48,1536]{2,1,0:T(8,128)(2,1)S(1)}, bf16[4,48,1536]{2,1,0:T(8,128)(2,1)S(1)}, u32[]{:S(2)}, u32[]{:S(2)}) collective-permute-start(bf16[4,48,1536]{2,1,0:T(8,128)(2,1)S(1)} %pad_maximum_fusion.1.w0), channel_id=1, source_target_pairs={{0,192},{1,193},{2,194},{3,195},{4,196},{5,197},{6,198},{7,199},{8... | collective-permute-start | bytes 1769480 | tf_op jit(solution)/shard_map/ppermute | solution.py:30
  119.8 6.8 %shard_map.141 = bf16[512,96]{1,0:T(8,128)(2,1)} custom-call(bf16[512,96]{1,0:T(8,128)(2,1)} %get-tuple-element.7.q_ref, bf16[512,96]{1,0:T(8,128)(2,1)} %get-tuple-element.8.k_ref, bf16[512,96]{1,0:T(8,128)(2,1)} %get-tuple-element.9.v_ref, f32[256,128]{1,0:T(8,128)} %get-tuple-element.10.info_ref, f32[4,1024]{1,0:T(4,128)} %reshape.146.kg_ref, ...), custom_call_target="tpu_custom_call" | custom-call | tf_op jit(solution)/shard_map/pallas_call | solution.py:214
  127.4 2.5 %collective-permute-start.20 = (bf16[2,64,96]{2,1,0:T(8,128)(2,1)S(1)}, bf16[2,64,96]{2,1,0:T(8,128)(2,1)S(1)}, u32[]{:S(2)}, u32[]{:S(2)}) collective-permute-start(bf16[2,64,96]{2,1,0:T(8,128)(2,1)S(1)} %get-tuple-element.23), channel_id=1, source_target_pairs={{0,32},{1,33},{2,34},{3,35},{4,36},{5,37},{6,38},{7,39},{8,40},{9,... | collective-permute-start | bytes 73736 | tf_op jit(solution)/shard_map/ppermute | solution.py:30
  130.8 3.4 %collective-permute-done.20 = bf16[2,64,96]{2,1,0:T(8,128)(2,1)S(1)} collective-permute-done((bf16[2,64,96]{2,1,0:T(8,128)(2,1)S(1)}, bf16[2,64,96]{2,1,0:T(8,128)(2,1)S(1)}, u32[]{:S(2)}, u32[]{:S(2)}) %collective-permute-start.20) | collective-permute-done | bytes 24608 | tf_op jit(solution)/shard_map/ppermute | solution.py:30
  137.6 8.0 %all-to-all-start = ((bf16[64,2,832]{2,1,0:T(2,128)(2,1)}), bf16[64,2,832]{2,1,0:T(2,128)(2,1)S(1)}, u32[]{:S(2)}, u32[]{:S(2)}) async-start(bf16[64,2,832]{2,1,0:T(2,128)(2,1)} %reshape.151), calls=%async_computation | async-start | bytes 458752 | tf_op jit(solution)/shard_map/all_to_all | solution.py:287
  146.5 4.2 %collective-permute-start.22 = (bf16[2,64,384]{2,1,0:T(8,128)(2,1)S(1)}, bf16[2,64,384]{2,1,0:T(8,128)(2,1)S(1)}, u32[]{:S(2)}, u32[]{:S(2)}) collective-permute-start(bf16[2,64,384]{2,1,0:T(8,128)(2,1)S(1)} %pad_maximum_fusion.14.a0), channel_id=1, source_target_pairs={{0,1},{1,0},{2,3},{3,2},{4,5},{5,4},{6,7},{7,6},{8,9},{9,8},{10,11... | collective-permute-start | bytes 294920 | tf_op jit(solution)/shard_map/ppermute | solution.py:30
  154.8 3.3 %shard_map.142.w_ref = bf16[4,4,4,48,384]{4,3,2,1,0:T(8,128)(2,1)} custom-call(s32[5]{0:T(128)} %stack.117.pos_ref, bf16[4,48,1536]{2,1,0:T(8,128)(2,1)} %copy-done.2, bf16[4,48,1536]{2,1,0:T(8,128)(2,1)} %collective-permute-done.29.w1, bf16[4,48,1536]{2,1,0:T(8,128)(2,1)} %copy-done.4, bf16[4,48,1536]{2,1,0:T(8,128)(2,1)} %copy-done.5), custom_call_target="tpu_custom_call" | custom-call | tf_op jit(solution)/shard_map/pallas_call | solution.py:214
  159.5 3.4 %shard_map.143 = bf16[64,1536]{1,0:T(8,128)(2,1)} custom-call(s32[5]{0:T(128)} %stack.117.pos_ref, bf16[2,64,384]{2,1,0:T(8,128)(2,1)} %copy-done.10, bf16[2,64,384]{2,1,0:T(8,128)(2,1)} %copy-done.17, bf16[2,64,384]{2,1,0:T(8,128)(2,1)} %copy-done.18, bf16[2,64,384]{2,1,0:T(8,128)(2,1)} %copy-done.19, bf16[4,4,4,48,384]{4,3,2,1,0:T(8,128)(2,1)} %shard_map.142.w_ref, ...), custom_call_target="tpu_custom_call" | custom-call | tf_op jit(solution)/shard_map/pallas_call | solution.py:214
  165.6 2.1 %shard_map.144 = bf16[64,1536]{1,0:T(8,128)(2,1)} custom-call(bf16[64,1664]{1,0:T(8,128)(2,1)} %bitcast.120), custom_call_target="tpu_custom_call" | custom-call | tf_op jit(solution)/shard_map/pallas_call | solution.py:214
  (165 shorter events, 52.2 us)
Async XLA Ops:
  3.6 15.7 %collective-permute-start = (bf16[64,3200]{1,0:T(8,128)(2,1)S(1)}, bf16[64,3200]{1,0:T(8,128)(2,1)S(1)}, u32[]{:S(2)}, u32[]{:S(2)}) collective-permute-start(bf16[64,3200]{1,0:T(8,128)(2,1)S(1)} %get-tuple-element.13), channel_id=1, source_target_pairs={{0,50},{1,51},{2,16},{3,17},{4,54},{5,55},{6,20},{7,21},{8,58},{9,... | collective-permute-start | bytes 1228808 | tf_op jit(solution)/shard_map/ppermute | solution.py:30
  19.2 10.0 %collective-permute-start.1 = (bf16[64,3200]{1,0:T(8,128)(2,1)S(1)}, bf16[64,3200]{1,0:T(8,128)(2,1)S(1)}, u32[]{:S(2)}, u32[]{:S(2)}) collective-permute-start(bf16[64,3200]{1,0:T(8,128)(2,1)S(1)} %collective-permute-done), channel_id=1, source_target_pairs={{0,2},{1,3},{2,0},{3,1},{4,6},{5,7},{6,4},{7,5},{8,10},{9,11},{10,... | collective-permute-start | bytes 1228808 | tf_op jit(solution)/shard_map/ppermute | solution.py:30
  20.3 30.4 %collective-permute-start.4 = (bf16[128,384]{1,0:T(8,128)(2,1)}, bf16[128,384]{1,0:T(8,128)(2,1)S(1)}, u32[]{:S(2)}, u32[]{:S(2)}) collective-permute-start(bf16[128,384]{1,0:T(8,128)(2,1)} %get-tuple-element.45), channel_id=1, source_target_pairs={{0,16},{1,17},{2,18},{3,19},{4,20},{5,21},{6,22},{7,23},{8,24},{9,... | collective-permute-start | bytes 294920 | tf_op jit(solution)/shard_map/ppermute | solution.py:30
  22.1 28.7 %collective-permute-start.5 = (bf16[128,384]{1,0:T(8,128)(2,1)}, bf16[128,384]{1,0:T(8,128)(2,1)S(1)}, u32[]{:S(2)}, u32[]{:S(2)}) collective-permute-start(bf16[128,384]{1,0:T(8,128)(2,1)} %get-tuple-element.44), channel_id=1, source_target_pairs={{0,32},{1,33},{2,34},{3,35},{4,36},{5,37},{6,38},{7,39},{8,40},{9,... | collective-permute-start | bytes 294920 | tf_op jit(solution)/shard_map/ppermute | solution.py:30
  25.9 24.8 %collective-permute-start.6 = (bf16[128,384]{1,0:T(8,128)(2,1)}, bf16[128,384]{1,0:T(8,128)(2,1)}, u32[]{:S(2)}, u32[]{:S(2)}) collective-permute-start(bf16[128,384]{1,0:T(8,128)(2,1)} %get-tuple-element.43), channel_id=1, source_target_pairs={{0,48},{1,49},{2,50},{3,51},{4,52},{5,53},{6,54},{7,55},{8,56},{9,... | collective-permute-start | bytes 294920 | tf_op jit(solution)/shard_map/ppermute | solution.py:30
  29.2 18.3 %collective-permute-start.2 = (bf16[64,3200]{1,0:T(8,128)(2,1)S(1)}, bf16[64,3200]{1,0:T(8,128)(2,1)S(1)}, u32[]{:S(2)}, u32[]{:S(2)}) collective-permute-start(bf16[64,3200]{1,0:T(8,128)(2,1)S(1)} %collective-permute-done.1), channel_id=1, source_target_pairs={{0,50},{1,51},{2,16},{3,17},{4,54},{5,55},{6,20},{7,21},{8,58},{9,... | collective-permute-start | bytes 1228808 | tf_op jit(solution)/shard_map/ppermute | solution.py:30
  48.9 60.8 %collective-permute-start.3 = (bf16[4,64,3200]{2,1,0:T(8,128)(2,1)S(1)}, bf16[4,64,3200]{2,1,0:T(8,128)(2,1)}, u32[]{:S(2)}, u32[]{:S(2)}) collective-permute-start(bf16[4,64,3200]{2,1,0:T(8,128)(2,1)S(1)} %pad_maximum_fusion.own_ref), channel_id=1, source_target_pairs={{0,1},{1,0},{2,3},{3,2},{4,5},{5,4},{6,7},{7,6},{8,9},{9,8},{10,11... | collective-permute-start | bytes 4915208 | tf_op jit(solution)/shard_map/ppermute | solution.py:30
  61.8 10.8 %collective-permute-start.13 = (bf16[32,1536]{1,0:T(8,128)(2,1)S(1)}, bf16[32,1536]{1,0:T(8,128)(2,1)S(1)}, u32[]{:S(2)}, u32[]{:S(2)}) collective-permute-start(bf16[32,1536]{1,0:T(8,128)(2,1)S(1)} %get-tuple-element.26), channel_id=1, source_target_pairs={{0,4},{1,5},{2,6},{3,7},{4,8},{5,9},{6,10},{7,11},{8,12},{9,13},{1... | collective-permute-start | bytes 294920 | tf_op jit(solution)/shard_map/ppermute | solution.py:30
  66.2 30.3 %collective-permute-start.10 = (bf16[4,48,1152]{2,1,0:T(8,128)(2,1)S(1)}, bf16[4,48,1152]{2,1,0:T(8,128)(2,1)S(1)}, u32[]{:S(2)}, u32[]{:S(2)}) collective-permute-start(bf16[4,48,1152]{2,1,0:T(8,128)(2,1)S(1)} %pad_maximum_fusion.2.w0), channel_id=1, source_target_pairs={{0,4},{1,5},{2,6},{3,7},{4,8},{5,9},{6,10},{7,11},{8,12},{9,13},{1... | collective-permute-start | bytes 1327112 | tf_op jit(solution)/shard_map/ppermute | solution.py:30
  67.8 30.1 %collective-permute-start.11 = (bf16[4,48,1152]{2,1,0:T(8,128)(2,1)S(1)}, bf16[4,48,1152]{2,1,0:T(8,128)(2,1)S(1)}, u32[]{:S(2)}, u32[]{:S(2)}) collective-permute-start(bf16[4,48,1152]{2,1,0:T(8,128)(2,1)S(1)} %pad_maximum_fusion.2.w0), channel_id=1, source_target_pairs={{0,8},{1,9},{2,10},{3,11},{4,12},{5,13},{6,14},{7,15},{8,0},{9,1},... | collective-permute-start | bytes 1327112 | tf_op jit(solution)/shard_map/ppermute | solution.py:30
  70.1 13.0 %collective-permute-start.28 = (bf16[48,1536]{1,0:T(8,128)(2,1)S(1)}, bf16[48,1536]{1,0:T(8,128)(2,1)S(1)}, u32[]{:S(2)}, u32[]{:S(2)}) collective-permute-start(bf16[48,1536]{1,0:T(8,128)(2,1)S(1)} %collective-permute-done.25), channel_id=1, source_target_pairs={{0,12},{1,13},{2,14},{3,15},{4,0},{5,1},{6,2},{7,3},{8,4},{9,5},{1... | collective-permute-start | bytes 442376 | tf_op jit(solution)/shard_map/ppermute | solution.py:30
  72.7 19.9 %collective-permute-start.27 = (bf16[48,1536]{1,0:T(8,128)(2,1)S(1)}, bf16[48,1536]{1,0:T(8,128)(2,1)S(1)}, u32[]{:S(2)}, u32[]{:S(2)}) collective-permute-start(bf16[48,1536]{1,0:T(8,128)(2,1)S(1)} %collective-permute-done.25), channel_id=1, source_target_pairs={{0,8},{1,9},{2,10},{3,11},{4,12},{5,13},{6,14},{7,15},{8,0},{9,1},... | collective-permute-start | bytes 442376 | tf_op jit(solution)/shard_map/ppermute | solution.py:30
  83.1 12.1 %collective-permute-start.26 = (bf16[48,1536]{1,0:T(8,128)(2,1)S(1)}, bf16[48,1536]{1,0:T(8,128)(2,1)S(1)}, u32[]{:S(2)}, u32[]{:S(2)}) collective-permute-start(bf16[48,1536]{1,0:T(8,128)(2,1)S(1)} %collective-permute-done.25), channel_id=1, source_target_pairs={{0,4},{1,5},{2,6},{3,7},{4,8},{5,9},{6,10},{7,11},{8,12},{9,13},{1... | collective-permute-start | bytes 442376 | tf_op jit(solution)/shard_map/ppermute | solution.py:30
  92.6 24.8 %collective-permute-start.16 = (bf16[4,32,1536]{2,1,0:T(8,128)(2,1)}, bf16[4,32,1536]{2,1,0:T(8,128)(2,1)}, u32[]{:S(2)}, u32[]{:S(2)}) collective-permute-start(bf16[4,32,1536]{2,1,0:T(8,128)(2,1)} %pad_maximum_fusion.3.p0), channel_id=1, source_target_pairs={{0,64},{1,65},{2,66},{3,67},{4,68},{5,69},{6,70},{7,71},{8,72},{9,... | collective-permute-start | bytes 1179656 | tf_op jit(solution)/shard_map/ppermute | solution.py:30
  95.2 24.6 %collective-permute-start.17 = (bf16[4,32,1536]{2,1,0:T(8,128)(2,1)}, bf16[4,32,1536]{2,1,0:T(8,128)(2,1)}, u32[]{:S(2)}, u32[]{:S(2)}) collective-permute-start(bf16[4,32,1536]{2,1,0:T(8,128)(2,1)} %pad_maximum_fusion.3.p0), channel_id=1, source_target_pairs={{0,128},{1,129},{2,130},{3,131},{4,132},{5,133},{6,134},{7,135},{8... | collective-permute-start | bytes 1179656 | tf_op jit(solution)/shard_map/ppermute | solution.py:30
  96.5 23.3 %collective-permute-start.18 = (bf16[4,32,1536]{2,1,0:T(8,128)(2,1)}, bf16[4,32,1536]{2,1,0:T(8,128)(2,1)}, u32[]{:S(2)}, u32[]{:S(2)}) collective-permute-start(bf16[4,32,1536]{2,1,0:T(8,128)(2,1)} %pad_maximum_fusion.3.p0), channel_id=1, source_target_pairs={{0,192},{1,193},{2,194},{3,195},{4,196},{5,197},{6,198},{7,199},{8... | collective-permute-start | bytes 1179656 | tf_op jit(solution)/shard_map/ppermute | solution.py:30
  97.9 10.6 %collective-permute-start.12 = (bf16[4,48,1152]{2,1,0:T(8,128)(2,1)S(1)}, bf16[4,48,1152]{2,1,0:T(8,128)(2,1)}, u32[]{:S(2)}, u32[]{:S(2)}) collective-permute-start(bf16[4,48,1152]{2,1,0:T(8,128)(2,1)S(1)} %pad_maximum_fusion.2.w0), channel_id=1, source_target_pairs={{0,12},{1,13},{2,14},{3,15},{4,0},{5,1},{6,2},{7,3},{8,4},{9,5},{1... | collective-permute-start | bytes 1327112 | tf_op jit(solution)/shard_map/ppermute | solution.py:30
  108.5 43.6 %collective-permute-start.29 = (bf16[4,48,1536]{2,1,0:T(8,128)(2,1)S(1)}, bf16[4,48,1536]{2,1,0:T(8,128)(2,1)}, u32[]{:S(2)}, u32[]{:S(2)}) collective-permute-start(bf16[4,48,1536]{2,1,0:T(8,128)(2,1)S(1)} %pad_maximum_fusion.1.w0), channel_id=1, source_target_pairs={{0,64},{1,65},{2,66},{3,67},{4,68},{5,69},{6,70},{7,71},{8,72},{9,... | collective-permute-start | bytes 1769480 | tf_op jit(solution)/shard_map/ppermute | solution.py:30
  109.8 43.4 %collective-permute-start.30 = (bf16[4,48,1536]{2,1,0:T(8,128)(2,1)S(1)}, bf16[4,48,1536]{2,1,0:T(8,128)(2,1)S(1)}, u32[]{:S(2)}, u32[]{:S(2)}) collective-permute-start(bf16[4,48,1536]{2,1,0:T(8,128)(2,1)S(1)} %pad_maximum_fusion.1.w0), channel_id=1, source_target_pairs={{0,128},{1,129},{2,130},{3,131},{4,132},{5,133},{6,134},{7,135},{8... | collective-permute-start | bytes 1769480 | tf_op jit(solution)/shard_map/ppermute | solution.py:30
  117.5 35.7 %collective-permute-start.31 = (bf16[4,48,1536]{2,1,0:T(8,128)(2,1)S(1)}, bf16[4,48,1536]{2,1,0:T(8,128)(2,1)S(1)}, u32[]{:S(2)}, u32[]{:S(2)}) collective-permute-start(bf16[4,48,1536]{2,1,0:T(8,128)(2,1)S(1)} %pad_maximum_fusion.1.w0), channel_id=1, source_target_pairs={{0,192},{1,193},{2,194},{3,195},{4,196},{5,197},{6,198},{7,199},{8... | collective-permute-start | bytes 1769480 | tf_op jit(solution)/shard_map/ppermute | solution.py:30
  130.0 15.6 %collective-permute-start.21 = (bf16[2,64,96]{2,1,0:T(8,128)(2,1)S(1)}, bf16[2,64,96]{2,1,0:T(8,128)(2,1)S(1)}, u32[]{:S(2)}, u32[]{:S(2)}) collective-permute-start(bf16[2,64,96]{2,1,0:T(8,128)(2,1)S(1)} %get-tuple-element.24), channel_id=1, source_target_pairs={{0,16},{1,17},{2,50},{3,51},{4,20},{5,21},{6,54},{7,55},{8,24},{9,... | collective-permute-start | bytes 73736 | tf_op jit(solution)/shard_map/ppermute | solution.py:30
  134.2 11.4 %collective-permute-start.19 = (bf16[2,64,96]{2,1,0:T(8,128)(2,1)S(1)}, bf16[2,64,96]{2,1,0:T(8,128)(2,1)S(1)}, u32[]{:S(2)}, u32[]{:S(2)}) collective-permute-start(bf16[2,64,96]{2,1,0:T(8,128)(2,1)S(1)} %get-tuple-element.22), channel_id=1, source_target_pairs={{0,48},{1,49},{2,18},{3,19},{4,52},{5,53},{6,22},{7,23},{8,56},{9,... | collective-permute-start | bytes 73736 | tf_op jit(solution)/shard_map/ppermute | solution.py:30
  137.6 27.0 %all-to-all-start = ((bf16[64,2,832]{2,1,0:T(2,128)(2,1)}), bf16[64,2,832]{2,1,0:T(2,128)(2,1)S(1)}, u32[]{:S(2)}, u32[]{:S(2)}) async-start(bf16[64,2,832]{2,1,0:T(2,128)(2,1)} %reshape.151), calls=%async_computation | async-start | bytes 458752 | tf_op jit(solution)/shard_map/all_to_all | solution.py:287
  146.5 11.6 %collective-permute-start.22 = (bf16[2,64,384]{2,1,0:T(8,128)(2,1)S(1)}, bf16[2,64,384]{2,1,0:T(8,128)(2,1)S(1)}, u32[]{:S(2)}, u32[]{:S(2)}) collective-permute-start(bf16[2,64,384]{2,1,0:T(8,128)(2,1)S(1)} %pad_maximum_fusion.14.a0), channel_id=1, source_target_pairs={{0,1},{1,0},{2,3},{3,2},{4,5},{5,4},{6,7},{7,6},{8,9},{9,8},{10,11... | collective-permute-start | bytes 294920 | tf_op jit(solution)/shard_map/ppermute | solution.py:30
  (38 other events, 491.1 us)

commit v3 on v2

--- a/solution.py
+++ b/solution.py
@@ -112,10 +112,11 @@
         block = info[64 * ky : 64 * ky + 64]
         pick = jnp.where(block[:, 0:1] == dest_iota, 1.0, 0.0).astype(jnp.bfloat16)
         moved = dot_tn(pick, packed[64 * ky : 64 * ky + 64])
-        send_out[:, 384 * ky : 384 * ky + 384] = moved.astype(jnp.bfloat16)
+        send_out[:, ky // 2, 384 * (ky % 2) : 384 * (ky % 2) + 384] = moved.astype(jnp.bfloat16)
         slot = jnp.where(lane_iota == ky, block[:, 1:2], 0.0).astype(jnp.bfloat16)
         extras = extras + dot_tn(pick, slot)
-    send_out[:, 1536:1664] = extras.astype(jnp.bfloat16)
+    for half in range(2):
+        send_out[:, half, 768:896] = extras.astype(jnp.bfloat16)
 
 
 def attend_kernel(q_ref, k_ref, v_ref, info_ref, kg_ref, p0, p1, p2, p3, out_ref, s_ref, keys_ref, values_ref):
@@ -187,24 +188,26 @@
         weight = w_ref[m ^ k].reshape(768, 384)
         part = dot_nt(block[...].reshape(128, 384), weight)
         acc = part if acc is None else acc + part
-    out_ref[:, 0:768] = acc[0:64].astype(jnp.bfloat16)
-    out_ref[:, 768:1536] = jnp.where(len_ref[...] > 1, acc[64:128], 0.0).astype(jnp.bfloat16)
+    out_ref[:, 0, :] = acc[0:64].astype(jnp.bfloat16)
+    out_ref[:, 1, :] = jnp.where(len_ref[...] > 1, acc[64:128], 0.0).astype(jnp.bfloat16)
 
 
 def unpack_kernel(recv_ref, out_ref):
     slot_iota = lax.broadcasted_iota(jnp.int32, (256, 64), 1).astype(jnp.float32)
     source_head = (lax.broadcasted_iota(jnp.int32, (256, 1), 0) // 4) % 4
-    data = jnp.concatenate([recv_ref[:, 384 * k : 384 * k + 384] for k in range(4)], axis=0)
-    tail = recv_ref[:, 1536:1664].astype(jnp.float32)
+    data = jnp.concatenate(
+        [recv_ref[:, k // 2, 384 * (k % 2) : 384 * (k % 2) + 384] for k in range(4)], axis=0
+    )
+    tail = recv_ref[:, 0, 768:896].astype(jnp.float32)
     slots = jnp.concatenate([tail[:, k : k + 1] for k in range(4)], axis=0)
+    moved = []
     for head in range(4):
         own = jnp.where(source_head == head, slots, -1.0)
         pick = jnp.where(own == slot_iota, 1.0, 0.0).astype(jnp.bfloat16)
-        moved = dot_tn(pick, data).astype(jnp.bfloat16)
-        for part in range(4):
-            out_ref[:, 384 * part + 96 * head : 384 * part + 96 * head + 96] = moved[
-                :, 96 * part : 96 * part + 96
-            ]
+        moved.append(dot_tn(pick, data).astype(jnp.bfloat16))
+    for part in range(4):
+        row = jnp.concatenate([one[:, 96 * part : 96 * part + 96] for one in moved], axis=1)
+        out_ref[:, part // 2, part % 2, :] = row
 
 
 def call(kernel, outs, inputs, scratch=(), scalars=0):
@@ -279,7 +282,7 @@
     cosine, sine = rope_tables()
     queries, keyed, valued, info, send = call(
         qkv_kernel,
-        [struct((512, 96)), struct((512, 96)), struct((512, 96)), struct((256, 128), jnp.float32), struct((64, 1664))],
+        [struct((512, 96)), struct((512, 96)), struct((512, 96)), struct((256, 128), jnp.float32), struct((64, 2, 896))],
         [pos, own_rows, other_rows, *weight_pieces, jnp.asarray(cosine), jnp.asarray(sine)],
         scratch=[pltpu.VMEM((4, 4, 4, 48, 288), jnp.bfloat16)],
         scalars=1,
@@ -319,10 +322,8 @@
     home_all = [home] + [mp_xor(home, k) for k in (1, 2, 3)]
 
     out_weight = call(order_kernel, struct((4, 4, 4, 48, 384)), [pos, *out_pieces], scalars=1)
-    hidden = call(
-        out_kernel, struct((64, 1536)), [pos, *home_all, out_weight, lengths[:, None]], scalars=1
-    ).reshape(64, 2, 768)
-    suffix_cache = call(unpack_kernel, struct((64, 1536)), [received]).reshape(64, 2, 2, 384)
+    hidden = call(out_kernel, struct((64, 2, 768)), [pos, *home_all, out_weight, lengths[:, None]], scalars=1)
+    suffix_cache = call(unpack_kernel, struct((64, 2, 2, 384)), [received])
     return hidden, suffix_cache
 
 

time: 170 us -> 171 us (level)
  starting transfers between devices: 66.8 us -> 69.7 us
  waiting for transfers between devices: 54.1 us -> 51.8 us
    ppermute x32, starting transfers between devices: 58.9 us -> 62.6 us  [move(): return lax.ppermute(value, ('dp', 'mp'), perm)]
    reshape x2 -> x0, local copies, waits for them, and re-layouts: 3.31 us -> none  [the longest x1 1.65 us: on_device(): call(unpack_kernel, struct((64, 1536)), [received]).reshape(64, 2, 2, 384)]
    ppermute x32, waiting for transfers between devices: 54.1 us -> 51.8 us  [move(): return lax.ppermute(value, ('dp', 'mp'), perm)]
    unnamed x62 -> x49, local copies, waits for them, and re-layouts: 4.99 us -> 4.03 us
  transfers between devices with their start and end apart: 33 -> 33, of which waited for: 11 -> 10; matrix products, arithmetic and copies ran while one was open for 10% -> 10% of each run, Pallas kernels for 12% -> 12%
where the time goes in v3:
time: 171 us; the launch traced here: 170 us
  starting transfers between devices  69.7 us (41%)
  waiting for transfers between devices  51.8 us (30%)
  Pallas kernels  22.7 us (13%)
  local copies, waits for them, and re-layouts  15.4 us (9%)
  other arithmetic  8.77 us (5%)
    ppermute x32, starting transfers between devices, move(): return lax.ppermute(value, ('dp', 'mp'), perm)  62.6 us
    ppermute x32, waiting for transfers between devices, move(): return lax.ppermute(value, ('dp', 'mp'), perm)  51.8 us
    pallas_call x5, Pallas kernels, call(): pl.pallas_call(kernel, out_shape=outs, in_specs=[smem] * scalars + [vmem]...  22.7 us
    all_to_all x1, starting transfers between devices, on_device(): lax.all_to_all(send, 'dp', split_axis=0, concat_axis=0, tiled=True)  7.09 us
    unnamed x49, local copies, waits for them, and re-layouts  4.03 us
  transfers between devices with their start and end apart: 33, of which 10 were waited for; matrix products, arithmetic and copies ran while one was open for 10% of the time, Pallas kernels for 12%

profile of v3, /device:TPU:1, one launch (start us, length us, event | category | flops | bytes accessed | tf_op | source)
XLA Modules:
  0.0 169.7 jit_solution(4130400347584086939)
XLA Ops:
  3.6 6.5 %collective-permute-start = (bf16[64,3200]{1,0:T(8,128)(2,1)S(1)}, bf16[64,3200]{1,0:T(8,128)(2,1)S(1)}, u32[]{:S(2)}, u32[]{:S(2)}) collective-permute-start(bf16[64,3200]{1,0:T(8,128)(2,1)S(1)} %get-tuple-element.13), channel_id=1, source_target_pairs={{0,50},{1,51},{2,16},{3,17},{4,54},{5,55},{6,20},{7,21},{8,58},{9,... | collective-permute-start | bytes 1228808 | tf_op jit(solution)/shard_map/ppermute | solution.py:30
  10.5 8.7 %collective-permute-done = bf16[64,3200]{1,0:T(8,128)(2,1)S(1)} collective-permute-done((bf16[64,3200]{1,0:T(8,128)(2,1)S(1)}, bf16[64,3200]{1,0:T(8,128)(2,1)S(1)}, u32[]{:S(2)}, u32[]{:S(2)}) %collective-permute-start) | collective-permute-done | bytes 409632 | tf_op jit(solution)/shard_map/ppermute | solution.py:30
  22.1 3.9 %collective-permute-start.5 = (bf16[128,384]{1,0:T(8,128)(2,1)}, bf16[128,384]{1,0:T(8,128)(2,1)}, u32[]{:S(2)}, u32[]{:S(2)}) collective-permute-start(bf16[128,384]{1,0:T(8,128)(2,1)} %get-tuple-element.44), channel_id=1, source_target_pairs={{0,32},{1,33},{2,34},{3,35},{4,36},{5,37},{6,38},{7,39},{8,40},{9,... | collective-permute-start | bytes 294920 | tf_op jit(solution)/shard_map/ppermute | solution.py:30
  29.2 4.1 %collective-permute-start.2 = (bf16[64,3200]{1,0:T(8,128)(2,1)}, bf16[64,3200]{1,0:T(8,128)(2,1)S(1)}, u32[]{:S(2)}, u32[]{:S(2)}) collective-permute-start(bf16[64,3200]{1,0:T(8,128)(2,1)} %collective-permute-done.1), channel_id=1, source_target_pairs={{0,50},{1,51},{2,16},{3,17},{4,54},{5,55},{6,20},{7,21},{8,58},{9,... | collective-permute-start | bytes 1228808 | tf_op jit(solution)/shard_map/ppermute | solution.py:30
  33.9 13.6 %collective-permute-done.2 = bf16[64,3200]{1,0:T(8,128)(2,1)S(1)} collective-permute-done((bf16[64,3200]{1,0:T(8,128)(2,1)}, bf16[64,3200]{1,0:T(8,128)(2,1)S(1)}, u32[]{:S(2)}, u32[]{:S(2)}) %collective-permute-start.2) | collective-permute-done | bytes 409632 | tf_op jit(solution)/shard_map/ppermute | solution.py:30
  48.8 1.9 %collective-permute-start.3 = (bf16[4,64,3200]{2,1,0:T(8,128)(2,1)S(1)}, bf16[4,64,3200]{2,1,0:T(8,128)(2,1)}, u32[]{:S(2)}, u32[]{:S(2)}) collective-permute-start(bf16[4,64,3200]{2,1,0:T(8,128)(2,1)S(1)} %pad_maximum_fusion.own_ref), channel_id=1, source_target_pairs={{0,1},{1,0},{2,3},{3,2},{4,5},{5,4},{6,7},{7,6},{8,9},{9,8},{10,11... | collective-permute-start | bytes 4915208 | tf_op jit(solution)/shard_map/ppermute | solution.py:30
  53.2 2.8 %collective-permute-start.9 = (bf16[48,1152]{1,0:T(8,128)(2,1)S(1)}, bf16[48,1152]{1,0:T(8,128)(2,1)S(1)}, u32[]{:S(2)}, u32[]{:S(2)}) collective-permute-start(bf16[48,1152]{1,0:T(8,128)(2,1)S(1)} %concatenate.76), channel_id=1, source_target_pairs={{0,192},{1,193},{2,194},{3,195},{4,196},{5,197},{6,198},{7,199},{8... | collective-permute-start | bytes 331784 | tf_op jit(solution)/shard_map/ppermute | solution.py:30
  59.3 2.6 %collective-permute-start.15 = (bf16[32,1536]{1,0:T(8,128)(2,1)S(1)}, bf16[32,1536]{1,0:T(8,128)(2,1)S(1)}, u32[]{:S(2)}, u32[]{:S(2)}) collective-permute-start(bf16[32,1536]{1,0:T(8,128)(2,1)S(1)} %get-tuple-element.26), channel_id=1, source_target_pairs={{0,12},{1,13},{2,14},{3,15},{4,0},{5,1},{6,2},{7,3},{8,4},{9,5},{1... | collective-permute-start | bytes 294920 | tf_op jit(solution)/shard_map/ppermute | solution.py:30
  66.2 5.1 %collective-permute-start.25 = (bf16[48,1536]{1,0:T(8,128)(2,1)S(1)}, bf16[48,1536]{1,0:T(8,128)(2,1)S(1)}, u32[]{:S(2)}, u32[]{:S(2)}) collective-permute-start(bf16[48,1536]{1,0:T(8,128)(2,1)S(1)} %pad_maximum_fusion.5), channel_id=1, source_target_pairs={{0,0},{1,64},{2,128},{3,192},{4,4},{5,68},{6,132},{7,196},{8,8},{9... | collective-permute-start | bytes 442376 | tf_op jit(solution)/shard_map/ppermute | solution.py:30
  76.0 2.1 %collective-permute-start.28 = (bf16[48,1536]{1,0:T(8,128)(2,1)S(1)}, bf16[48,1536]{1,0:T(8,128)(2,1)}, u32[]{:S(2)}, u32[]{:S(2)}) collective-permute-start(bf16[48,1536]{1,0:T(8,128)(2,1)S(1)} %collective-permute-done.25), channel_id=1, source_target_pairs={{0,12},{1,13},{2,14},{3,15},{4,0},{5,1},{6,2},{7,3},{8,4},{9,5},{1... | collective-permute-start | bytes 442376 | tf_op jit(solution)/shard_map/ppermute | solution.py:30
  79.5 9.2 %collective-permute-done.28 = bf16[48,1536]{1,0:T(8,128)(2,1)} collective-permute-done((bf16[48,1536]{1,0:T(8,128)(2,1)S(1)}, bf16[48,1536]{1,0:T(8,128)(2,1)}, u32[]{:S(2)}, u32[]{:S(2)}) %collective-permute-start.28) | collective-permute-done | bytes 147488 | tf_op jit(solution)/shard_map/ppermute | solution.py:30
  91.1 6.2 %collective-permute-done.27 = bf16[48,1536]{1,0:T(8,128)(2,1)} collective-permute-done((bf16[48,1536]{1,0:T(8,128)(2,1)S(1)}, bf16[48,1536]{1,0:T(8,128)(2,1)}, u32[]{:S(2)}, u32[]{:S(2)}) %collective-permute-start.27) | collective-permute-done | bytes 147488 | tf_op jit(solution)/shard_map/ppermute | solution.py:30
  99.0 2.6 %collective-permute-start.17 = (bf16[4,32,1536]{2,1,0:T(8,128)(2,1)}, bf16[4,32,1536]{2,1,0:T(8,128)(2,1)}, u32[]{:S(2)}, u32[]{:S(2)}) collective-permute-start(bf16[4,32,1536]{2,1,0:T(8,128)(2,1)} %pad_maximum_fusion.3.p0), channel_id=1, source_target_pairs={{0,128},{1,129},{2,130},{3,131},{4,132},{5,133},{6,134},{7,135},{8... | collective-permute-start | bytes 1179656 | tf_op jit(solution)/shard_map/ppermute | solution.py:30
  106.5 7.7 %collective-permute-done.12.w3 = bf16[4,48,1152]{2,1,0:T(8,128)(2,1)} collective-permute-done((bf16[4,48,1152]{2,1,0:T(8,128)(2,1)S(1)}, bf16[4,48,1152]{2,1,0:T(8,128)(2,1)}, u32[]{:S(2)}, u32[]{:S(2)}) %collective-permute-start.12) | collective-permute-done | bytes 442400 | tf_op jit(solution)/shard_map/ppermute | solution.py:30
  115.7 6.5 %shard_map.140 = (bf16[512,96]{1,0:T(8,128)(2,1)}, bf16[512,96]{1,0:T(8,128)(2,1)}, bf16[512,96]{1,0:T(8,128)(2,1)}, f32[256,128]{1,0:T(8,128)}, bf16[64,2,896]{2,1,0:T(2,128)(2,1)}) custom-call(s32[5]{0:T(128)} %stack.117.pos_ref, bf16[4,64,3200]{2,1,0:T(8,128)(2,1)} %copy-done.1, bf16[4,64,3200]{2,1,0:T(8,128)(2,1)} %collective-permute-done.3.oth_ref, ...), custom_call_target="tpu_custom_call" | custom-call | tf_op jit(solution)/shard_map/pallas_call | solution.py:217
  123.9 6.8 %shard_map.141 = bf16[512,96]{1,0:T(8,128)(2,1)} custom-call(bf16[512,96]{1,0:T(8,128)(2,1)} %get-tuple-element.7.q_ref, bf16[512,96]{1,0:T(8,128)(2,1)} %get-tuple-element.8.k_ref, bf16[512,96]{1,0:T(8,128)(2,1)} %get-tuple-element.9.v_ref, f32[256,128]{1,0:T(8,128)} %get-tuple-element.10.info_ref, f32[4,1024]{1,0:T(4,128)} %reshape.138.kg_ref, ...), custom_call_target="tpu_custom_call" | custom-call | tf_op jit(solution)/shard_map/pallas_call | solution.py:217
  131.5 3.1 %collective-permute-start.20 = (bf16[2,64,96]{2,1,0:T(8,128)(2,1)S(1)}, bf16[2,64,96]{2,1,0:T(8,128)(2,1)S(1)}, u32[]{:S(2)}, u32[]{:S(2)}) collective-permute-start(bf16[2,64,96]{2,1,0:T(8,128)(2,1)S(1)} %get-tuple-element.23), channel_id=1, source_target_pairs={{0,32},{1,33},{2,34},{3,35},{4,36},{5,37},{6,38},{7,39},{8,40},{9,... | collective-permute-start | bytes 73736 | tf_op jit(solution)/shard_map/ppermute | solution.py:30
  134.6 2.3 %collective-permute-start.21 = (bf16[2,64,96]{2,1,0:T(8,128)(2,1)S(1)}, bf16[2,64,96]{2,1,0:T(8,128)(2,1)S(1)}, u32[]{:S(2)}, u32[]{:S(2)}) collective-permute-start(bf16[2,64,96]{2,1,0:T(8,128)(2,1)S(1)} %get-tuple-element.24), channel_id=1, source_target_pairs={{0,16},{1,17},{2,50},{3,51},{4,20},{5,21},{6,54},{7,55},{8,24},{9,... | collective-permute-start | bytes 73736 | tf_op jit(solution)/shard_map/ppermute | solution.py:30
  138.2 3.5 %collective-permute-start.19 = (bf16[2,64,96]{2,1,0:T(8,128)(2,1)S(1)}, bf16[2,64,96]{2,1,0:T(8,128)(2,1)S(1)}, u32[]{:S(2)}, u32[]{:S(2)}) collective-permute-start(bf16[2,64,96]{2,1,0:T(8,128)(2,1)S(1)} %get-tuple-element.22), channel_id=1, source_target_pairs={{0,48},{1,49},{2,18},{3,19},{4,52},{5,53},{6,22},{7,23},{8,56},{9,... | collective-permute-start | bytes 73736 | tf_op jit(solution)/shard_map/ppermute | solution.py:30
  141.7 7.1 %all-to-all-start = ((bf16[64,2,896]{2,1,0:T(2,128)(2,1)}), bf16[64,2,896]{2,1,0:T(2,128)(2,1)S(1)}, u32[]{:S(2)}, u32[]{:S(2)}) async-start(bf16[64,2,896]{2,1,0:T(2,128)(2,1)} %get-tuple-element.11), calls=%async_computation | async-start | bytes 458752 | tf_op jit(solution)/shard_map/all_to_all | solution.py:290
  149.8 4.4 %collective-permute-start.22 = (bf16[2,64,384]{2,1,0:T(8,128)(2,1)S(1)}, bf16[2,64,384]{2,1,0:T(8,128)(2,1)S(1)}, u32[]{:S(2)}, u32[]{:S(2)}) collective-permute-start(bf16[2,64,384]{2,1,0:T(8,128)(2,1)S(1)} %pad_maximum_fusion.14.a0), channel_id=1, source_target_pairs={{0,1},{1,0},{2,3},{3,2},{4,5},{5,4},{6,7},{7,6},{8,9},{9,8},{10,11... | collective-permute-start | bytes 294920 | tf_op jit(solution)/shard_map/ppermute | solution.py:30
  158.4 3.3 %shard_map.142.w_ref = bf16[4,4,4,48,384]{4,3,2,1,0:T(8,128)(2,1)} custom-call(s32[5]{0:T(128)} %stack.117.pos_ref, bf16[4,48,1536]{2,1,0:T(8,128)(2,1)} %copy-done.2, bf16[4,48,1536]{2,1,0:T(8,128)(2,1)} %collective-permute-done.29.w1, bf16[4,48,1536]{2,1,0:T(8,128)(2,1)} %copy-done.5, bf16[4,48,1536]{2,1,0:T(8,128)(2,1)} %copy-done.6), custom_call_target="tpu_custom_call" | custom-call | tf_op jit(solution)/shard_map/pallas_call | solution.py:217
  162.9 3.5 %shard_map.143 = bf16[64,2,768]{2,1,0:T(2,128)(2,1)} custom-call(s32[5]{0:T(128)} %stack.117.pos_ref, bf16[2,64,384]{2,1,0:T(8,128)(2,1)} %copy-done.9, bf16[2,64,384]{2,1,0:T(8,128)(2,1)} %copy-done.13, bf16[2,64,384]{2,1,0:T(8,128)(2,1)} %copy-done.14, bf16[2,64,384]{2,1,0:T(8,128)(2,1)} %copy-done.15, bf16[4,4,4,48,384]{4,3,2,1,0:T(8,128)(2,1)} %shard_map.142.w_ref, ...), custom_call_target="tpu_custom_call" | custom-call | tf_op jit(solution)/shard_map/pallas_call | solution.py:217
  167.1 2.7 %shard_map.144 = bf16[64,2,2,384]{3,2,1,0:T(2,128)(2,1)} custom-call(bf16[64,2,896]{2,1,0:T(2,128)(2,1)} %copy-done.4), custom_call_target="tpu_custom_call" | custom-call | tf_op jit(solution)/shard_map/pallas_call | solution.py:217
  (148 shorter events, 48.5 us)
Async XLA Ops:
  3.6 15.7 %collective-permute-start = (bf16[64,3200]{1,0:T(8,128)(2,1)S(1)}, bf16[64,3200]{1,0:T(8,128)(2,1)S(1)}, u32[]{:S(2)}, u32[]{:S(2)}) collective-permute-start(bf16[64,3200]{1,0:T(8,128)(2,1)S(1)} %get-tuple-element.13), channel_id=1, source_target_pairs={{0,50},{1,51},{2,16},{3,17},{4,54},{5,55},{6,20},{7,21},{8,58},{9,... | collective-permute-start | bytes 1228808 | tf_op jit(solution)/shard_map/ppermute | solution.py:30
  20.3 30.4 %collective-permute-start.4 = (bf16[128,384]{1,0:T(8,128)(2,1)}, bf16[128,384]{1,0:T(8,128)(2,1)}, u32[]{:S(2)}, u32[]{:S(2)}) collective-permute-start(bf16[128,384]{1,0:T(8,128)(2,1)} %get-tuple-element.45), channel_id=1, source_target_pairs={{0,16},{1,17},{2,18},{3,19},{4,20},{5,21},{6,22},{7,23},{8,24},{9,... | collective-permute-start | bytes 294920 | tf_op jit(solution)/shard_map/ppermute | solution.py:30
  22.1 29.4 %collective-permute-start.5 = (bf16[128,384]{1,0:T(8,128)(2,1)}, bf16[128,384]{1,0:T(8,128)(2,1)}, u32[]{:S(2)}, u32[]{:S(2)}) collective-permute-start(bf16[128,384]{1,0:T(8,128)(2,1)} %get-tuple-element.44), channel_id=1, source_target_pairs={{0,32},{1,33},{2,34},{3,35},{4,36},{5,37},{6,38},{7,39},{8,40},{9,... | collective-permute-start | bytes 294920 | tf_op jit(solution)/shard_map/ppermute | solution.py:30
  26.0 26.3 %collective-permute-start.6 = (bf16[128,384]{1,0:T(8,128)(2,1)}, bf16[128,384]{1,0:T(8,128)(2,1)}, u32[]{:S(2)}, u32[]{:S(2)}) collective-permute-start(bf16[128,384]{1,0:T(8,128)(2,1)} %get-tuple-element.43), channel_id=1, source_target_pairs={{0,48},{1,49},{2,50},{3,51},{4,52},{5,53},{6,54},{7,55},{8,56},{9,... | collective-permute-start | bytes 294920 | tf_op jit(solution)/shard_map/ppermute | solution.py:30
  29.2 18.3 %collective-permute-start.2 = (bf16[64,3200]{1,0:T(8,128)(2,1)}, bf16[64,3200]{1,0:T(8,128)(2,1)S(1)}, u32[]{:S(2)}, u32[]{:S(2)}) collective-permute-start(bf16[64,3200]{1,0:T(8,128)(2,1)} %collective-permute-done.1), channel_id=1, source_target_pairs={{0,50},{1,51},{2,16},{3,17},{4,54},{5,55},{6,20},{7,21},{8,58},{9,... | collective-permute-start | bytes 1228808 | tf_op jit(solution)/shard_map/ppermute | solution.py:30
  48.8 65.9 %collective-permute-start.3 = (bf16[4,64,3200]{2,1,0:T(8,128)(2,1)S(1)}, bf16[4,64,3200]{2,1,0:T(8,128)(2,1)}, u32[]{:S(2)}, u32[]{:S(2)}) collective-permute-start(bf16[4,64,3200]{2,1,0:T(8,128)(2,1)S(1)} %pad_maximum_fusion.own_ref), channel_id=1, source_target_pairs={{0,1},{1,0},{2,3},{3,2},{4,5},{5,4},{6,7},{7,6},{8,9},{9,8},{10,11... | collective-permute-start | bytes 4915208 | tf_op jit(solution)/shard_map/ppermute | solution.py:30
  53.2 11.8 %collective-permute-start.9 = (bf16[48,1152]{1,0:T(8,128)(2,1)S(1)}, bf16[48,1152]{1,0:T(8,128)(2,1)S(1)}, u32[]{:S(2)}, u32[]{:S(2)}) collective-permute-start(bf16[48,1152]{1,0:T(8,128)(2,1)S(1)} %concatenate.76), channel_id=1, source_target_pairs={{0,192},{1,193},{2,194},{3,195},{4,196},{5,197},{6,198},{7,199},{8... | collective-permute-start | bytes 331784 | tf_op jit(solution)/shard_map/ppermute | solution.py:30
  59.3 12.1 %collective-permute-start.15 = (bf16[32,1536]{1,0:T(8,128)(2,1)S(1)}, bf16[32,1536]{1,0:T(8,128)(2,1)S(1)}, u32[]{:S(2)}, u32[]{:S(2)}) collective-permute-start(bf16[32,1536]{1,0:T(8,128)(2,1)S(1)} %get-tuple-element.26), channel_id=1, source_target_pairs={{0,12},{1,13},{2,14},{3,15},{4,0},{5,1},{6,2},{7,3},{8,4},{9,5},{1... | collective-permute-start | bytes 294920 | tf_op jit(solution)/shard_map/ppermute | solution.py:30
  65.6 12.6 %collective-permute-start.13 = (bf16[32,1536]{1,0:T(8,128)(2,1)S(1)}, bf16[32,1536]{1,0:T(8,128)(2,1)S(1)}, u32[]{:S(2)}, u32[]{:S(2)}) collective-permute-start(bf16[32,1536]{1,0:T(8,128)(2,1)S(1)} %get-tuple-element.26), channel_id=1, source_target_pairs={{0,4},{1,5},{2,6},{3,7},{4,8},{5,9},{6,10},{7,11},{8,12},{9,13},{1... | collective-permute-start | bytes 294920 | tf_op jit(solution)/shard_map/ppermute | solution.py:30
  71.4 30.2 %collective-permute-start.10 = (bf16[4,48,1152]{2,1,0:T(8,128)(2,1)S(1)}, bf16[4,48,1152]{2,1,0:T(8,128)(2,1)S(1)}, u32[]{:S(2)}, u32[]{:S(2)}) collective-permute-start(bf16[4,48,1152]{2,1,0:T(8,128)(2,1)S(1)} %pad_maximum_fusion.2.w0), channel_id=1, source_target_pairs={{0,4},{1,5},{2,6},{3,7},{4,8},{5,9},{6,10},{7,11},{8,12},{9,13},{1... | collective-permute-start | bytes 1327112 | tf_op jit(solution)/shard_map/ppermute | solution.py:30
  73.0 29.6 %collective-permute-start.11 = (bf16[4,48,1152]{2,1,0:T(8,128)(2,1)S(1)}, bf16[4,48,1152]{2,1,0:T(8,128)(2,1)S(1)}, u32[]{:S(2)}, u32[]{:S(2)}) collective-permute-start(bf16[4,48,1152]{2,1,0:T(8,128)(2,1)S(1)} %pad_maximum_fusion.2.w0), channel_id=1, source_target_pairs={{0,8},{1,9},{2,10},{3,11},{4,12},{5,13},{6,14},{7,15},{8,0},{9,1},... | collective-permute-start | bytes 1327112 | tf_op jit(solution)/shard_map/ppermute | solution.py:30
  76.0 12.7 %collective-permute-start.28 = (bf16[48,1536]{1,0:T(8,128)(2,1)S(1)}, bf16[48,1536]{1,0:T(8,128)(2,1)}, u32[]{:S(2)}, u32[]{:S(2)}) collective-permute-start(bf16[48,1536]{1,0:T(8,128)(2,1)S(1)} %collective-permute-done.25), channel_id=1, source_target_pairs={{0,12},{1,13},{2,14},{3,15},{4,0},{5,1},{6,2},{7,3},{8,4},{9,5},{1... | collective-permute-start | bytes 442376 | tf_op jit(solution)/shard_map/ppermute | solution.py:30
  78.1 19.1 %collective-permute-start.27 = (bf16[48,1536]{1,0:T(8,128)(2,1)S(1)}, bf16[48,1536]{1,0:T(8,128)(2,1)}, u32[]{:S(2)}, u32[]{:S(2)}) collective-permute-start(bf16[48,1536]{1,0:T(8,128)(2,1)S(1)} %collective-permute-done.25), channel_id=1, source_target_pairs={{0,8},{1,9},{2,10},{3,11},{4,12},{5,13},{6,14},{7,15},{8,0},{9,1},... | collective-permute-start | bytes 442376 | tf_op jit(solution)/shard_map/ppermute | solution.py:30
  97.3 25.0 %collective-permute-start.16 = (bf16[4,32,1536]{2,1,0:T(8,128)(2,1)}, bf16[4,32,1536]{2,1,0:T(8,128)(2,1)}, u32[]{:S(2)}, u32[]{:S(2)}) collective-permute-start(bf16[4,32,1536]{2,1,0:T(8,128)(2,1)} %pad_maximum_fusion.3.p0), channel_id=1, source_target_pairs={{0,64},{1,65},{2,66},{3,67},{4,68},{5,69},{6,70},{7,71},{8,72},{9,... | collective-permute-start | bytes 1179656 | tf_op jit(solution)/shard_map/ppermute | solution.py:30
  99.0 24.9 %collective-permute-start.17 = (bf16[4,32,1536]{2,1,0:T(8,128)(2,1)}, bf16[4,32,1536]{2,1,0:T(8,128)(2,1)}, u32[]{:S(2)}, u32[]{:S(2)}) collective-permute-start(bf16[4,32,1536]{2,1,0:T(8,128)(2,1)} %pad_maximum_fusion.3.p0), channel_id=1, source_target_pairs={{0,128},{1,129},{2,130},{3,131},{4,132},{5,133},{6,134},{7,135},{8... | collective-permute-start | bytes 1179656 | tf_op jit(solution)/shard_map/ppermute | solution.py:30
  101.6 22.3 %collective-permute-start.18 = (bf16[4,32,1536]{2,1,0:T(8,128)(2,1)}, bf16[4,32,1536]{2,1,0:T(8,128)(2,1)}, u32[]{:S(2)}, u32[]{:S(2)}) collective-permute-start(bf16[4,32,1536]{2,1,0:T(8,128)(2,1)} %pad_maximum_fusion.3.p0), channel_id=1, source_target_pairs={{0,192},{1,193},{2,194},{3,195},{4,196},{5,197},{6,198},{7,199},{8... | collective-permute-start | bytes 1179656 | tf_op jit(solution)/shard_map/ppermute | solution.py:30
  103.4 10.8 %collective-permute-start.12 = (bf16[4,48,1152]{2,1,0:T(8,128)(2,1)S(1)}, bf16[4,48,1152]{2,1,0:T(8,128)(2,1)}, u32[]{:S(2)}, u32[]{:S(2)}) collective-permute-start(bf16[4,48,1152]{2,1,0:T(8,128)(2,1)S(1)} %pad_maximum_fusion.2.w0), channel_id=1, source_target_pairs={{0,12},{1,13},{2,14},{3,15},{4,0},{5,1},{6,2},{7,3},{8,4},{9,5},{1... | collective-permute-start | bytes 1327112 | tf_op jit(solution)/shard_map/ppermute | solution.py:30
  114.2 40.4 %collective-permute-start.29 = (bf16[4,48,1536]{2,1,0:T(8,128)(2,1)S(1)}, bf16[4,48,1536]{2,1,0:T(8,128)(2,1)}, u32[]{:S(2)}, u32[]{:S(2)}) collective-permute-start(bf16[4,48,1536]{2,1,0:T(8,128)(2,1)S(1)} %pad_maximum_fusion.1.w0), channel_id=1, source_target_pairs={{0,64},{1,65},{2,66},{3,67},{4,68},{5,69},{6,70},{7,71},{8,72},{9,... | collective-permute-start | bytes 1769480 | tf_op jit(solution)/shard_map/ppermute | solution.py:30
  114.7 42.0 %collective-permute-start.30 = (bf16[4,48,1536]{2,1,0:T(8,128)(2,1)S(1)}, bf16[4,48,1536]{2,1,0:T(8,128)(2,1)S(1)}, u32[]{:S(2)}, u32[]{:S(2)}) collective-permute-start(bf16[4,48,1536]{2,1,0:T(8,128)(2,1)S(1)} %pad_maximum_fusion.1.w0), channel_id=1, source_target_pairs={{0,128},{1,129},{2,130},{3,131},{4,132},{5,133},{6,134},{7,135},{8... | collective-permute-start | bytes 1769480 | tf_op jit(solution)/shard_map/ppermute | solution.py:30
  122.3 34.4 %collective-permute-start.31 = (bf16[4,48,1536]{2,1,0:T(8,128)(2,1)S(1)}, bf16[4,48,1536]{2,1,0:T(8,128)(2,1)S(1)}, u32[]{:S(2)}, u32[]{:S(2)}) collective-permute-start(bf16[4,48,1536]{2,1,0:T(8,128)(2,1)S(1)} %pad_maximum_fusion.1.w0), channel_id=1, source_target_pairs={{0,192},{1,193},{2,194},{3,195},{4,196},{5,197},{6,198},{7,199},{8... | collective-permute-start | bytes 1769480 | tf_op jit(solution)/shard_map/ppermute | solution.py:30
  134.6 14.3 %collective-permute-start.21 = (bf16[2,64,96]{2,1,0:T(8,128)(2,1)S(1)}, bf16[2,64,96]{2,1,0:T(8,128)(2,1)S(1)}, u32[]{:S(2)}, u32[]{:S(2)}) collective-permute-start(bf16[2,64,96]{2,1,0:T(8,128)(2,1)S(1)} %get-tuple-element.24), channel_id=1, source_target_pairs={{0,16},{1,17},{2,50},{3,51},{4,20},{5,21},{6,54},{7,55},{8,24},{9,... | collective-permute-start | bytes 73736 | tf_op jit(solution)/shard_map/ppermute | solution.py:30
  138.2 10.7 %collective-permute-start.19 = (bf16[2,64,96]{2,1,0:T(8,128)(2,1)S(1)}, bf16[2,64,96]{2,1,0:T(8,128)(2,1)S(1)}, u32[]{:S(2)}, u32[]{:S(2)}) collective-permute-start(bf16[2,64,96]{2,1,0:T(8,128)(2,1)S(1)} %get-tuple-element.22), channel_id=1, source_target_pairs={{0,48},{1,49},{2,18},{3,19},{4,52},{5,53},{6,22},{7,23},{8,56},{9,... | collective-permute-start | bytes 73736 | tf_op jit(solution)/shard_map/ppermute | solution.py:30
  141.7 24.7 %all-to-all-start = ((bf16[64,2,896]{2,1,0:T(2,128)(2,1)}), bf16[64,2,896]{2,1,0:T(2,128)(2,1)S(1)}, u32[]{:S(2)}, u32[]{:S(2)}) async-start(bf16[64,2,896]{2,1,0:T(2,128)(2,1)} %get-tuple-element.11), calls=%async_computation | async-start | bytes 458752 | tf_op jit(solution)/shard_map/all_to_all | solution.py:290
  149.8 11.8 %collective-permute-start.22 = (bf16[2,64,384]{2,1,0:T(8,128)(2,1)S(1)}, bf16[2,64,384]{2,1,0:T(8,128)(2,1)S(1)}, u32[]{:S(2)}, u32[]{:S(2)}) collective-permute-start(bf16[2,64,384]{2,1,0:T(8,128)(2,1)S(1)} %pad_maximum_fusion.14.a0), channel_id=1, source_target_pairs={{0,1},{1,0},{2,3},{3,2},{4,5},{5,4},{6,7},{7,6},{8,9},{9,8},{10,11... | collective-permute-start | bytes 294920 | tf_op jit(solution)/shard_map/ppermute | solution.py:30
  (33 other events, 412.0 us)

commit v4 on v3

--- a/solution.py
+++ b/solution.py
@@ -173,20 +173,22 @@
         one_slot(t)
 
 
-def order_kernel(pos_ref, w0, w1, w2, w3, out_ref):
-    y, zh, x = pos_ref[0], pos_ref[1], pos_ref[2]
+def out_kernel(pos_ref, a0, a1, a2, a3, w0, w1, w2, w3, dest_ref, len_ref, out_ref, att_ref):
+    y, m = pos_ref[0], pos_ref[4]
+    for k, block in enumerate((a0, a1, a2, a3)):
+        att_ref[m ^ k] = block[...].reshape(128, 384)
+    parts = [None] * 4
     for ky, piece in enumerate((w0, w1, w2, w3)):
-        for kx in range(4):
-            for kz in range(4):
-                out_ref[(y - ky) & 3, (zh - kz) & 3, (x - kx) & 3] = piece[kx, :, 384 * kz : 384 * kz + 384]
-
-
-def out_kernel(pos_ref, a0, a1, a2, a3, w_ref, len_ref, out_ref):
-    m = pos_ref[4]
+        rows = att_ref[(y - ky) & 3]
+        for kz in range(4):
+            weight = piece[:, :, 384 * kz : 384 * kz + 384].reshape(192, 384)
+            part = dot_nt(rows, weight)
+            parts[kz] = part if parts[kz] is None else parts[kz] + part
+    column = lax.broadcasted_iota(jnp.int32, (192, 768), 1).astype(jnp.float32)
     acc = None
-    for k, block in enumerate((a0, a1, a2, a3)):
-        weight = w_ref[m ^ k].reshape(768, 384)
-        part = dot_nt(block[...].reshape(128, 384), weight)
+    for kz in range(4):
+        pick = jnp.where(dest_ref[192 * kz : 192 * kz + 192, :] == column, 1.0, 0.0).astype(jnp.bfloat16)
+        part = jnp.dot(parts[kz].astype(jnp.bfloat16), pick, preferred_element_type=jnp.float32)
         acc = part if acc is None else acc + part
     out_ref[:, 0, :] = acc[0:64].astype(jnp.bfloat16)
     out_ref[:, 1, :] = jnp.where(len_ref[...] > 1, acc[64:128], 0.0).astype(jnp.bfloat16)
@@ -321,8 +323,17 @@
     home = jnp.concatenate(heads, axis=2)
     home_all = [home] + [mp_xor(home, k) for k in (1, 2, 3)]
 
-    out_weight = call(order_kernel, struct((4, 4, 4, 48, 384)), [pos, *out_pieces], scalars=1)
-    hidden = call(out_kernel, struct((64, 2, 768)), [pos, *home_all, out_weight, lengths[:, None]], scalars=1)
+    row = np.arange(768, dtype=np.int32)
+    place_of = (
+        ((zh - row // 192) % 4) * 192 + ((x - (row // 48) % 4) % 4) * 48 + row % 48
+    ).astype(jnp.float32)[:, None]
+    hidden = call(
+        out_kernel,
+        struct((64, 2, 768)),
+        [pos, *home_all, *out_pieces, place_of, lengths[:, None]],
+        scratch=[pltpu.VMEM((4, 128, 384), jnp.bfloat16)],
+        scalars=1,
+    )
     suffix_cache = call(unpack_kernel, struct((64, 2, 2, 384)), [received])
     return hidden, suffix_cache
 

time: 171 us -> 176 us (1.029)
  waiting for transfers between devices: 51.8 us -> 61.7 us
  Pallas kernels: 22.7 us -> 20 us
  starting transfers between devices: 69.7 us -> 67.3 us
    ppermute x32, waiting for transfers between devices: 51.8 us -> 61.7 us  [move(): return lax.ppermute(value, ('dp', 'mp'), perm)]
    pallas_call x5 -> x4, Pallas kernels: 22.7 us -> 20 us  [call(): pl.pallas_call(kernel, out_shape=outs, in_specs=[smem] * scalars + [vmem]...]
    ppermute x32, starting transfers between devices: 62.6 us -> 60.1 us  [move(): return lax.ppermute(value, ('dp', 'mp'), perm)]
    unnamed x49 -> x55, local copies, waits for them, and re-layouts: 4.03 us -> 3.07 us
  transfers between devices with their start and end apart: 33 -> 33, of which waited for: 10 -> 9; matrix products, arithmetic and copies ran while one was open for 10% -> 10% of each run, Pallas kernels for 12% -> 10%
where the time goes in v4:
time: 176 us; the launch traced here: 174 us
  starting transfers between devices  67.3 us (38%)
  waiting for transfers between devices  61.7 us (35%)
  Pallas kernels  20 us (11%)
  local copies, waits for them, and re-layouts  15.4 us (9%)
  other arithmetic  8.78 us (5%)
    ppermute x32, waiting for transfers between devices, move(): return lax.ppermute(value, ('dp', 'mp'), perm)  61.7 us
    ppermute x32, starting transfers between devices, move(): return lax.ppermute(value, ('dp', 'mp'), perm)  60.1 us
    pallas_call x4, Pallas kernels, call(): pl.pallas_call(kernel, out_shape=outs, in_specs=[smem] * scalars + [vmem]...  20 us
    all_to_all x1, starting transfers between devices, on_device(): lax.all_to_all(send, 'dp', split_axis=0, concat_axis=0, tiled=True)  7.15 us
  transfers between devices with their start and end apart: 33, of which 9 were waited for; matrix products, arithmetic and copies ran while one was open for 10% of the time, Pallas kernels for 10%

profile of v4, /device:TPU:1, one launch (start us, length us, event | category | flops | bytes accessed | tf_op | source)
XLA Modules:
  0.0 174.4 jit_solution(638940006994364036)
XLA Ops:
  3.6 6.5 %collective-permute-start = (bf16[64,3200]{1,0:T(8,128)(2,1)S(1)}, bf16[64,3200]{1,0:T(8,128)(2,1)S(1)}, u32[]{:S(2)}, u32[]{:S(2)}) collective-permute-start(bf16[64,3200]{1,0:T(8,128)(2,1)S(1)} %get-tuple-element.13), channel_id=1, source_target_pairs={{0,50},{1,51},{2,16},{3,17},{4,54},{5,55},{6,20},{7,21},{8,58},{9,... | collective-permute-start | bytes 1228808 | tf_op jit(solution)/shard_map/ppermute | solution.py:30
  10.5 8.7 %collective-permute-done = bf16[64,3200]{1,0:T(8,128)(2,1)S(1)} collective-permute-done((bf16[64,3200]{1,0:T(8,128)(2,1)S(1)}, bf16[64,3200]{1,0:T(8,128)(2,1)S(1)}, u32[]{:S(2)}, u32[]{:S(2)}) %collective-permute-start) | collective-permute-done | bytes 409632 | tf_op jit(solution)/shard_map/ppermute | solution.py:30
  22.1 3.9 %collective-permute-start.5 = (bf16[128,384]{1,0:T(8,128)(2,1)}, bf16[128,384]{1,0:T(8,128)(2,1)}, u32[]{:S(2)}, u32[]{:S(2)}) collective-permute-start(bf16[128,384]{1,0:T(8,128)(2,1)} %get-tuple-element.44), channel_id=1, source_target_pairs={{0,32},{1,33},{2,34},{3,35},{4,36},{5,37},{6,38},{7,39},{8,40},{9,... | collective-permute-start | bytes 294920 | tf_op jit(solution)/shard_map/ppermute | solution.py:30
  29.2 4.1 %collective-permute-start.2 = (bf16[64,3200]{1,0:T(8,128)(2,1)}, bf16[64,3200]{1,0:T(8,128)(2,1)S(1)}, u32[]{:S(2)}, u32[]{:S(2)}) collective-permute-start(bf16[64,3200]{1,0:T(8,128)(2,1)} %collective-permute-done.1), channel_id=1, source_target_pairs={{0,50},{1,51},{2,16},{3,17},{4,54},{5,55},{6,20},{7,21},{8,58},{9,... | collective-permute-start | bytes 1228808 | tf_op jit(solution)/shard_map/ppermute | solution.py:30
  33.9 13.6 %collective-permute-done.2 = bf16[64,3200]{1,0:T(8,128)(2,1)S(1)} collective-permute-done((bf16[64,3200]{1,0:T(8,128)(2,1)}, bf16[64,3200]{1,0:T(8,128)(2,1)S(1)}, u32[]{:S(2)}, u32[]{:S(2)}) %collective-permute-start.2) | collective-permute-done | bytes 409632 | tf_op jit(solution)/shard_map/ppermute | solution.py:30
  48.8 1.9 %collective-permute-start.3 = (bf16[4,64,3200]{2,1,0:T(8,128)(2,1)S(1)}, bf16[4,64,3200]{2,1,0:T(8,128)(2,1)}, u32[]{:S(2)}, u32[]{:S(2)}) collective-permute-start(bf16[4,64,3200]{2,1,0:T(8,128)(2,1)S(1)} %pad_maximum_fusion.own_ref), channel_id=1, source_target_pairs={{0,1},{1,0},{2,3},{3,2},{4,5},{5,4},{6,7},{7,6},{8,9},{9,8},{10,11... | collective-permute-start | bytes 4915208 | tf_op jit(solution)/shard_map/ppermute | solution.py:30
  53.2 2.8 %collective-permute-start.9 = (bf16[48,1152]{1,0:T(8,128)(2,1)S(1)}, bf16[48,1152]{1,0:T(8,128)(2,1)S(1)}, u32[]{:S(2)}, u32[]{:S(2)}) collective-permute-start(bf16[48,1152]{1,0:T(8,128)(2,1)S(1)} %concatenate.76), channel_id=1, source_target_pairs={{0,192},{1,193},{2,194},{3,195},{4,196},{5,197},{6,198},{7,199},{8... | collective-permute-start | bytes 331784 | tf_op jit(solution)/shard_map/ppermute | solution.py:30
  59.3 2.6 %collective-permute-start.15 = (bf16[32,1536]{1,0:T(8,128)(2,1)S(1)}, bf16[32,1536]{1,0:T(8,128)(2,1)S(1)}, u32[]{:S(2)}, u32[]{:S(2)}) collective-permute-start(bf16[32,1536]{1,0:T(8,128)(2,1)S(1)} %get-tuple-element.26), channel_id=1, source_target_pairs={{0,12},{1,13},{2,14},{3,15},{4,0},{5,1},{6,2},{7,3},{8,4},{9,5},{1... | collective-permute-start | bytes 294920 | tf_op jit(solution)/shard_map/ppermute | solution.py:30
  66.2 5.1 %collective-permute-start.25 = (bf16[48,1536]{1,0:T(8,128)(2,1)S(1)}, bf16[48,1536]{1,0:T(8,128)(2,1)S(1)}, u32[]{:S(2)}, u32[]{:S(2)}) collective-permute-start(bf16[48,1536]{1,0:T(8,128)(2,1)S(1)} %pad_maximum_fusion.5), channel_id=1, source_target_pairs={{0,0},{1,64},{2,128},{3,192},{4,4},{5,68},{6,132},{7,196},{8,8},{9... | collective-permute-start | bytes 442376 | tf_op jit(solution)/shard_map/ppermute | solution.py:30
  76.0 2.1 %collective-permute-start.28 = (bf16[48,1536]{1,0:T(8,128)(2,1)S(1)}, bf16[48,1536]{1,0:T(8,128)(2,1)}, u32[]{:S(2)}, u32[]{:S(2)}) collective-permute-start(bf16[48,1536]{1,0:T(8,128)(2,1)S(1)} %collective-permute-done.25), channel_id=1, source_target_pairs={{0,12},{1,13},{2,14},{3,15},{4,0},{5,1},{6,2},{7,3},{8,4},{9,5},{1... | collective-permute-start | bytes 442376 | tf_op jit(solution)/shard_map/ppermute | solution.py:30
  79.5 9.2 %collective-permute-done.28 = bf16[48,1536]{1,0:T(8,128)(2,1)} collective-permute-done((bf16[48,1536]{1,0:T(8,128)(2,1)S(1)}, bf16[48,1536]{1,0:T(8,128)(2,1)}, u32[]{:S(2)}, u32[]{:S(2)}) %collective-permute-start.28) | collective-permute-done | bytes 147488 | tf_op jit(solution)/shard_map/ppermute | solution.py:30
  91.0 6.2 %collective-permute-done.27 = bf16[48,1536]{1,0:T(8,128)(2,1)} collective-permute-done((bf16[48,1536]{1,0:T(8,128)(2,1)S(1)}, bf16[48,1536]{1,0:T(8,128)(2,1)}, u32[]{:S(2)}, u32[]{:S(2)}) %collective-permute-start.27) | collective-permute-done | bytes 147488 | tf_op jit(solution)/shard_map/ppermute | solution.py:30
  99.0 2.6 %collective-permute-start.17 = (bf16[4,32,1536]{2,1,0:T(8,128)(2,1)}, bf16[4,32,1536]{2,1,0:T(8,128)(2,1)}, u32[]{:S(2)}, u32[]{:S(2)}) collective-permute-start(bf16[4,32,1536]{2,1,0:T(8,128)(2,1)} %pad_maximum_fusion.3.p0), channel_id=1, source_target_pairs={{0,128},{1,129},{2,130},{3,131},{4,132},{5,133},{6,134},{7,135},{8... | collective-permute-start | bytes 1179656 | tf_op jit(solution)/shard_map/ppermute | solution.py:30
  106.6 7.7 %collective-permute-done.12.w3 = bf16[4,48,1152]{2,1,0:T(8,128)(2,1)} collective-permute-done((bf16[4,48,1152]{2,1,0:T(8,128)(2,1)S(1)}, bf16[4,48,1152]{2,1,0:T(8,128)(2,1)}, u32[]{:S(2)}, u32[]{:S(2)}) %collective-permute-start.12) | collective-permute-done | bytes 442400 | tf_op jit(solution)/shard_map/ppermute | solution.py:30
  114.7 6.5 %shard_map.167 = (bf16[512,96]{1,0:T(8,128)(2,1)}, bf16[512,96]{1,0:T(8,128)(2,1)}, bf16[512,96]{1,0:T(8,128)(2,1)}, f32[256,128]{1,0:T(8,128)}, bf16[64,2,896]{2,1,0:T(2,128)(2,1)}) custom-call(s32[5]{0:T(128)} %stack.117.pos_ref, bf16[4,64,3200]{2,1,0:T(8,128)(2,1)} %copy-done.1, bf16[4,64,3200]{2,1,0:T(8,128)(2,1)} %collective-permute-done.3.oth_ref, ...), custom_call_target="tpu_custom_call" | custom-call | tf_op jit(solution)/shard_map/pallas_call | solution.py:219
  121.2 6.8 %shard_map.168 = bf16[512,96]{1,0:T(8,128)(2,1)} custom-call(bf16[512,96]{1,0:T(8,128)(2,1)} %get-tuple-element.7.q_ref, bf16[512,96]{1,0:T(8,128)(2,1)} %get-tuple-element.8.k_ref, bf16[512,96]{1,0:T(8,128)(2,1)} %get-tuple-element.9.v_ref, f32[256,128]{1,0:T(8,128)} %get-tuple-element.10.info_ref, f32[4,1024]{1,0:T(4,128)} %reshape.138.kg_ref, ...), custom_call_target="tpu_custom_call" | custom-call | tf_op jit(solution)/shard_map/pallas_call | solution.py:219
  128.8 3.1 %collective-permute-start.20 = (bf16[2,64,96]{2,1,0:T(8,128)(2,1)S(1)}, bf16[2,64,96]{2,1,0:T(8,128)(2,1)S(1)}, u32[]{:S(2)}, u32[]{:S(2)}) collective-permute-start(bf16[2,64,96]{2,1,0:T(8,128)(2,1)S(1)} %get-tuple-element.23), channel_id=1, source_target_pairs={{0,32},{1,33},{2,34},{3,35},{4,36},{5,37},{6,38},{7,39},{8,40},{9,... | collective-permute-start | bytes 73736 | tf_op jit(solution)/shard_map/ppermute | solution.py:30
  131.9 2.3 %collective-permute-start.21 = (bf16[2,64,96]{2,1,0:T(8,128)(2,1)S(1)}, bf16[2,64,96]{2,1,0:T(8,128)(2,1)S(1)}, u32[]{:S(2)}, u32[]{:S(2)}) collective-permute-start(bf16[2,64,96]{2,1,0:T(8,128)(2,1)S(1)} %get-tuple-element.24), channel_id=1, source_target_pairs={{0,16},{1,17},{2,50},{3,51},{4,20},{5,21},{6,54},{7,55},{8,24},{9,... | collective-permute-start | bytes 73736 | tf_op jit(solution)/shard_map/ppermute | solution.py:30
  136.0 2.0 %collective-permute-start.31 = (bf16[4,48,1536]{2,1,0:T(8,128)(2,1)S(1)}, bf16[4,48,1536]{2,1,0:T(8,128)(2,1)S(1)}, u32[]{:S(2)}, u32[]{:S(2)}) collective-permute-start(bf16[4,48,1536]{2,1,0:T(8,128)(2,1)S(1)} %pad_maximum_fusion.1.w0), channel_id=1, source_target_pairs={{0,192},{1,193},{2,194},{3,195},{4,196},{5,197},{6,198},{7,199},{8... | collective-permute-start | bytes 1769480 | tf_op jit(solution)/shard_map/ppermute | solution.py:30
  137.9 7.1 %all-to-all-start = ((bf16[64,2,896]{2,1,0:T(2,128)(2,1)}), bf16[64,2,896]{2,1,0:T(2,128)(2,1)S(1)}, u32[]{:S(2)}, u32[]{:S(2)}) async-start(bf16[64,2,896]{2,1,0:T(2,128)(2,1)} %get-tuple-element.11), calls=%async_computation | async-start | bytes 458752 | tf_op jit(solution)/shard_map/all_to_all | solution.py:292
  146.0 4.3 %collective-permute-start.22 = (bf16[2,64,384]{2,1,0:T(8,128)(2,1)S(1)}, bf16[2,64,384]{2,1,0:T(8,128)(2,1)S(1)}, u32[]{:S(2)}, u32[]{:S(2)}) collective-permute-start(bf16[2,64,384]{2,1,0:T(8,128)(2,1)S(1)} %pad_maximum_fusion.14.a0), channel_id=1, source_target_pairs={{0,1},{1,0},{2,3},{3,2},{4,5},{5,4},{6,7},{7,6},{8,9},{9,8},{10,11... | collective-permute-start | bytes 294920 | tf_op jit(solution)/shard_map/ppermute | solution.py:30
  153.7 11.7 %collective-permute-done.31.w3 = bf16[4,48,1536]{2,1,0:T(8,128)(2,1)S(1)} collective-permute-done((bf16[4,48,1536]{2,1,0:T(8,128)(2,1)S(1)}, bf16[4,48,1536]{2,1,0:T(8,128)(2,1)S(1)}, u32[]{:S(2)}, u32[]{:S(2)}) %collective-permute-start.31) | collective-permute-done | bytes 589856 | tf_op jit(solution)/shard_map/ppermute | solution.py:30
  167.0 4.1 %shard_map.169 = bf16[64,2,768]{2,1,0:T(2,128)(2,1)} custom-call(s32[5]{0:T(128)} %stack.117.pos_ref, bf16[2,64,384]{2,1,0:T(8,128)(2,1)} %copy-done.9, bf16[2,64,384]{2,1,0:T(8,128)(2,1)} %copy-done.13, bf16[2,64,384]{2,1,0:T(8,128)(2,1)} %copy-done.14, bf16[2,64,384]{2,1,0:T(8,128)(2,1)} %copy-done.15, bf16[4,48,1536]{2,1,0:T(8,128)(2,1)} %copy-done.2, ...), custom_call_target="tpu_custom_call" | custom-call | tf_op jit(solution)/shard_map/pallas_call | solution.py:219
  171.7 2.7 %shard_map.170 = bf16[64,2,2,384]{3,2,1,0:T(2,128)(2,1)} custom-call(bf16[64,2,896]{2,1,0:T(2,128)(2,1)} %copy-done.4), custom_call_target="tpu_custom_call" | custom-call | tf_op jit(solution)/shard_map/pallas_call | solution.py:219
  (155 shorter events, 45.7 us)
Async XLA Ops:
  3.6 15.7 %collective-permute-start = (bf16[64,3200]{1,0:T(8,128)(2,1)S(1)}, bf16[64,3200]{1,0:T(8,128)(2,1)S(1)}, u32[]{:S(2)}, u32[]{:S(2)}) collective-permute-start(bf16[64,3200]{1,0:T(8,128)(2,1)S(1)} %get-tuple-element.13), channel_id=1, source_target_pairs={{0,50},{1,51},{2,16},{3,17},{4,54},{5,55},{6,20},{7,21},{8,58},{9,... | collective-permute-start | bytes 1228808 | tf_op jit(solution)/shard_map/ppermute | solution.py:30
  20.3 30.4 %collective-permute-start.4 = (bf16[128,384]{1,0:T(8,128)(2,1)}, bf16[128,384]{1,0:T(8,128)(2,1)}, u32[]{:S(2)}, u32[]{:S(2)}) collective-permute-start(bf16[128,384]{1,0:T(8,128)(2,1)} %get-tuple-element.45), channel_id=1, source_target_pairs={{0,16},{1,17},{2,18},{3,19},{4,20},{5,21},{6,22},{7,23},{8,24},{9,... | collective-permute-start | bytes 294920 | tf_op jit(solution)/shard_map/ppermute | solution.py:30
  22.1 29.4 %collective-permute-start.5 = (bf16[128,384]{1,0:T(8,128)(2,1)}, bf16[128,384]{1,0:T(8,128)(2,1)}, u32[]{:S(2)}, u32[]{:S(2)}) collective-permute-start(bf16[128,384]{1,0:T(8,128)(2,1)} %get-tuple-element.44), channel_id=1, source_target_pairs={{0,32},{1,33},{2,34},{3,35},{4,36},{5,37},{6,38},{7,39},{8,40},{9,... | collective-permute-start | bytes 294920 | tf_op jit(solution)/shard_map/ppermute | solution.py:30
  25.9 26.3 %collective-permute-start.6 = (bf16[128,384]{1,0:T(8,128)(2,1)}, bf16[128,384]{1,0:T(8,128)(2,1)}, u32[]{:S(2)}, u32[]{:S(2)}) collective-permute-start(bf16[128,384]{1,0:T(8,128)(2,1)} %get-tuple-element.43), channel_id=1, source_target_pairs={{0,48},{1,49},{2,50},{3,51},{4,52},{5,53},{6,54},{7,55},{8,56},{9,... | collective-permute-start | bytes 294920 | tf_op jit(solution)/shard_map/ppermute | solution.py:30
  29.2 18.3 %collective-permute-start.2 = (bf16[64,3200]{1,0:T(8,128)(2,1)}, bf16[64,3200]{1,0:T(8,128)(2,1)S(1)}, u32[]{:S(2)}, u32[]{:S(2)}) collective-permute-start(bf16[64,3200]{1,0:T(8,128)(2,1)} %collective-permute-done.1), channel_id=1, source_target_pairs={{0,50},{1,51},{2,16},{3,17},{4,54},{5,55},{6,20},{7,21},{8,58},{9,... | collective-permute-start | bytes 1228808 | tf_op jit(solution)/shard_map/ppermute | solution.py:30
  48.8 65.9 %collective-permute-start.3 = (bf16[4,64,3200]{2,1,0:T(8,128)(2,1)S(1)}, bf16[4,64,3200]{2,1,0:T(8,128)(2,1)}, u32[]{:S(2)}, u32[]{:S(2)}) collective-permute-start(bf16[4,64,3200]{2,1,0:T(8,128)(2,1)S(1)} %pad_maximum_fusion.own_ref), channel_id=1, source_target_pairs={{0,1},{1,0},{2,3},{3,2},{4,5},{5,4},{6,7},{7,6},{8,9},{9,8},{10,11... | collective-permute-start | bytes 4915208 | tf_op jit(solution)/shard_map/ppermute | solution.py:30
  53.2 11.8 %collective-permute-start.9 = (bf16[48,1152]{1,0:T(8,128)(2,1)S(1)}, bf16[48,1152]{1,0:T(8,128)(2,1)S(1)}, u32[]{:S(2)}, u32[]{:S(2)}) collective-permute-start(bf16[48,1152]{1,0:T(8,128)(2,1)S(1)} %concatenate.76), channel_id=1, source_target_pairs={{0,192},{1,193},{2,194},{3,195},{4,196},{5,197},{6,198},{7,199},{8... | collective-permute-start | bytes 331784 | tf_op jit(solution)/shard_map/ppermute | solution.py:30
  59.3 12.1 %collective-permute-start.15 = (bf16[32,1536]{1,0:T(8,128)(2,1)S(1)}, bf16[32,1536]{1,0:T(8,128)(2,1)S(1)}, u32[]{:S(2)}, u32[]{:S(2)}) collective-permute-start(bf16[32,1536]{1,0:T(8,128)(2,1)S(1)} %get-tuple-element.26), channel_id=1, source_target_pairs={{0,12},{1,13},{2,14},{3,15},{4,0},{5,1},{6,2},{7,3},{8,4},{9,5},{1... | collective-permute-start | bytes 294920 | tf_op jit(solution)/shard_map/ppermute | solution.py:30
  65.6 12.6 %collective-permute-start.13 = (bf16[32,1536]{1,0:T(8,128)(2,1)S(1)}, bf16[32,1536]{1,0:T(8,128)(2,1)S(1)}, u32[]{:S(2)}, u32[]{:S(2)}) collective-permute-start(bf16[32,1536]{1,0:T(8,128)(2,1)S(1)} %get-tuple-element.26), channel_id=1, source_target_pairs={{0,4},{1,5},{2,6},{3,7},{4,8},{5,9},{6,10},{7,11},{8,12},{9,13},{1... | collective-permute-start | bytes 294920 | tf_op jit(solution)/shard_map/ppermute | solution.py:30
  71.4 30.2 %collective-permute-start.10 = (bf16[4,48,1152]{2,1,0:T(8,128)(2,1)S(1)}, bf16[4,48,1152]{2,1,0:T(8,128)(2,1)S(1)}, u32[]{:S(2)}, u32[]{:S(2)}) collective-permute-start(bf16[4,48,1152]{2,1,0:T(8,128)(2,1)S(1)} %pad_maximum_fusion.2.w0), channel_id=1, source_target_pairs={{0,4},{1,5},{2,6},{3,7},{4,8},{5,9},{6,10},{7,11},{8,12},{9,13},{1... | collective-permute-start | bytes 1327112 | tf_op jit(solution)/shard_map/ppermute | solution.py:30
  73.0 29.6 %collective-permute-start.11 = (bf16[4,48,1152]{2,1,0:T(8,128)(2,1)S(1)}, bf16[4,48,1152]{2,1,0:T(8,128)(2,1)S(1)}, u32[]{:S(2)}, u32[]{:S(2)}) collective-permute-start(bf16[4,48,1152]{2,1,0:T(8,128)(2,1)S(1)} %pad_maximum_fusion.2.w0), channel_id=1, source_target_pairs={{0,8},{1,9},{2,10},{3,11},{4,12},{5,13},{6,14},{7,15},{8,0},{9,1},... | collective-permute-start | bytes 1327112 | tf_op jit(solution)/shard_map/ppermute | solution.py:30
  76.0 12.7 %collective-permute-start.28 = (bf16[48,1536]{1,0:T(8,128)(2,1)S(1)}, bf16[48,1536]{1,0:T(8,128)(2,1)}, u32[]{:S(2)}, u32[]{:S(2)}) collective-permute-start(bf16[48,1536]{1,0:T(8,128)(2,1)S(1)} %collective-permute-done.25), channel_id=1, source_target_pairs={{0,12},{1,13},{2,14},{3,15},{4,0},{5,1},{6,2},{7,3},{8,4},{9,5},{1... | collective-permute-start | bytes 442376 | tf_op jit(solution)/shard_map/ppermute | solution.py:30
  78.1 19.1 %collective-permute-start.27 = (bf16[48,1536]{1,0:T(8,128)(2,1)S(1)}, bf16[48,1536]{1,0:T(8,128)(2,1)}, u32[]{:S(2)}, u32[]{:S(2)}) collective-permute-start(bf16[48,1536]{1,0:T(8,128)(2,1)S(1)} %collective-permute-done.25), channel_id=1, source_target_pairs={{0,8},{1,9},{2,10},{3,11},{4,12},{5,13},{6,14},{7,15},{8,0},{9,1},... | collective-permute-start | bytes 442376 | tf_op jit(solution)/shard_map/ppermute | solution.py:30
  97.3 23.9 %collective-permute-start.16 = (bf16[4,32,1536]{2,1,0:T(8,128)(2,1)}, bf16[4,32,1536]{2,1,0:T(8,128)(2,1)}, u32[]{:S(2)}, u32[]{:S(2)}) collective-permute-start(bf16[4,32,1536]{2,1,0:T(8,128)(2,1)} %pad_maximum_fusion.3.p0), channel_id=1, source_target_pairs={{0,64},{1,65},{2,66},{3,67},{4,68},{5,69},{6,70},{7,71},{8,72},{9,... | collective-permute-start | bytes 1179656 | tf_op jit(solution)/shard_map/ppermute | solution.py:30
  99.0 22.2 %collective-permute-start.17 = (bf16[4,32,1536]{2,1,0:T(8,128)(2,1)}, bf16[4,32,1536]{2,1,0:T(8,128)(2,1)}, u32[]{:S(2)}, u32[]{:S(2)}) collective-permute-start(bf16[4,32,1536]{2,1,0:T(8,128)(2,1)} %pad_maximum_fusion.3.p0), channel_id=1, source_target_pairs={{0,128},{1,129},{2,130},{3,131},{4,132},{5,133},{6,134},{7,135},{8... | collective-permute-start | bytes 1179656 | tf_op jit(solution)/shard_map/ppermute | solution.py:30
  101.6 19.6 %collective-permute-start.18 = (bf16[4,32,1536]{2,1,0:T(8,128)(2,1)}, bf16[4,32,1536]{2,1,0:T(8,128)(2,1)}, u32[]{:S(2)}, u32[]{:S(2)}) collective-permute-start(bf16[4,32,1536]{2,1,0:T(8,128)(2,1)} %pad_maximum_fusion.3.p0), channel_id=1, source_target_pairs={{0,192},{1,193},{2,194},{3,195},{4,196},{5,197},{6,198},{7,199},{8... | collective-permute-start | bytes 1179656 | tf_op jit(solution)/shard_map/ppermute | solution.py:30
  114.3 36.7 %collective-permute-start.29 = (bf16[4,48,1536]{2,1,0:T(8,128)(2,1)S(1)}, bf16[4,48,1536]{2,1,0:T(8,128)(2,1)}, u32[]{:S(2)}, u32[]{:S(2)}) collective-permute-start(bf16[4,48,1536]{2,1,0:T(8,128)(2,1)S(1)} %pad_maximum_fusion.1.w0), channel_id=1, source_target_pairs={{0,64},{1,65},{2,66},{3,67},{4,68},{5,69},{6,70},{7,71},{8,72},{9,... | collective-permute-start | bytes 1769480 | tf_op jit(solution)/shard_map/ppermute | solution.py:30
  131.9 13.2 %collective-permute-start.21 = (bf16[2,64,96]{2,1,0:T(8,128)(2,1)S(1)}, bf16[2,64,96]{2,1,0:T(8,128)(2,1)S(1)}, u32[]{:S(2)}, u32[]{:S(2)}) collective-permute-start(bf16[2,64,96]{2,1,0:T(8,128)(2,1)S(1)} %get-tuple-element.24), channel_id=1, source_target_pairs={{0,16},{1,17},{2,50},{3,51},{4,20},{5,21},{6,54},{7,55},{8,24},{9,... | collective-permute-start | bytes 73736 | tf_op jit(solution)/shard_map/ppermute | solution.py:30
  135.5 18.2 %collective-permute-start.30 = (bf16[4,48,1536]{2,1,0:T(8,128)(2,1)S(1)}, bf16[4,48,1536]{2,1,0:T(8,128)(2,1)S(1)}, u32[]{:S(2)}, u32[]{:S(2)}) collective-permute-start(bf16[4,48,1536]{2,1,0:T(8,128)(2,1)S(1)} %pad_maximum_fusion.1.w0), channel_id=1, source_target_pairs={{0,128},{1,129},{2,130},{3,131},{4,132},{5,133},{6,134},{7,135},{8... | collective-permute-start | bytes 1769480 | tf_op jit(solution)/shard_map/ppermute | solution.py:30
  136.0 29.5 %collective-permute-start.31 = (bf16[4,48,1536]{2,1,0:T(8,128)(2,1)S(1)}, bf16[4,48,1536]{2,1,0:T(8,128)(2,1)S(1)}, u32[]{:S(2)}, u32[]{:S(2)}) collective-permute-start(bf16[4,48,1536]{2,1,0:T(8,128)(2,1)S(1)} %pad_maximum_fusion.1.w0), channel_id=1, source_target_pairs={{0,192},{1,193},{2,194},{3,195},{4,196},{5,197},{6,198},{7,199},{8... | collective-permute-start | bytes 1769480 | tf_op jit(solution)/shard_map/ppermute | solution.py:30
  137.9 33.1 %all-to-all-start = ((bf16[64,2,896]{2,1,0:T(2,128)(2,1)}), bf16[64,2,896]{2,1,0:T(2,128)(2,1)S(1)}, u32[]{:S(2)}, u32[]{:S(2)}) async-start(bf16[64,2,896]{2,1,0:T(2,128)(2,1)} %get-tuple-element.11), calls=%async_computation | async-start | bytes 458752 | tf_op jit(solution)/shard_map/all_to_all | solution.py:292
  146.0 19.4 %collective-permute-start.22 = (bf16[2,64,384]{2,1,0:T(8,128)(2,1)S(1)}, bf16[2,64,384]{2,1,0:T(8,128)(2,1)S(1)}, u32[]{:S(2)}, u32[]{:S(2)}) collective-permute-start(bf16[2,64,384]{2,1,0:T(8,128)(2,1)S(1)} %pad_maximum_fusion.14.a0), channel_id=1, source_target_pairs={{0,1},{1,0},{2,3},{3,2},{4,5},{5,4},{6,7},{7,6},{8,9},{9,8},{10,11... | collective-permute-start | bytes 294920 | tf_op jit(solution)/shard_map/ppermute | solution.py:30
  150.3 15.1 %collective-permute-start.23 = (bf16[2,64,384]{2,1,0:T(8,128)(2,1)S(1)}, bf16[2,64,384]{2,1,0:T(8,128)(2,1)S(1)}, u32[]{:S(2)}, u32[]{:S(2)}) collective-permute-start(bf16[2,64,384]{2,1,0:T(8,128)(2,1)S(1)} %pad_maximum_fusion.14.a0), channel_id=1, source_target_pairs={{0,2},{1,3},{2,0},{3,1},{4,6},{5,7},{6,4},{7,5},{8,10},{9,11},{10,... | collective-permute-start | bytes 294920 | tf_op jit(solution)/shard_map/ppermute | solution.py:30
  151.0 14.5 %collective-permute-start.24 = (bf16[2,64,384]{2,1,0:T(8,128)(2,1)S(1)}, bf16[2,64,384]{2,1,0:T(8,128)(2,1)S(1)}, u32[]{:S(2)}, u32[]{:S(2)}) collective-permute-start(bf16[2,64,384]{2,1,0:T(8,128)(2,1)S(1)} %pad_maximum_fusion.14.a0), channel_id=1, source_target_pairs={{0,3},{1,2},{2,1},{3,0},{4,7},{5,6},{6,5},{7,4},{8,11},{9,10},{10,... | collective-permute-start | bytes 294920 | tf_op jit(solution)/shard_map/ppermute | solution.py:30
  (36 other events, 542.7 us)
